TPU v7x, 32 devices: a whole 2x2x4 slice. The times are simulated.
32 devices in a mesh: prow: 8 (over z, core), pcol: 4 (over y, x).
Axes of the slice: x: 2, y: 2, z: 4, core: 2. Of those that a mesh axis runs over, the one named last changes fastest.
Arguments:
- leaf_source: bfloat16 [8, 4, 8, 256, 128], P('prow', 'pcol'), may hold values from -6 to 6
- band_source: bfloat16 [8, 256, 128], P('prow'), may hold values from -6 to 6
- strip_source: bfloat16 [4, 256, 128], P('pcol'), may hold values from -6 to 6
- summit_source: bfloat16 [256, 128], replicated, may hold values from -6 to 6
- leaf_inverse: bfloat16 [8, 4, 8, 256, 256], P('prow', 'pcol'), may hold values from -1 to 2
- band_inverse: bfloat16 [8, 256, 256], P('prow'), may hold values from -1 to 2
- strip_inverse: bfloat16 [4, 256, 256], P('pcol'), may hold values from -1 to 2
- summit_inverse: bfloat16 [256, 256], replicated, may hold values from -1 to 2
- leaf_blocks: bfloat16 [8, 4, 28, 256, 256], P('prow', 'pcol'), may hold values from -0.09375 to 0.09375
- band_blocks: bfloat16 [8, 4, 8, 256, 256], P('prow', 'pcol'), may hold values from -0.046875 to 0.046875
- strip_blocks: bfloat16 [8, 4, 8, 256, 256], P('prow', 'pcol'), may hold values from -0.03125 to 0.03125
- summit_blocks: bfloat16 [8, 4, 8, 256, 256], P('prow', 'pcol'), may hold values from -0.046875 to 0.046875
- coupling: bfloat16 [8, 4, 256, 256], P('prow', 'pcol'), may hold values from -0.09375 to 0.09375
- summit_band: bfloat16 [8, 256, 256], P('prow', 'pcol'), may hold values from -0.078125 to 0.078125
- summit_strip: bfloat16 [4, 256, 256], P('pcol'), may hold values from -0.078125 to 0.078125
- parents: int32 [8, 4, 8], P('prow', 'pcol'), may hold values from 1 to 8, as said below
- widths: int32 [8, 4, 8], P('prow', 'pcol'), may hold values from 64 to 256
Outputs:
- leaf_answer: bfloat16 [8, 4, 8, 256, 128], P('prow', 'pcol')
- band_answer: bfloat16 [8, 256, 128], P('prow')
- strip_answer: bfloat16 [4, 256, 128], P('pcol')
- summit_answer: bfloat16 [256, 128], replicated
Inputs may be any that keep to these rules, and one draw needn't show every extreme that they name: parents[r, c, a] is a later leaf of the same subtree, or 8 where leaf a links only to the separators.
All inputs are finite; a program needn't handle non-finite values.
Results may differ from a plain program's by a relative error of at most 0.015.
Values sent between devices are 32-bit elements; how exact they have to be, the bound alone decides.
No kernel may reach another device: no remote copies, remote signals or barrier semaphores. Data moves between devices by JAX's collectives and lax.ppermute only.
A program may use at most 64 MiB of HBM per device.

v0:
```python
import jax
import jax.numpy as jnp
from jax import lax
from jax.sharding import PartitionSpec as P

PASSES = 2


def ancestors(parent_list, leaf_count):
    node_ids = jnp.arange(leaf_count + 1, dtype=jnp.int32)
    current = parent_list
    extended = jnp.concatenate([current, jnp.full((1,), leaf_count, jnp.int32)])
    reached = jnp.zeros((leaf_count + 1, leaf_count), jnp.float32)
    for repeat in range(leaf_count):
        matches = current[None, :] == node_ids[:, None]
        reached = jnp.maximum(reached, matches.astype(jnp.float32))
        current = jnp.sum(jnp.where(matches, extended[:, None], 0), axis=0)
    return reached[:leaf_count]


def multiply(left, right, form):
    return jnp.einsum(form, left, right, preferred_element_type=jnp.float32)


def forward_block(inverse, source, partial_value):
    residual = (source.astype(jnp.float32) - partial_value).astype(jnp.bfloat16)
    return multiply(inverse, residual, "ij,jr->ir").astype(jnp.bfloat16)


def backward_block(inverse, source, partial_value):
    residual = (source.astype(jnp.float32) - partial_value).astype(jnp.bfloat16)
    return multiply(inverse, residual, "ji,jr->ir").astype(jnp.bfloat16)


def leaf_forward(pair_blocks, inverses, sources, reached, row_mask):
    leaf_count = sources.shape[0]
    solved = []
    for position in range(leaf_count):
        residual = sources[position].astype(jnp.float32)
        if position > 0:
            first_pair = position * (position - 1) // 2
            weights = reached[position, :position].astype(jnp.bfloat16)
            stacked = jnp.stack(solved) * weights[:, None, None]
            residual = residual - multiply(
                pair_blocks[first_pair : first_pair + position], stacked, "bij,bjr->ir"
            )
        residual = (row_mask[position] * residual).astype(jnp.bfloat16)
        solved.append(
            (row_mask[position] * multiply(inverses[position], residual, "ij,jr->ir")).astype(
                jnp.bfloat16
            )
        )
    return jnp.stack(solved)


def leaf_backward(pair_blocks, inverses, solved, outer, reached, row_mask):
    leaf_count = solved.shape[0]
    pending = outer
    answers = [None] * leaf_count
    for position in reversed(range(leaf_count)):
        residual = (
            row_mask[position] * (solved[position].astype(jnp.float32) - pending[position])
        ).astype(jnp.bfloat16)
        update = (row_mask[position] * multiply(inverses[position], residual, "ji,jr->ir")).astype(
            jnp.bfloat16
        )
        answers[position] = update
        if position > 0:
            first_pair = position * (position - 1) // 2
            pushed = multiply(
                pair_blocks[first_pair : first_pair + position], update, "bji,jr->bir"
            )
            pending = pending.at[:position].add(
                reached[position, :position][:, None, None] * pushed
            )
    return jnp.stack(answers)


def per_device(
    leaf_source,
    band_source,
    strip_source,
    summit_source,
    leaf_inverse,
    band_inverse,
    strip_inverse,
    summit_inverse,
    leaf_blocks,
    band_blocks,
    strip_blocks,
    summit_blocks,
    coupling,
    summit_band,
    summit_strip,
    parents,
    widths,
):
    leaf_count = leaf_source.shape[2]
    block_width = leaf_source.shape[3]
    reached = ancestors(parents[0, 0], leaf_count)
    column_ids = jnp.arange(block_width, dtype=jnp.int32)
    row_mask = (column_ids[None, :] < widths[0, 0][:, None]).astype(jnp.float32)[:, :, None]
    band_slab = summit_band.shape[1]
    column_place = lax.axis_index("pcol") * band_slab
    inverses = leaf_inverse[0, 0]
    pair_blocks = leaf_blocks[0, 0]
    to_band = band_blocks[0, 0]
    to_strip = strip_blocks[0, 0]
    to_summit = summit_blocks[0, 0]
    link_block = coupling[0, 0]
    lift_band = summit_band[0]
    lift_strip = summit_strip[0]
    current = (leaf_source[0, 0], band_source[0], strip_source[0], summit_source)
    for iteration in range(PASSES):
        leaf_now, band_now, strip_now, summit_now = current
        solved = leaf_forward(pair_blocks, inverses, leaf_now, reached, row_mask)
        band_term = multiply(to_band, solved, "aij,ajr->ir")
        strip_term = multiply(to_strip, solved, "aij,ajr->ir")
        summit_term = multiply(to_summit, solved, "aij,ajr->ir")
        band_partial = lax.psum(band_term, "pcol")
        band_solved = forward_block(band_inverse[0], band_now, band_partial)
        own_band = lax.dynamic_slice_in_dim(band_solved, column_place, band_slab, 0)
        summit_term = summit_term + multiply(lift_band, own_band, "ki,kn->in")
        strip_term = strip_term + multiply(link_block, band_solved, "ij,jn->in")
        strip_partial, summit_early = lax.psum((strip_term, summit_term), "prow")
        strip_solved = forward_block(strip_inverse[0], strip_now, strip_partial)
        summit_partial = lax.psum(
            summit_early + multiply(lift_strip, strip_solved, "ki,kn->in"), "pcol"
        )
        summit_solved = forward_block(summit_inverse, summit_now, summit_partial)
        summit_answer = backward_block(
            summit_inverse, summit_solved, jnp.zeros(summit_solved.shape, jnp.float32)
        )
        strip_answer = backward_block(
            strip_inverse[0], strip_solved, multiply(lift_strip, summit_answer, "ki,in->kn")
        )
        downward = multiply(link_block, strip_answer, "ji,jn->in")
        band_piece = multiply(lift_band, summit_answer, "ki,in->kn")
        band_back = lax.psum(downward, "pcol") + lax.all_gather(
            band_piece, "pcol", axis=0, tiled=True
        )
        band_answer = backward_block(band_inverse[0], band_solved, band_back)
        outer = (
            multiply(to_band, band_answer, "aij,ir->ajr")
            + multiply(to_strip, strip_answer, "aij,ir->ajr")
            + multiply(to_summit, summit_answer, "aij,ir->ajr")
        )
        leaf_answer = leaf_backward(pair_blocks, inverses, solved, outer, reached, row_mask)
        current = (leaf_answer, band_answer, strip_answer, summit_answer)
    return (current[0][None, None], current[1][None], current[2][None], current[3])


def solution(mesh):
    placed = (
        P("prow", "pcol", None, None, None),
        P("prow", None, None),
        P("pcol", None, None),
        P(),
        P("prow", "pcol", None, None, None),
        P("prow", None, None),
        P("pcol", None, None),
        P(),
        P("prow", "pcol", None, None, None),
        P("prow", "pcol", None, None, None),
        P("prow", "pcol", None, None, None),
        P("prow", "pcol", None, None, None),
        P("prow", "pcol", None, None),
        P("prow", "pcol", None),
        P("pcol", None, None),
        P("prow", "pcol", None),
        P("prow", "pcol", None),
    )
    return jax.shard_map(
        per_device,
        mesh=mesh,
        in_specs=placed,
        out_specs=(
            P("prow", "pcol", None, None, None),
            P("prow", None, None),
            P("pcol", None, None),
            P(),
        ),
        check_vma=False,
    )
```

profile of v0, /device:TPU:0, one launch (start us, length us, event | category | flops | bytes accessed | tf_op | source)
XLA Modules:
  0.0 482.1 jit_solution(6182447190945887679)
XLA Ops:
  13.9 1.9 constant_dynamic-update-slice_fusion.17
  15.8 2.0 constant_dynamic-update-slice_fusion.16
  17.8 2.1 constant_dynamic-update-slice_fusion.15
  19.8 2.1 constant_dynamic-update-slice_fusion.14
  21.9 2.2 constant_dynamic-update-slice_fusion.13
  25.1 2.5 constant_dynamic-update-slice_fusion.12
  28.4 2.6 constant_dynamic-update-slice_fusion.11
  31.0 2.6 constant_dynamic-update-slice_fusion.18
  33.6 2.2 convolution_bitcast_fusion.21
  40.8 2.1 convolution_bitcast_fusion.19
  43.0 2.1 convolution_bitcast_fusion.20
  45.1 35.8 %all-reduce.11.cloned.1.call-done = f32[256,128]{1,0:T(8,128)} async-done(((f32[256,128]{1,0:T(8,128)}), f32[256,128]{1,0:T(8,128)}) %all-reduce.11.cloned.1.call-update) | async-done | bytes 131088 | tf_op jit(solution)/shard_map/psum | solution.py:120
  82.1 1.8 fusion.31
  83.9 1.8 fusion.36
  87.1 54.4 %all-reduce.25.cloned.1.call-done = (f32[256,128]{1,0:T(8,128)}, f32[256,128]{1,0:T(8,128)}) async-done(((f32[256,128]{1,0:T(8,128)}, f32[256,128]{1,0:T(8,128)}), (f32[256,128]{1,0:T(8,128)}, f32[256,128]{1,0:T(8,128)})) %all-reduce.25.cloned.1.call-update) | async-done | bytes 262160 | tf_op jit(solution)/shard_map/psum | solution.py:125
  143.2 1.8 fusion.30
  146.3 40.2 %all-reduce.13.cloned.1.call-done = f32[256,128]{1,0:T(8,128)} async-done(((f32[256,128]{1,0:T(8,128)}), f32[256,128]{1,0:T(8,128)}) %all-reduce.13.cloned.1.call-update) | async-done | bytes 131088 | tf_op jit(solution)/shard_map/psum | solution.py:127
  186.5 2.0 convolution_convert_fusion.8
  188.5 1.8 convolution_convert_fusion.7
  190.3 1.7 convolution_bitcast_fusion.11
  193.0 9.1 %all_gather.6 = f32[256,128]{1,0:T(8,128)} all-gather(f32[64,128]{1,0:T(8,128)S(1)} %convolution_bitcast_fusion.24), channel_id=1, replica_groups=mesh['prow'=8,'pcol'=4] {'pcol'}, dimensions={0}, use_global_device_ids=true | all-gather | bytes 163840 | tf_op jit(solution)/shard_map/all_gather | solution.py:139
  202.1 1.7 copy.39
  203.8 30.6 %all-reduce.15.cloned.1.call-done = f32[256,128]{0,1:T(8,128)} async-done(((f32[256,128]{0,1:T(8,128)}), f32[256,128]{0,1:T(8,128)}) %all-reduce.15.cloned.1.call-update) | async-done | bytes 131088 | tf_op jit(solution)/shard_map/psum | solution.py:139
  244.6 2.0 constant_dynamic-update-slice_fusion.43
  246.6 2.1 constant_dynamic-update-slice_fusion.42
  248.7 2.2 constant_dynamic-update-slice_fusion.41
  250.9 2.3 constant_dynamic-update-slice_fusion.40
  253.2 2.4 constant_dynamic-update-slice_fusion.39
  255.6 2.5 constant_dynamic-update-slice_fusion.38
  258.1 2.6 constant_dynamic-update-slice_fusion.37
  260.7 2.7 constant_dynamic-update-slice_fusion.44
  263.4 2.2 convolution_bitcast_fusion.15
  265.6 2.2 convolution_bitcast_fusion.17
  267.9 2.2 convolution_bitcast_fusion.16
  270.0 40.1 %all-reduce.17.cloned.1.call-done = f32[256,128]{0,1:T(8,128)} async-done(((f32[256,128]{0,1:T(8,128)}), f32[256,128]{0,1:T(8,128)}) %all-reduce.17.cloned.1.call-update) | async-done | bytes 131088 | tf_op jit(solution)/shard_map/psum | solution.py:120
  311.4 1.8 fusion.35
  313.2 1.8 fusion.28
  315.1 55.6 %all-reduce.23.cloned.1.call-done = (f32[256,128]{0,1:T(8,128)}, f32[256,128]{0,1:T(8,128)}) async-done(((f32[256,128]{0,1:T(8,128)}, f32[256,128]{0,1:T(8,128)}), (f32[256,128]{0,1:T(8,128)}, f32[256,128]{0,1:T(8,128)})) %all-reduce.23.cloned.1.call-update) | async-done | bytes 262160 | tf_op jit(solution)/shard_map/psum | solution.py:125
  372.4 1.7 fusion.27
  374.2 41.4 %all-reduce.19.cloned.1.call-done = f32[256,128]{0,1:T(8,128)} async-done(((f32[256,128]{0,1:T(8,128)}), f32[256,128]{0,1:T(8,128)}) %all-reduce.19.cloned.1.call-update) | async-done | bytes 131088 | tf_op jit(solution)/shard_map/psum | solution.py:127
  415.6 2.0 convolution_convert_fusion.2
  417.6 1.8 convolution_convert_fusion.1
  419.5 1.7 convolution_bitcast_fusion.8
  422.2 1.6 copy.44
  425.4 8.8 %all_gather.7 = f32[256,128]{1,0:T(8,128)S(1)} all-gather(f32[64,128]{1,0:T(8,128)S(1)} %convolution_bitcast_fusion.23), channel_id=1, replica_groups=mesh['prow'=8,'pcol'=4] {'pcol'}, dimensions={0}, use_global_device_ids=true | all-gather | bytes 163840 | tf_op jit(solution)/shard_map/all_gather | solution.py:139
  434.2 29.4 %all-reduce.21.cloned.1.call-done = f32[256,128]{0,1:T(8,128)} async-done(((f32[256,128]{0,1:T(8,128)}), f32[256,128]{0,1:T(8,128)}) %all-reduce.21.cloned.1.call-update) | async-done | bytes 131088 | tf_op jit(solution)/shard_map/psum | solution.py:139
  466.8 1.7 convolution_add_fusion.1
  472.3 1.9 fusion.123
  (257 shorter events, 42.4 us)
Async XLA Ops:
  7.2 26.5 %copy-start = (bf16[1,1,8,256,256]{4,3,2,1,0:T(8,128)(2,1)S(1)}, bf16[1,1,8,256,256]{4,3,2,1,0:T(8,128)(2,1)}, u32[]{:S(2)}) copy-start(bf16[1,1,8,256,256]{4,3,2,1,0:T(8,128)(2,1)} %param.54) | copy-start | bytes 3145732
  7.2 73.7 %all-reduce.11.cloned.1.call-start = ((), (), s32[]{:S(2)}) async-start(), calls=%async_computation | async-start | bytes 262144 | tf_op jit(solution)/shard_map/psum | solution.py:120
  10.5 20.5 %copy-start.73 = (bf16[7]{0:T(256)(128)(2,1)}, bf16[7]{0:T(256)(128)(2,1)S(1)}, u32[]{:S(2)}) copy-start(bf16[7]{0:T(256)(128)(2,1)S(1)} %fusion.586) | copy-start | bytes 46
  10.5 17.8 %copy-start.74 = (bf16[6]{0:T(256)(128)(2,1)}, bf16[6]{0:T(256)(128)(2,1)S(1)}, u32[]{:S(2)}) copy-start(bf16[6]{0:T(256)(128)(2,1)S(1)} %fusion.585) | copy-start | bytes 40
  10.6 14.5 %copy-start.75 = (bf16[5]{0:T(256)(128)(2,1)}, bf16[5]{0:T(256)(128)(2,1)S(1)}, u32[]{:S(2)}) copy-start(bf16[5]{0:T(256)(128)(2,1)S(1)} %fusion.584) | copy-start | bytes 34
  10.6 13.6 %copy-start.76 = (bf16[4]{0:T(256)(128)(2,1)}, bf16[4]{0:T(256)(128)(2,1)S(1)}, u32[]{:S(2)}) copy-start(bf16[4]{0:T(256)(128)(2,1)S(1)} %fusion.583) | copy-start | bytes 28
  10.6 13.5 %copy-start.77 = (bf16[3]{0:T(256)(128)(2,1)}, bf16[3]{0:T(256)(128)(2,1)S(1)}, u32[]{:S(2)}) copy-start(bf16[3]{0:T(256)(128)(2,1)S(1)} %fusion.582) | copy-start | bytes 22
  10.6 13.5 %copy-start.78 = (bf16[2]{0:T(256)(128)(2,1)}, bf16[2]{0:T(256)(128)(2,1)S(1)}, u32[]{:S(2)}) copy-start(bf16[2]{0:T(256)(128)(2,1)S(1)} %fusion.581) | copy-start | bytes 16
  12.0 12.1 %copy-start.55 = (f32[1,256]{1,0:T(1,128)}, f32[1,256]{1,0:T(1,128)S(1)}, u32[]{:S(2)}) copy-start(f32[1,256]{1,0:T(1,128)S(1)} %get-tuple-element.248) | copy-start | bytes 3076
  12.0 13.1 %copy-start.45 = (f32[1,256]{1,0:T(1,128)}, f32[1,256]{1,0:T(1,128)S(1)}, u32[]{:S(2)}) copy-start(f32[1,256]{1,0:T(1,128)S(1)} %get-tuple-element.243) | copy-start | bytes 3076
  12.1 16.3 %copy-start.48 = (f32[1,256]{1,0:T(1,128)}, f32[1,256]{1,0:T(1,128)S(1)}, u32[]{:S(2)}) copy-start(f32[1,256]{1,0:T(1,128)S(1)} %get-tuple-element.242) | copy-start | bytes 3076
  12.1 18.9 %copy-start.51 = (f32[1,256]{1,0:T(1,128)}, f32[1,256]{1,0:T(1,128)S(1)}, u32[]{:S(2)}) copy-start(f32[1,256]{1,0:T(1,128)S(1)} %get-tuple-element.241) | copy-start | bytes 3076
  15.8 11.8 %copy-start.26 = (bf16[128,256]{1,0:T(8,128)(2,1)}, bf16[128,256]{1,0:T(8,128)(2,1)S(1)}, u32[]{:S(2)}) copy-start(bf16[128,256]{1,0:T(8,128)(2,1)S(1)} %get-tuple-element.249) | copy-start | bytes 196612
  17.8 9.8 %copy-start.29 = (bf16[128,256]{1,0:T(8,128)(2,1)}, bf16[128,256]{1,0:T(8,128)(2,1)S(1)}, u32[]{:S(2)}) copy-start(bf16[128,256]{1,0:T(8,128)(2,1)S(1)} %get-tuple-element.250) | copy-start | bytes 196612
  19.8 7.8 %copy-start.31 = (bf16[128,256]{1,0:T(8,128)(2,1)}, bf16[128,256]{1,0:T(8,128)(2,1)S(1)}, u32[]{:S(2)}) copy-start(bf16[128,256]{1,0:T(8,128)(2,1)S(1)} %get-tuple-element.251) | copy-start | bytes 196612
  21.9 5.7 %copy-start.34 = (bf16[128,256]{1,0:T(8,128)(2,1)}, bf16[128,256]{1,0:T(8,128)(2,1)S(1)}, u32[]{:S(2)}) copy-start(bf16[128,256]{1,0:T(8,128)(2,1)S(1)} %get-tuple-element.252) | copy-start | bytes 196612
  25.1 15.7 %copy-start.2 = (bf16[1,1,8,256,256]{4,3,2,1,0:T(8,128)(2,1)S(1)}, bf16[1,1,8,256,256]{4,3,2,1,0:T(8,128)(2,1)}, u32[]{:S(2)}) copy-start(bf16[1,1,8,256,256]{4,3,2,1,0:T(8,128)(2,1)} %param.56) | copy-start | bytes 3145732
  28.4 14.6 %copy-start.1 = (bf16[1,1,8,256,256]{4,3,2,1,0:T(8,128)(2,1)S(1)}, bf16[1,1,8,256,256]{4,3,2,1,0:T(8,128)(2,1)}, u32[]{:S(2)}) copy-start(bf16[1,1,8,256,256]{4,3,2,1,0:T(8,128)(2,1)} %param.55) | copy-start | bytes 3145732
  31.0 51.1 %copy-start.10 = (bf16[1,1,256,256]{3,2,1,0:T(8,128)(2,1)S(1)}, bf16[1,1,256,256]{3,2,1,0:T(8,128)(2,1)}, u32[]{:S(2)}) copy-start(bf16[1,1,256,256]{3,2,1,0:T(8,128)(2,1)} %param.57) | copy-start | bytes 393220
  33.6 107.8 %copy-start.8 = (bf16[1,256,256]{2,1,0:T(8,128)(2,1)S(1)}, bf16[1,256,256]{2,1,0:T(8,128)(2,1)}, u32[]{:S(2)}) copy-start(bf16[1,256,256]{2,1,0:T(8,128)(2,1)} %param.51) | copy-start | bytes 393220
  33.6 109.6 %copy-start.9 = (bf16[1,256,256]{2,1,0:T(8,128)(2,1)S(1)}, bf16[1,256,256]{2,1,0:T(8,128)(2,1)}, u32[]{:S(2)}) copy-start(bf16[1,256,256]{2,1,0:T(8,128)(2,1)} %param.59) | copy-start | bytes 393220
  35.8 105.6 %all-reduce.25.cloned.1.call-start = ((), (), s32[]{:S(2)}) async-start(), calls=%async_computation.7 | async-start | bytes 524288 | tf_op jit(solution)/shard_map/psum | solution.py:125
  85.8 100.7 %all-reduce.13.cloned.1.call-start = ((), (), s32[]{:S(2)}) async-start(), calls=%async_computation.1 | async-start | bytes 262144 | tf_op jit(solution)/shard_map/psum | solution.py:127
  145.0 89.3 %all-reduce.15.cloned.1.call-start = ((), (), s32[]{:S(2)}) async-start(), calls=%async_computation.2 | async-start | bytes 262144 | tf_op jit(solution)/shard_map/psum | solution.py:139
  192.0 118.2 %all-reduce.17.cloned.1.call-start = ((), (), s32[]{:S(2)}) async-start(), calls=%async_computation.3 | async-start | bytes 262144 | tf_op jit(solution)/shard_map/psum | solution.py:120
  234.4 3.6 copy-start.12
  236.6 2.4 copy-start.3
  236.6 2.4 copy-start.62
  238.3 1.9 copy-start.39
  238.3 1.9 copy-start.46
  238.3 2.0 copy-start.60
  239.5 2.4 copy-start.32
  240.2 1.9 copy-start.66
  240.2 2.1 copy-start.30
  240.4 2.1 copy-start.20
  240.4 2.8 copy-start.27
  240.4 2.8 copy-start.56
  267.8 102.9 %all-reduce.23.cloned.1.call-start = ((), (), s32[]{:S(2)}) async-start(), calls=%async_computation.6 | async-start | bytes 524288 | tf_op jit(solution)/shard_map/psum | solution.py:125
  311.4 1.8 copy-start.14
  315.0 100.6 %all-reduce.19.cloned.1.call-start = ((), (), s32[]{:S(2)}) async-start(), calls=%async_computation.4 | async-start | bytes 262144 | tf_op jit(solution)/shard_map/psum | solution.py:127
  374.2 89.4 %all-reduce.21.cloned.1.call-start = ((), (), s32[]{:S(2)}) async-start(), calls=%async_computation.5 | async-start | bytes 262144 | tf_op jit(solution)/shard_map/psum | solution.py:139
  419.5 47.3 %copy-start.13 = (bf16[128,256]{1,0:T(8,128)(2,1)S(1)}, bf16[128,256]{1,0:T(8,128)(2,1)}, u32[]{:S(2)}) copy-start(bf16[128,256]{1,0:T(8,128)(2,1)} %convolution_convert_fusion.1) | copy-start | bytes 196612
  419.5 49.0 %copy-start.11 = (bf16[128,256]{1,0:T(8,128)(2,1)S(1)}, bf16[128,256]{1,0:T(8,128)(2,1)}, u32[]{:S(2)}) copy-start(bf16[128,256]{1,0:T(8,128)(2,1)} %convolution_convert_fusion.2) | copy-start | bytes 196612
  466.1 2.8 copy-start.44
  466.1 2.8 copy-start.53
  466.1 3.0 copy-start.63
  466.8 2.1 copy-start.7
  466.8 2.7 copy-start.4
  (39 other events, 52.6 us)
Sparse Core Ops, SparseCore 0:
  36.0 44.9 all-reduce.10
  85.9 55.5 all-reduce.24
  145.1 41.2 all-reduce.12
  192.1 42.2 all-reduce.14
  267.9 42.2 all-reduce.16
  315.1 55.5 all-reduce.22
  374.3 41.2 all-reduce.18
  421.3 42.2 all-reduce.20
where the time goes:
time: 484 us; the launch traced here: 482 us
  waiting for transfers between devices  328 us (68%)
  matrix products  94.3 us (19%)
  local copies, waits for them, and re-layouts  22.6 us (5%)
  blocking collectives  17.8 us (4%)
  between operations  16 us (3%)
    psum x2, waiting for transfers between devices, per_device(): strip_partial, summit_early = lax.psum((strip_term, summit_term), 'prow')  110 us
    dot_general x76, matrix products, multiply(): return jnp.einsum(form, left, right, preferred_element_type=jnp.float32)  94.3 us
    psum x2, waiting for transfers between devices, per_device(): lax.psum(summit_early + multiply(lift_strip, strip_solved, 'ki,kn->in'),...  81.6 us
    psum x2, waiting for transfers between devices, per_device(): band_partial = lax.psum(band_term, 'pcol')  76 us
    psum x2, waiting for transfers between devices, per_device(): lax.psum(downward, 'pcol')  60 us
    all_gather x2, blocking collectives, per_device(): lax.all_gather(band_piece, 'pcol', axis=0, tiled=True)  17.8 us
    unnamed x175, local copies, waits for them, and re-layouts  11.7 us
  transfers between devices with their start and end apart: 8, of which 8 were waited for; matrix products, arithmetic and copies ran while one was open for 4% of the time, Pallas kernels for 0%

commit v1 on v0

v1 whole, which is shorter than its diff:
```python
import functools

import jax
import jax.numpy as jnp
from jax import lax
from jax.experimental import pallas as pl
from jax.experimental.pallas import tpu as pltpu
from jax.sharding import PartitionSpec as P

PASSES = 2
F32, BF = jnp.float32, jnp.bfloat16
VMEM = pl.BlockSpec(memory_space=pltpu.VMEM)
SMEM = pl.BlockSpec(memory_space=pltpu.SMEM)
ANY = pl.BlockSpec(memory_space=pl.ANY)


def by(rows, weights):
    return lax.dot_general(rows, weights, (((1,), (0,)), ((), ())), preferred_element_type=F32)


def by_t(rows, weights):
    return lax.dot_general(rows, weights, (((1,), (1,)), ((), ())), preferred_element_type=F32)


def fill_ancestors(parents, ancestors, leaves):
    ancestors[leaves] = 0
    for b in reversed(range(leaves)):
        ancestors[b] = jnp.left_shift(1, parents[b]) | ancestors[parents[b]]


def reach(ancestors, a, b):
    return (jnp.right_shift(ancestors[b], a) & 1).astype(F32)


def mask_of(widths, a, size):
    return (lax.broadcasted_iota(jnp.int32, (1, size), 1) < widths[a]).astype(F32)


def pair(a, b):
    return a * (a - 1) // 2 + b


class Weights:
    def __init__(self, sources, buffers, sems):
        self.sources, self.buffers, self.sems = sources, buffers, sems
        self.copies, self.waited, self.count = {}, set(), 0

    def start(self, name, first, count=1):
        src, dst = self.sources[name], self.buffers[name]
        copy = pltpu.make_async_copy(
            src.at[pl.ds(first, count)], dst.at[pl.ds(first, count)], self.sems.at[self.count]
        )
        self.count += 1
        copy.start()
        for i in range(first, first + count):
            self.copies[name, i] = copy

    def get(self, name, i):
        copy = self.copies[name, i]
        if id(copy) not in self.waited:
            self.waited.add(id(copy))
            copy.wait()
        return self.buffers[name][i]


LINKS = ("band", "strip", "summit")


def forward(w, leaves, source, widths, ancestors, pending, totals, solved):
    size = pending.shape[2]

    def push(a, b, rows):
        term = reach(ancestors, a, b) * by_t(rows, w.get("pair", pair(a, b)))
        if b:
            pending[a] += term
        else:
            pending[a] = term

    def sides(b):
        rows = solved[b]
        for a in range(b + 2, leaves):
            push(a, b, rows)
        for i, name in enumerate(LINKS):
            term = by_t(rows, w.get(name, b))
            if b:
                totals[i] += term
            else:
                totals[i] = term

    for b in range(leaves):
        mask = mask_of(widths, b, size)
        rows = source(b)
        if b:
            rows = rows - pending[b]
        rows = (mask * rows).astype(BF)
        rows = (mask * by_t(rows, w.get("inverse", b))).astype(BF)
        solved[b] = rows
        if b:
            sides(b - 1)
        if b + 1 < leaves:
            push(b + 1, b, rows)
    sides(leaves - 1)


def backward(w, leaves, tops, solved, widths, ancestors, pending, answer):
    size = pending.shape[2]

    def outer(a):
        return sum(by(top, w.get(name, a)) for top, name in zip(tops, LINKS))

    def push(a, b, rows):
        pending[b] += reach(ancestors, a, b) * by(rows, w.get("pair", pair(a, b)))

    pending[leaves - 1] = outer(leaves - 1)
    for a in reversed(range(leaves)):
        mask = mask_of(widths, a, size)
        rows = (mask * (solved[a].astype(F32) - pending[a])).astype(BF)
        rows = (mask * by(rows, w.get("inverse", a))).astype(BF)
        answer[a] = rows
        if a:
            pending[a - 1] = outer(a - 1) if a == leaves - 1 else pending[a - 1] + outer(a - 1)
            push(a, a - 1, rows)
        for b in range(a - 1):
            term = reach(ancestors, a, b) * by(rows, w.get("pair", pair(a, b)))
            if a == leaves - 1:
                pending[b] = term
            else:
                pending[b] += term


def send_pieces(place, totals, sources, outs):
    peers = len(outs)
    part = totals.shape[1] // peers
    r, c = place[0], place[1]
    counted = (c == 0, r == 0, (r == 0) & (c == 0))
    for i, (here, source) in enumerate(zip(counted, sources)):

        @pl.when(here)
        def _(i=i, source=source):
            totals[i] -= source()

    for m, out in enumerate(outs):
        rows = pl.ds(pl.multiple_of((c ^ m) * part, part), part)
        for i in range(3):
            out[pl.ds(i * part, part)] = totals[i, rows]


def join_pieces(place, pieces, tops):
    part = tops.shape[1] // len(pieces)
    for m, piece in enumerate(pieces):
        rows = pl.ds(pl.multiple_of((place[1] ^ m) * part, part), part)
        for i in range(3):
            tops[i, rows] = piece[pl.ds(i * part, part)]


def first_kernel(n, place, parents, widths, leaf_source, band_source, strip_source, summit_source, *refs):
    sources, refs = refs[:5], refs[5:]
    outs, solved, refs = refs[:n], refs[n], refs[n + 1 :]
    buffers, (pending, totals, ancestors, sems) = refs[:5], refs[5:]
    names = ("inverse", "pair") + LINKS
    w = Weights(dict(zip(names, sources)), dict(zip(names, buffers)), sems)
    leaves = leaf_source.shape[0]
    start_forward(w, leaves)
    fill_ancestors(parents, ancestors, leaves)
    forward(w, leaves, lambda b: leaf_source[b].astype(F32).T, widths, ancestors, pending, totals, solved)
    send_pieces(
        place,
        totals,
        [lambda ref=ref: ref[...].astype(F32).T for ref in (band_source, strip_source, summit_source)],
        outs,
    )


def start_forward(w, leaves):
    for b in range(leaves):
        w.start("inverse", b)
        if b + 1 < leaves:
            w.start("pair", pair(b + 1, b))
        for a in range(b + 2, leaves):
            w.start("pair", pair(a, b))
        for name in LINKS:
            w.start(name, b)


def start_backward(w, leaves):
    for a in reversed(range(leaves)):
        for name in LINKS:
            w.start(name, a)
        w.start("inverse", a)
        if a:
            w.start("pair", pair(a, 0), a)


def middle_kernel(n, last, place, parents, widths, solved_before, *refs):
    pieces, sources, refs = refs[:n], refs[n : n + 5], refs[n + 5 :]
    if last:
        leaf_answer, *top_answers = refs[:4]
        refs = refs[4:]
    else:
        outs, solved, refs = refs[:n], refs[n], refs[n + 1 :]
    buffers, (pending, totals, tops, answer, ancestors, sems) = refs[:5], refs[5:]
    names = ("inverse", "pair") + LINKS
    w = Weights(dict(zip(names, sources)), dict(zip(names, buffers)), sems)
    leaves = solved_before.shape[0]
    start_backward(w, leaves)
    fill_ancestors(parents, ancestors, leaves)
    join_pieces(place, pieces, tops)
    rows = [tops[i].astype(BF) for i in range(3)]
    backward(w, leaves, rows, solved_before, widths, ancestors, pending, answer)
    if last:
        for a in range(leaves):
            leaf_answer[a] = answer[a].astype(F32).T.astype(BF)
        for i, out in enumerate(top_answers):
            out[...] = tops[i].T.astype(BF)
    else:
        forward(w, leaves, lambda b: answer[b].astype(F32), widths, ancestors, pending, totals, solved)
        send_pieces(place, totals, [lambda i=i: tops[i] for i in range(3)], outs)


def band_kernel(n, place, inverse, lift, *refs):
    pieces, links, (solved, keep, send), (both,) = refs[:n], refs[n : 2 * n], refs[2 * n : 2 * n + 3], refs[2 * n + 3 :]
    part = solved.shape[0]
    half = keep.shape[0]

    def block(piece, i):
        return piece[pl.ds(i * part, part)]

    partial = sum(block(piece, 0) for piece in pieces)
    rows = by_t((-partial).astype(BF), inverse[...]).astype(BF)
    solved[...] = rows
    for m in range(n):
        both[pl.ds(m * part, part)] = block(pieces[m], 1) + by_t(rows, links[m][...])
    both[pl.ds(n * part, part)] = sum(block(piece, 2) for piece in pieces) + by(rows, lift[...])
    if 2 * half > (n + 1) * part:
        both[pl.ds((n + 1) * part, 2 * half - (n + 1) * part)] = jnp.zeros((2 * half - (n + 1) * part, both.shape[1]), F32)
    core = place[0] & 1
    keep[...] = both[pl.ds(pl.multiple_of(core * half, 8), half)]
    send[...] = both[pl.ds(pl.multiple_of((1 - core) * half, 8), half)]


def top_kernel(n, place, inverse, lift, summit_inverse, solved, mine, other, *refs):
    links, inverses, lifts = refs[:n], refs[n : 2 * n], refs[2 * n : 3 * n]
    outs, (both,) = refs[3 * n : 4 * n], refs[4 * n :]
    half = mine.shape[0]
    part = solved.shape[0]
    core = place[0] & 1
    both[pl.ds(pl.multiple_of(core * half, 8), half)] = mine[...]
    both[pl.ds(pl.multiple_of((1 - core) * half, 8), half)] = other[...]
    strips = [
        by_t((-both[pl.ds(m * part, part)]).astype(BF), inverses[m][...]).astype(BF) for m in range(n)
    ]
    partial = both[pl.ds(n * part, part)] + sum(by(strips[m], lifts[m][...]) for m in range(n))
    summit = by_t((-partial).astype(BF), summit_inverse[...]).astype(BF)
    summit = by(summit, summit_inverse[...]).astype(BF)
    answers = [
        by((strips[m].astype(F32) - by_t(summit, lifts[m][...])).astype(BF), inverses[m][...]).astype(BF)
        for m in range(n)
    ]
    back = by_t(summit, lift[...]) + sum(by(answers[m], links[m][...]) for m in range(n))
    band = by((solved[...].astype(F32) - back).astype(BF), inverse[...]).astype(BF)
    for m in range(n):
        outs[m][pl.ds(0, part)] = band.astype(F32)
        outs[m][pl.ds(part, part)] = answers[m].astype(F32)
        outs[m][pl.ds(2 * part, part)] = summit.astype(F32)


def gather_kernel(n, place, slab, *refs):
    pieces, links, lift = refs[: n - 1], refs[n - 1 : 2 * n - 2], refs[2 * n - 2]
    rows = slab.shape[0]
    size = lift.shape[0]
    for m in range(n):
        spot = pl.ds(pl.multiple_of((place[1] ^ m) * rows, rows), rows)
        if m:
            links[m - 1][...] = pieces[m - 1][pl.ds(0, size)].astype(BF)
            lift[spot] = pieces[m - 1][pl.ds(size, rows)].astype(BF)
        else:
            lift[spot] = slab[...]


def sort_kernel(n, place, *refs):
    k = n - 1
    mine, other, inverses, lifts = refs[:k], refs[k : 2 * k], refs[2 * k : 3 * k], refs[3 * k :]

    @pl.when(place[0] & 1 == 0)
    def _():
        for m in range(k):
            inverses[m][...] = mine[m][...].astype(BF)
            lifts[m][...] = other[m][...].astype(BF)

    @pl.when(place[0] & 1 == 1)
    def _():
        for m in range(k):
            inverses[m][...] = other[m][...].astype(BF)
            lifts[m][...] = mine[m][...].astype(BF)


def cost(flops, moved):
    return pl.CostEstimate(flops=int(flops), bytes_accessed=int(moved), transcendentals=0)


def shape_of(shape, dtype):
    return jax.ShapeDtypeStruct(tuple(shape), dtype)


def swap(array, axis, mask, size):
    return lax.ppermute(array, axis, [(i, i ^ mask) for i in range(size)])


def spread(arrays, size):
    order = sorted(range(1, size), key=lambda m: -bin(m).count("1"))
    got = {m: swap(arrays[m - 1], "pcol", m, size) for m in order}
    return [got[m] for m in range(1, size)]


def per_device(
    n_prow,
    n,
    leaf_source,
    band_source,
    strip_source,
    summit_source,
    leaf_inverse,
    band_inverse,
    strip_inverse,
    summit_inverse,
    leaf_blocks,
    band_blocks,
    strip_blocks,
    summit_blocks,
    coupling,
    summit_band,
    summit_strip,
    parents,
    widths,
):
    leaves, size, vectors = leaf_source.shape[2:]
    pairs = leaf_blocks.shape[2]
    part = vectors // n
    half = -(-(n + 1) * part // 16) * 8
    place = jnp.stack([lax.axis_index("prow"), lax.axis_index("pcol")]).astype(jnp.int32)
    block = (size, size)
    leaf_weights = (leaf_inverse[0, 0], leaf_blocks[0, 0], band_blocks[0, 0], strip_blocks[0, 0], summit_blocks[0, 0])
    buffers = [pltpu.VMEM((count,) + block, BF) for count in (leaves, pairs, leaves, leaves, leaves)]
    n_copies = 4 * leaves + pairs
    scratch = buffers + [pltpu.VMEM((leaves, vectors, size), F32), pltpu.VMEM((3, vectors, size), F32)]
    ends = [pltpu.SMEM((leaves + 1,), jnp.int32), pltpu.SemaphoreType.DMA((n_copies,))]
    pieces = [shape_of((3 * part, size), F32)] * n
    solved_shape = shape_of((leaves, vectors, size), BF)
    sweep_flops = 2 * vectors * size * size * (pairs + 4 * leaves)
    weight_bytes = 2 * size * size * (pairs + 4 * leaves)
    lists = (parents[0, 0], widths[0, 0])

    link_out = jnp.concatenate([coupling[0, 0], summit_band[0]], 0).astype(F32)
    link_in = spread([link_out] * (n - 1), n)
    core = place[0] & 1
    strip_out = jnp.where(core == 0, strip_inverse[0], summit_strip[0]).astype(F32)

    *sent, solved = pl.pallas_call(
        functools.partial(first_kernel, n),
        out_shape=pieces + [solved_shape],
        in_specs=[SMEM] * 3 + [VMEM] * 4 + [ANY] * 5,
        out_specs=[VMEM] * (n + 1),
        scratch_shapes=scratch + ends,
        cost_estimate=cost(sweep_flops, weight_bytes),
        name="first_sweep",
    )(place, *lists, leaf_source[0, 0], band_source[0], strip_source[0], summit_source, *leaf_weights)

    *links, lift = pl.pallas_call(
        functools.partial(gather_kernel, n),
        out_shape=[shape_of(block, BF)] * n,
        in_specs=[SMEM] + [VMEM] * n,
        out_specs=[VMEM] * n,
        cost_estimate=cost(0, 6 * n * size * size),
        name="gather_links",
    )(place, summit_band[0], *link_in)
    links = [coupling[0, 0]] + links

    for step in range(PASSES):
        last = step == PASSES - 1
        got = list(sent[:1]) + spread(sent[1:], n)
        if step == 0:
            strip_out, got = lax.optimization_barrier((strip_out, got))
            strip_in = spread([strip_out] * (n - 1), n)
            strip_over = [swap(array, "prow", 1, n_prow) for array in strip_in]
            sorted_in = pl.pallas_call(
                functools.partial(sort_kernel, n),
                out_shape=[shape_of(block, BF)] * (2 * n - 2),
                in_specs=[SMEM] + [VMEM] * (2 * n - 2),
                out_specs=[VMEM] * (2 * n - 2),
                cost_estimate=cost(0, 12 * n * size * size),
                name="sort_strips",
            )(place, *strip_in, *strip_over)
            inverses = [strip_inverse[0]] + list(sorted_in[: n - 1])
            lifts = [summit_strip[0]] + list(sorted_in[n - 1 :])
        band_solved, keep, send = pl.pallas_call(
            functools.partial(band_kernel, n),
            out_shape=[shape_of((part, size), BF)] + [shape_of((half, size), F32)] * 2,
            in_specs=[SMEM] + [VMEM] * (2 * n + 2),
            out_specs=[VMEM] * 3,
            scratch_shapes=[pltpu.VMEM((2 * half, size), F32)],
            cost_estimate=cost(2 * part * size * size * (n + 2), 2 * size * size * (n + 2)),
            name="band_solve",
        )(place, band_inverse[0], lift, *got, *links)
        mine = keep + swap(send, "prow", 1, n_prow)
        mask = 2
        while mask < n_prow:
            mine = mine + swap(mine, "prow", mask, n_prow)
            mask *= 2
        other = swap(mine, "prow", 1, n_prow)
        back = pl.pallas_call(
            functools.partial(top_kernel, n),
            out_shape=pieces,
            in_specs=[SMEM] + [VMEM] * (6 + 3 * n),
            out_specs=[VMEM] * n,
            scratch_shapes=[pltpu.VMEM((2 * half, size), F32)],
            cost_estimate=cost(2 * part * size * size * (5 * n + 4), 2 * size * size * (3 * n + 3)),
            name="top_solve",
        )(place, band_inverse[0], lift, summit_inverse, band_solved, mine, other, *links, *inverses, *lifts)
        tops = list(back[:1]) + spread(back[1:], n)
        if last:
            shapes = [shape_of((leaves, size, vectors), BF)] + [shape_of((size, vectors), BF)] * 3
        else:
            shapes = pieces + [solved_shape]
        results = pl.pallas_call(
            functools.partial(middle_kernel, n, last),
            out_shape=shapes,
            in_specs=[SMEM] * 3 + [VMEM] * (n + 1) + [ANY] * 5,
            out_specs=[VMEM] * len(shapes),
            scratch_shapes=scratch
            + [pltpu.VMEM((3, vectors, size), F32), pltpu.VMEM((leaves, vectors, size), BF)]
            + ends,
            cost_estimate=cost(sweep_flops * (1 if last else 2), weight_bytes),
            name="last_sweep" if last else "middle_sweep",
        )(place, *lists, solved, *tops, *leaf_weights)
        if not last:
            *sent, solved = results
    leaf_answer, band_answer, strip_answer, summit_answer = results
    return leaf_answer[None, None], band_answer[None], strip_answer[None], summit_answer


def solution(mesh):
    placed = (
        P("prow", "pcol", None, None, None),
        P("prow", None, None),
        P("pcol", None, None),
        P(),
        P("prow", "pcol", None, None, None),
        P("prow", None, None),
        P("pcol", None, None),
        P(),
        P("prow", "pcol", None, None, None),
        P("prow", "pcol", None, None, None),
        P("prow", "pcol", None, None, None),
        P("prow", "pcol", None, None, None),
        P("prow", "pcol", None, None),
        P("prow", "pcol", None),
        P("pcol", None, None),
        P("prow", "pcol", None),
        P("prow", "pcol", None),
    )
    return jax.shard_map(
        functools.partial(per_device, mesh.shape["prow"], mesh.shape["pcol"]),
        mesh=mesh,
        in_specs=placed,
        out_specs=(
            P("prow", "pcol", None, None, None),
            P("prow", None, None),
            P("pcol", None, None),
            P(),
        ),
        check_vma=False,
    )
```

time: 484 us -> 144 us (0.30)
  waiting for transfers between devices: 328 us -> 46.3 us
  matrix products: 94.3 us -> 0 us
  Pallas kernels: 0 us -> 53.9 us
  starting transfers between devices: 0.33 us -> 34 us
  blocking collectives: 17.8 us -> 0 us
  local copies, waits for them, and re-layouts: 22.6 us -> 6.17 us
  between operations: 16 us -> 1.04 us
    psum x8 -> x0, waiting for transfers between devices: 327 us -> none  [the longest x2 110 us: per_device(): strip_partial, summit_early = lax.psum((strip_term, summit_term), 'prow')]
    dot_general x76 -> x0, matrix products: 94.3 us -> none  [multiply(): return jnp.einsum(form, left, right, preferred_element_type=jnp.float32)]
    pallas_call x0 -> x9, Pallas kernels: none -> 53.9 us  [the longest x2 21.6 us: per_device(): pl.pallas_call(functools.partial(middle_kernel, n, last), out_shape=shape...]
    ppermute x0 -> x29, waiting for transfers between devices: none -> 46.3 us  [swap(): return lax.ppermute(array, axis, [(i, i ^ mask) for i in range(size)])]
    ppermute x0 -> x29, starting transfers between devices: none -> 34 us  [swap(): return lax.ppermute(array, axis, [(i, i ^ mask) for i in range(size)])]
    all_gather x2 -> x0, blocking collectives: 17.8 us -> none  [per_device(): lax.all_gather(band_piece, 'pcol', axis=0, tiled=True)]
    squeeze x6 -> x0, local copies, waits for them, and re-layouts: 7.41 us -> none  [leaf_forward(): weights = reached[position, :position].astype(jnp.bfloat16)]
    unnamed x175 -> x58, local copies, waits for them, and re-layouts: 11.7 us -> 6.17 us
  transfers between devices with their start and end apart: 8 -> 29, of which waited for: 8 -> 15; matrix products, arithmetic and copies ran while one was open for 4% -> 1% of each run, Pallas kernels for 0% -> 5%
where the time goes in v1:
time: 144 us
  Pallas kernels  53.9 us (37%)
  waiting for transfers between devices  46.3 us (32%)
  starting transfers between devices  34 us (24%)
  local copies, waits for them, and re-layouts  6.17 us (4%)
  other arithmetic  2.54 us (2%)
    ppermute x29, waiting for transfers between devices, swap(): return lax.ppermute(array, axis, [(i, i ^ mask) for i in range(size)])  46.3 us
    ppermute x29, starting transfers between devices, swap(): return lax.ppermute(array, axis, [(i, i ^ mask) for i in range(size)])  34 us
    pallas_call x2, Pallas kernels, per_device(): pl.pallas_call(functools.partial(middle_kernel, n, last), out_shape=shape...  21.6 us
    pallas_call x1, Pallas kernels, per_device(): pl.pallas_call(functools.partial(first_kernel, n), out_shape=pieces + [so...  14.6 us
    pallas_call x2, Pallas kernels, per_device(): pl.pallas_call(functools.partial(top_kernel, n), out_shape=pieces, in_spe...  8.48 us
    unnamed x58, local copies, waits for them, and re-layouts  6.17 us
    pallas_call x2, Pallas kernels, per_device(): pl.pallas_call(functools.partial(band_kernel, n), out_shape=[shape_of((pa...  4.88 us
  transfers between devices with their start and end apart: 29, of which 15 were waited for; matrix products, arithmetic and copies ran while one was open for 1% of the time, Pallas kernels for 5%

profile of v1, /device:TPU:0, one launch (start us, length us, event | category | flops | bytes accessed | tf_op | source)
XLA Modules:
  0.0 144.0 jit_solution(10842452987853644503)
XLA Ops:
  1.3 14.6 %first_sweep.1 = (f32[96,256]{1,0:T(8,128)}, f32[96,256]{1,0:T(8,128)}, f32[96,256]{1,0:T(8,128)}, f32[96,256]{1,0:T(8,128)}, bf16[8,128,256]{2,1,0:T(8,128)(2,1)}) custom-call(s32[2]{0:T(128)} %pad_add_fusion.place, s32[8]{0:T(128)} %bitcast.55, s32[8]{0:T(128)} %bitcast.58, bf16[8,256,128]{2,1,0:T(8,128)(2,1)} %bitcast.50, bf16[256,128]{1,0:T(8,128)(2,1)} %bitcast.53, ...), custom_call_target="tpu_custom_call" | custom-call | flops 1006632960 | bytes 7864320 | tf_op jit(solution)/shard_map/first_sweep/pallas_call | solution.py:358
  15.9 2.9 %collective-permute-start.3 = (f32[96,256]{1,0:T(8,128)}, f32[96,256]{1,0:T(8,128)S(1)}, u32[]{:S(2)}, u32[]{:S(2)}) collective-permute-start(f32[96,256]{1,0:T(8,128)} %get-tuple-element.50), channel_id=1, source_target_pairs={{0,1},{1,0},{2,3},{3,2},{4,5},{5,4},{6,7},{7,6},{8,9},{9,8},{10,11... | collective-permute-start | bytes 294920 | tf_op jit(solution)/shard_map/ppermute | solution.py:306
  18.9 2.0 %collective-permute-start.1 = (f32[320,256]{1,0:T(8,128)S(1)}, f32[320,256]{1,0:T(8,128)S(1)}, u32[]{:S(2)}, u32[]{:S(2)}) collective-permute-start(f32[320,256]{1,0:T(8,128)S(1)} %maximum_convert_fusion), channel_id=1, source_target_pairs={{0,2},{1,3},{2,0},{3,1},{4,6},{5,7},{6,4},{7,5},{8,10},{9,11},{10,... | collective-permute-start | bytes 983048 | tf_op jit(solution)/shard_map/ppermute | solution.py:306
  20.9 1.4 collective-permute-start.2
  22.3 1.5 %collective-permute-start.4 = (f32[96,256]{1,0:T(8,128)}, f32[96,256]{1,0:T(8,128)S(1)}, u32[]{:S(2)}, u32[]{:S(2)}) collective-permute-start(f32[96,256]{1,0:T(8,128)} %get-tuple-element.51), channel_id=1, source_target_pairs={{0,2},{1,3},{2,0},{3,1},{4,6},{5,7},{6,4},{7,5},{8,10},{9,11},{10,... | collective-permute-start | bytes 294920 | tf_op jit(solution)/shard_map/ppermute | solution.py:306
  23.8 1.7 %collective-permute-start.5 = (f32[96,256]{1,0:T(8,128)}, f32[96,256]{1,0:T(8,128)S(1)}, u32[]{:S(2)}, u32[]{:S(2)}) collective-permute-start(f32[96,256]{1,0:T(8,128)} %get-tuple-element.52), channel_id=1, source_target_pairs={{0,3},{1,2},{2,1},{3,0},{4,7},{5,6},{6,5},{7,4},{8,11},{9,10},{10,... | collective-permute-start | bytes 294920 | tf_op jit(solution)/shard_map/ppermute | solution.py:306
  25.6 13.6 %collective-permute-done.4.refs_2_ = f32[96,256]{1,0:T(8,128)S(1)} collective-permute-done((f32[96,256]{1,0:T(8,128)}, f32[96,256]{1,0:T(8,128)S(1)}, u32[]{:S(2)}, u32[]{:S(2)}) %collective-permute-start.4) | collective-permute-done | bytes 98336 | tf_op jit(solution)/shard_map/ppermute | solution.py:306
  39.2 1.7 %collective-permute-start.10 = (f32[256,256]{1,0:T(8,128)S(1)}, f32[256,256]{1,0:T(8,128)S(1)}, u32[]{:S(2)}, u32[]{:S(2)}) collective-permute-start(f32[256,256]{1,0:T(8,128)S(1)} %select_convert_fusion), channel_id=1, source_target_pairs={{0,1},{1,0},{2,3},{3,2},{4,5},{5,4},{6,7},{7,6},{8,9},{9,8},{10,11... | collective-permute-start | bytes 786440 | tf_op jit(solution)/shard_map/ppermute | solution.py:306
  40.9 1.5 %collective-permute-start.11 = (f32[256,256]{1,0:T(8,128)S(1)}, f32[256,256]{1,0:T(8,128)S(1)}, u32[]{:S(2)}, u32[]{:S(2)}) collective-permute-start(f32[256,256]{1,0:T(8,128)S(1)} %select_convert_fusion), channel_id=1, source_target_pairs={{0,2},{1,3},{2,0},{3,1},{4,6},{5,7},{6,4},{7,5},{8,10},{9,11},{10,... | collective-permute-start | bytes 786440 | tf_op jit(solution)/shard_map/ppermute | solution.py:306
  43.5 0.7 copy-done.7
  44.2 2.0 %gather_links.1 = (bf16[256,256]{1,0:T(8,128)(2,1)}, bf16[256,256]{1,0:T(8,128)(2,1)}, bf16[256,256]{1,0:T(8,128)(2,1)}, bf16[256,256]{1,0:T(8,128)(2,1)}) custom-call(s32[2]{0:T(128)} %pad_add_fusion.place, bf16[64,256]{1,0:T(8,128)(2,1)} %bitcast.51, f32[320,256]{1,0:T(8,128)} %copy-done.5, f32[320,256]{1,0:T(8,128)} %copy-done.6, f32[320,256]{1,0:T(8,128)} %copy-done.7), custom_call_target="tpu_custom_call" | custom-call | bytes 1572864 | tf_op jit(solution)/shard_map/gather_links/pallas_call | solution.py:368
  46.3 2.4 %band_solve.2 = (bf16[32,256]{1,0:T(8,128)(2,1)}, f32[80,256]{1,0:T(8,128)}, f32[80,256]{1,0:T(8,128)}) custom-call(s32[2]{0:T(128)} %pad_add_fusion.place, bf16[256,256]{1,0:T(8,128)(2,1)} %bitcast.42, bf16[256,256]{1,0:T(8,128)(2,1)} %get-tuple-element.48.lift, f32[96,256]{1,0:T(8,128)} %get-tuple-element.53.refs_0_, f32[96,256]{1,0:T(8,128)} %copy-done.21, ...), custom_call_target="tpu_custom_call" | custom-call | flops 25165824 | bytes 786432 | tf_op jit(solution)/shard_map/band_solve/pallas_call | solution.py:395
  49.2 3.7 %collective-permute-done.11.refs_1_ = f32[256,256]{1,0:T(8,128)S(1)} collective-permute-done((f32[256,256]{1,0:T(8,128)S(1)}, f32[256,256]{1,0:T(8,128)S(1)}, u32[]{:S(2)}, u32[]{:S(2)}) %collective-permute-start.11) | collective-permute-done | bytes 262176 | tf_op jit(solution)/shard_map/ppermute | solution.py:306
  53.5 0.9 add.18
  54.4 1.7 %collective-permute-start.7 = (f32[80,256]{1,0:T(8,128)S(1)}, f32[80,256]{1,0:T(8,128)S(1)}, u32[]{:S(2)}, u32[]{:S(2)}) collective-permute-start(f32[80,256]{1,0:T(8,128)S(1)} %add.18), channel_id=1, source_target_pairs={{0,8},{4,12},{8,0},{12,4},{16,24},{20,28},{24,16},{28,20},{1,9},{5... | collective-permute-start | bytes 245768 | tf_op jit(solution)/shard_map/ppermute | solution.py:306
  56.1 2.8 %collective-permute-done.7 = f32[80,256]{1,0:T(8,128)S(1)} collective-permute-done((f32[80,256]{1,0:T(8,128)S(1)}, f32[80,256]{1,0:T(8,128)S(1)}, u32[]{:S(2)}, u32[]{:S(2)}) %collective-permute-start.7) | collective-permute-done | bytes 81952 | tf_op jit(solution)/shard_map/ppermute | solution.py:306
  58.9 2.8 %collective-permute-start.8 = (f32[80,256]{1,0:T(8,128)S(1)}, f32[80,256]{1,0:T(8,128)S(1)}, u32[]{:S(2)}, u32[]{:S(2)}) collective-permute-start(f32[80,256]{1,0:T(8,128)S(1)} %add.19), channel_id=1, source_target_pairs={{0,16},{4,20},{8,24},{12,28},{16,0},{20,4},{24,8},{28,12},{1,17},{... | collective-permute-start | bytes 245768 | tf_op jit(solution)/shard_map/ppermute | solution.py:306
  61.7 2.9 %collective-permute-done.8 = f32[80,256]{1,0:T(8,128)S(1)} collective-permute-done((f32[80,256]{1,0:T(8,128)S(1)}, f32[80,256]{1,0:T(8,128)S(1)}, u32[]{:S(2)}, u32[]{:S(2)}) %collective-permute-start.8) | collective-permute-done | bytes 81952 | tf_op jit(solution)/shard_map/ppermute | solution.py:306
  65.5 0.7 copy-done.13
  66.2 2.3 %sort_strips.1 = (bf16[256,256]{1,0:T(8,128)(2,1)}, bf16[256,256]{1,0:T(8,128)(2,1)}, bf16[256,256]{1,0:T(8,128)(2,1)}, bf16[256,256]{1,0:T(8,128)(2,1)}, bf16[2...) custom-call(s32[2]{0:T(128)} %pad_add_fusion.place, f32[256,256]{1,0:T(8,128)} %copy-done.8, f32[256,256]{1,0:T(8,128)} %copy-done.9, ...), custom_call_target="tpu_custom_call" | custom-call | bytes 3145728 | tf_op jit(solution)/shard_map/sort_strips/pallas_call | solution.py:385
  69.2 4.3 %top_solve.2 = (f32[96,256]{1,0:T(8,128)}, f32[96,256]{1,0:T(8,128)}, f32[96,256]{1,0:T(8,128)}, f32[96,256]{1,0:T(8,128)}) custom-call(s32[2]{0:T(128)} %pad_add_fusion.place, bf16[256,256]{1,0:T(8,128)(2,1)} %bitcast.43, bf16[256,256]{1,0:T(8,128)(2,1)} %get-tuple-element.48.lift, bf16[256,256]{1,0:T(8,128)(2,1)} %summit_inverse.3, ...), custom_call_target="tpu_custom_call" | custom-call | flops 100663296 | bytes 1966080 | tf_op jit(solution)/shard_map/top_solve/pallas_call | solution.py:410
  73.4 0.7 collective-permute-start.16
  74.1 1.3 collective-permute-start.17
  75.4 1.6 %collective-permute-start.18 = (f32[96,256]{1,0:T(8,128)}, f32[96,256]{1,0:T(8,128)S(1)}, u32[]{:S(2)}, u32[]{:S(2)}) collective-permute-start(f32[96,256]{1,0:T(8,128)} %get-tuple-element.73), channel_id=1, source_target_pairs={{0,3},{1,2},{2,1},{3,0},{4,7},{5,6},{6,5},{7,4},{8,11},{9,10},{10,... | collective-permute-start | bytes 294920 | tf_op jit(solution)/shard_map/ppermute | solution.py:306
  77.0 2.4 %collective-permute-done.16.refs_1_ = f32[96,256]{1,0:T(8,128)S(1)} collective-permute-done((f32[96,256]{1,0:T(8,128)}, f32[96,256]{1,0:T(8,128)S(1)}, u32[]{:S(2)}, u32[]{:S(2)}) %collective-permute-start.16) | collective-permute-done | bytes 98336 | tf_op jit(solution)/shard_map/ppermute | solution.py:306
  79.4 2.1 %collective-permute-done.18.refs_3_ = f32[96,256]{1,0:T(8,128)S(1)} collective-permute-done((f32[96,256]{1,0:T(8,128)}, f32[96,256]{1,0:T(8,128)S(1)}, u32[]{:S(2)}, u32[]{:S(2)}) %collective-permute-start.18) | collective-permute-done | bytes 98336 | tf_op jit(solution)/shard_map/ppermute | solution.py:306
  82.1 12.4 %middle_sweep.1 = (f32[96,256]{1,0:T(8,128)}, f32[96,256]{1,0:T(8,128)}, f32[96,256]{1,0:T(8,128)}, f32[96,256]{1,0:T(8,128)}, bf16[8,128,256]{2,1,0:T(8,128)(2,1)}) custom-call(s32[2]{0:T(128)} %pad_add_fusion.place, s32[8]{0:T(128)} %bitcast.56, s32[8]{0:T(128)} %bitcast.59, bf16[8,128,256]{2,1,0:T(8,128)(2,1)} %get-tuple-element.47.solved_before, ...), custom_call_target="tpu_custom_call" | custom-call | flops 2013265920 | bytes 7864320 | tf_op jit(solution)/shard_map/middle_sweep/pallas_call | solution.py:424
  94.6 1.3 collective-permute-start.19
  95.9 1.1 collective-permute-start.20
  96.9 1.2 collective-permute-start.21
  98.1 2.3 %collective-permute-done.19.refs_1_ = f32[96,256]{1,0:T(8,128)S(1)} collective-permute-done((f32[96,256]{1,0:T(8,128)}, f32[96,256]{1,0:T(8,128)S(1)}, u32[]{:S(2)}, u32[]{:S(2)}) %collective-permute-start.19) | collective-permute-done | bytes 98336 | tf_op jit(solution)/shard_map/ppermute | solution.py:306
  100.4 0.7 collective-permute-done.20.refs_2_
  101.2 1.5 %collective-permute-done.21.refs_3_ = f32[96,256]{1,0:T(8,128)S(1)} collective-permute-done((f32[96,256]{1,0:T(8,128)}, f32[96,256]{1,0:T(8,128)S(1)}, u32[]{:S(2)}, u32[]{:S(2)}) %collective-permute-start.21) | collective-permute-done | bytes 98336 | tf_op jit(solution)/shard_map/ppermute | solution.py:306
  103.3 2.4 %band_solve.3 = (bf16[32,256]{1,0:T(8,128)(2,1)}, f32[80,256]{1,0:T(8,128)}, f32[80,256]{1,0:T(8,128)}) custom-call(s32[2]{0:T(128)} %pad_add_fusion.place, bf16[256,256]{1,0:T(8,128)(2,1)} %bitcast.44, bf16[256,256]{1,0:T(8,128)(2,1)} %get-tuple-element.48.lift, f32[96,256]{1,0:T(8,128)} %get-tuple-element.75.refs_0_, f32[96,256]{1,0:T(8,128)} %copy-done.24, ...), custom_call_target="tpu_custom_call" | custom-call | flops 25165824 | bytes 786432 | tf_op jit(solution)/shard_map/band_solve/pallas_call | solution.py:395
  105.7 1.5 %collective-permute-done.22 = f32[80,256]{1,0:T(8,128)S(1)} collective-permute-done((f32[80,256]{1,0:T(8,128)}, f32[80,256]{1,0:T(8,128)S(1)}, u32[]{:S(2)}, u32[]{:S(2)}) %collective-permute-start.22) | collective-permute-done | bytes 81952 | tf_op jit(solution)/shard_map/ppermute | solution.py:306
  107.2 0.9 add.21
  108.1 1.5 %collective-permute-start.23 = (f32[80,256]{1,0:T(8,128)S(1)}, f32[80,256]{1,0:T(8,128)S(1)}, u32[]{:S(2)}, u32[]{:S(2)}) collective-permute-start(f32[80,256]{1,0:T(8,128)S(1)} %add.21), channel_id=1, source_target_pairs={{0,8},{4,12},{8,0},{12,4},{16,24},{20,28},{24,16},{28,20},{1,9},{5... | collective-permute-start | bytes 245768 | tf_op jit(solution)/shard_map/ppermute | solution.py:306
  109.6 3.1 %collective-permute-done.23 = f32[80,256]{1,0:T(8,128)S(1)} collective-permute-done((f32[80,256]{1,0:T(8,128)S(1)}, f32[80,256]{1,0:T(8,128)S(1)}, u32[]{:S(2)}, u32[]{:S(2)}) %collective-permute-start.23) | collective-permute-done | bytes 81952 | tf_op jit(solution)/shard_map/ppermute | solution.py:306
  112.7 3.1 %collective-permute-start.24 = (f32[80,256]{1,0:T(8,128)S(1)}, f32[80,256]{1,0:T(8,128)S(1)}, u32[]{:S(2)}, u32[]{:S(2)}) collective-permute-start(f32[80,256]{1,0:T(8,128)S(1)} %add.22), channel_id=1, source_target_pairs={{0,16},{4,20},{8,24},{12,28},{16,0},{20,4},{24,8},{28,12},{1,17},{... | collective-permute-start | bytes 245768 | tf_op jit(solution)/shard_map/ppermute | solution.py:306
  115.8 4.0 %collective-permute-done.24 = f32[80,256]{1,0:T(8,128)S(1)} collective-permute-done((f32[80,256]{1,0:T(8,128)S(1)}, f32[80,256]{1,0:T(8,128)S(1)}, u32[]{:S(2)}, u32[]{:S(2)}) %collective-permute-start.24) | collective-permute-done | bytes 81952 | tf_op jit(solution)/shard_map/ppermute | solution.py:306
  119.9 1.3 collective-permute-done.25.other
  121.8 4.2 %top_solve.3 = (f32[96,256]{1,0:T(8,128)}, f32[96,256]{1,0:T(8,128)}, f32[96,256]{1,0:T(8,128)}, f32[96,256]{1,0:T(8,128)}) custom-call(s32[2]{0:T(128)} %pad_add_fusion.place, bf16[256,256]{1,0:T(8,128)(2,1)} %bitcast.45, bf16[256,256]{1,0:T(8,128)(2,1)} %get-tuple-element.48.lift, bf16[256,256]{1,0:T(8,128)(2,1)} %summit_inverse.3, ...), custom_call_target="tpu_custom_call" | custom-call | flops 100663296 | bytes 1966080 | tf_op jit(solution)/shard_map/top_solve/pallas_call | solution.py:410
  126.0 1.0 collective-permute-start.26
  127.0 1.0 collective-permute-start.27
  128.0 1.6 %collective-permute-start.28 = (f32[96,256]{1,0:T(8,128)}, f32[96,256]{1,0:T(8,128)S(1)}, u32[]{:S(2)}, u32[]{:S(2)}) collective-permute-start(f32[96,256]{1,0:T(8,128)} %get-tuple-element.85), channel_id=1, source_target_pairs={{0,3},{1,2},{2,1},{3,0},{4,7},{5,6},{6,5},{7,4},{8,11},{9,10},{10,... | collective-permute-start | bytes 294920 | tf_op jit(solution)/shard_map/ppermute | solution.py:306
  129.5 1.9 %collective-permute-done.26.refs_1_ = f32[96,256]{1,0:T(8,128)S(1)} collective-permute-done((f32[96,256]{1,0:T(8,128)}, f32[96,256]{1,0:T(8,128)S(1)}, u32[]{:S(2)}, u32[]{:S(2)}) %collective-permute-start.26) | collective-permute-done | bytes 98336 | tf_op jit(solution)/shard_map/ppermute | solution.py:306
  131.4 2.5 %collective-permute-done.27.refs_2_ = f32[96,256]{1,0:T(8,128)S(1)} collective-permute-done((f32[96,256]{1,0:T(8,128)}, f32[96,256]{1,0:T(8,128)S(1)}, u32[]{:S(2)}, u32[]{:S(2)}) %collective-permute-start.27) | collective-permute-done | bytes 98336 | tf_op jit(solution)/shard_map/ppermute | solution.py:306
  134.6 9.2 %last_sweep.1 = (bf16[8,256,128]{2,1,0:T(8,128)(2,1)}, bf16[256,128]{1,0:T(8,128)(2,1)}, bf16[256,128]{1,0:T(8,128)(2,1)}, bf16[256,128]{1,0:T(8,128)(2,1)}) custom-call(s32[2]{0:T(128)} %pad_add_fusion.place, s32[8]{0:T(128)} %bitcast.57, s32[8]{0:T(128)} %bitcast.60, bf16[8,128,256]{2,1,0:T(8,128)(2,1)} %get-tuple-element.74.solved_before, ...), custom_call_target="tpu_custom_call" | custom-call | flops 1006632960 | bytes 7864320 | tf_op jit(solution)/shard_map/last_sweep/pallas_call | solution.py:424
  (86 shorter events, 7.1 us)
Async XLA Ops:
  1.3 17.4 %copy-start = (bf16[1,1,256,256]{3,2,1,0:T(8,128)(2,1)S(1)}, bf16[1,1,256,256]{3,2,1,0:T(8,128)(2,1)}, u32[]{:S(2)}) copy-start(bf16[1,1,256,256]{3,2,1,0:T(8,128)(2,1)} %param.29) | copy-start | bytes 393220
  1.3 17.4 %copy-start.14 = (bf16[1,64,256]{2,1,0:T(8,128)(2,1)S(1)}, bf16[1,64,256]{2,1,0:T(8,128)(2,1)}, u32[]{:S(2)}) copy-start(bf16[1,64,256]{2,1,0:T(8,128)(2,1)} %param.30) | copy-start | bytes 98308
  1.3 24.3 %copy-start.1 = (bf16[1,256,256]{2,1,0:T(8,128)(2,1)S(1)}, bf16[1,256,256]{2,1,0:T(8,128)(2,1)}, u32[]{:S(2)}) copy-start(bf16[1,256,256]{2,1,0:T(8,128)(2,1)} %param.23) | copy-start | bytes 393220
  1.3 24.3 %copy-start.2 = (bf16[1,256,256]{2,1,0:T(8,128)(2,1)S(1)}, bf16[1,256,256]{2,1,0:T(8,128)(2,1)}, u32[]{:S(2)}) copy-start(bf16[1,256,256]{2,1,0:T(8,128)(2,1)} %param.31) | copy-start | bytes 393220
  15.9 8.0 %collective-permute-start.3 = (f32[96,256]{1,0:T(8,128)}, f32[96,256]{1,0:T(8,128)S(1)}, u32[]{:S(2)}, u32[]{:S(2)}) collective-permute-start(f32[96,256]{1,0:T(8,128)} %get-tuple-element.50), channel_id=1, source_target_pairs={{0,1},{1,0},{2,3},{3,2},{4,5},{5,4},{6,7},{7,6},{8,9},{9,8},{10,11... | collective-permute-start | bytes 294920 | tf_op jit(solution)/shard_map/ppermute | solution.py:306
  18.8 23.7 %collective-permute-start = (f32[320,256]{1,0:T(8,128)S(1)}, f32[320,256]{1,0:T(8,128)S(1)}, u32[]{:S(2)}, u32[]{:S(2)}) collective-permute-start(f32[320,256]{1,0:T(8,128)S(1)} %maximum_convert_fusion), channel_id=1, source_target_pairs={{0,1},{1,0},{2,3},{3,2},{4,5},{5,4},{6,7},{7,6},{8,9},{9,8},{10,11... | collective-permute-start | bytes 983048 | tf_op jit(solution)/shard_map/ppermute | solution.py:306
  18.9 23.9 %collective-permute-start.1 = (f32[320,256]{1,0:T(8,128)S(1)}, f32[320,256]{1,0:T(8,128)S(1)}, u32[]{:S(2)}, u32[]{:S(2)}) collective-permute-start(f32[320,256]{1,0:T(8,128)S(1)} %maximum_convert_fusion), channel_id=1, source_target_pairs={{0,2},{1,3},{2,0},{3,1},{4,6},{5,7},{6,4},{7,5},{8,10},{9,11},{10,... | collective-permute-start | bytes 983048 | tf_op jit(solution)/shard_map/ppermute | solution.py:306
  20.9 21.9 %collective-permute-start.2 = (f32[320,256]{1,0:T(8,128)S(1)}, f32[320,256]{1,0:T(8,128)S(1)}, u32[]{:S(2)}, u32[]{:S(2)}) collective-permute-start(f32[320,256]{1,0:T(8,128)S(1)} %maximum_convert_fusion), channel_id=1, source_target_pairs={{0,3},{1,2},{2,1},{3,0},{4,7},{5,6},{6,5},{7,4},{8,11},{9,10},{10,... | collective-permute-start | bytes 983048 | tf_op jit(solution)/shard_map/ppermute | solution.py:306
  22.3 16.9 %collective-permute-start.4 = (f32[96,256]{1,0:T(8,128)}, f32[96,256]{1,0:T(8,128)S(1)}, u32[]{:S(2)}, u32[]{:S(2)}) collective-permute-start(f32[96,256]{1,0:T(8,128)} %get-tuple-element.51), channel_id=1, source_target_pairs={{0,2},{1,3},{2,0},{3,1},{4,6},{5,7},{6,4},{7,5},{8,10},{9,11},{10,... | collective-permute-start | bytes 294920 | tf_op jit(solution)/shard_map/ppermute | solution.py:306
  23.8 22.4 %copy-start.21 = (f32[96,256]{1,0:T(8,128)}, f32[96,256]{1,0:T(8,128)S(1)}, u32[]{:S(2)}) copy-start(f32[96,256]{1,0:T(8,128)S(1)} %collective-permute-done.3.refs_1_) | copy-start | bytes 294916
  23.8 15.4 %collective-permute-start.5 = (f32[96,256]{1,0:T(8,128)}, f32[96,256]{1,0:T(8,128)S(1)}, u32[]{:S(2)}, u32[]{:S(2)}) collective-permute-start(f32[96,256]{1,0:T(8,128)} %get-tuple-element.52), channel_id=1, source_target_pairs={{0,3},{1,2},{2,1},{3,0},{4,7},{5,6},{6,5},{7,4},{8,11},{9,10},{10,... | collective-permute-start | bytes 294920 | tf_op jit(solution)/shard_map/ppermute | solution.py:306
  39.2 7.1 %copy-start.22 = (f32[96,256]{1,0:T(8,128)}, f32[96,256]{1,0:T(8,128)S(1)}, u32[]{:S(2)}) copy-start(f32[96,256]{1,0:T(8,128)S(1)} %collective-permute-done.4.refs_2_) | copy-start | bytes 294916
  39.2 7.1 %copy-start.23 = (f32[96,256]{1,0:T(8,128)}, f32[96,256]{1,0:T(8,128)S(1)}, u32[]{:S(2)}) copy-start(f32[96,256]{1,0:T(8,128)S(1)} %collective-permute-done.5.refs_3_) | copy-start | bytes 294916
  39.2 9.5 %collective-permute-start.10 = (f32[256,256]{1,0:T(8,128)S(1)}, f32[256,256]{1,0:T(8,128)S(1)}, u32[]{:S(2)}, u32[]{:S(2)}) collective-permute-start(f32[256,256]{1,0:T(8,128)S(1)} %select_convert_fusion), channel_id=1, source_target_pairs={{0,1},{1,0},{2,3},{3,2},{4,5},{5,4},{6,7},{7,6},{8,9},{9,8},{10,11... | collective-permute-start | bytes 786440 | tf_op jit(solution)/shard_map/ppermute | solution.py:306
  40.9 12.0 %collective-permute-start.11 = (f32[256,256]{1,0:T(8,128)S(1)}, f32[256,256]{1,0:T(8,128)S(1)}, u32[]{:S(2)}, u32[]{:S(2)}) collective-permute-start(f32[256,256]{1,0:T(8,128)S(1)} %select_convert_fusion), channel_id=1, source_target_pairs={{0,2},{1,3},{2,0},{3,1},{4,6},{5,7},{6,4},{7,5},{8,10},{9,11},{10,... | collective-permute-start | bytes 786440 | tf_op jit(solution)/shard_map/ppermute | solution.py:306
  42.5 10.5 %collective-permute-start.12 = (f32[256,256]{1,0:T(8,128)S(1)}, f32[256,256]{1,0:T(8,128)S(1)}, u32[]{:S(2)}, u32[]{:S(2)}) collective-permute-start(f32[256,256]{1,0:T(8,128)S(1)} %select_convert_fusion), channel_id=1, source_target_pairs={{0,3},{1,2},{2,1},{3,0},{4,7},{5,6},{6,5},{7,4},{8,11},{9,10},{10,... | collective-permute-start | bytes 786440 | tf_op jit(solution)/shard_map/ppermute | solution.py:306
  43.5 0.7 copy-start.7
  48.7 4.7 %collective-permute-start.6 = (f32[80,256]{1,0:T(8,128)}, f32[80,256]{1,0:T(8,128)S(1)}, u32[]{:S(2)}, u32[]{:S(2)}) collective-permute-start(f32[80,256]{1,0:T(8,128)} %get-tuple-element.62), channel_id=1, source_target_pairs={{0,4},{4,0},{8,12},{12,8},{16,20},{20,16},{24,28},{28,24},{1,5},{5... | collective-permute-start | bytes 245768 | tf_op jit(solution)/shard_map/ppermute | solution.py:306
  48.7 16.0 %copy-start.8 = (f32[256,256]{1,0:T(8,128)}, f32[256,256]{1,0:T(8,128)S(1)}, u32[]{:S(2)}) copy-start(f32[256,256]{1,0:T(8,128)S(1)} %collective-permute-done.10.refs_0_) | copy-start | bytes 786436
  48.7 16.0 %collective-permute-start.13 = (f32[256,256]{1,0:T(8,128)S(1)}, f32[256,256]{1,0:T(8,128)S(1)}, u32[]{:S(2)}, u32[]{:S(2)}) collective-permute-start(f32[256,256]{1,0:T(8,128)S(1)} %collective-permute-done.10.refs_0_), channel_id=1, source_target_pairs={{0,4},{4,0},{8,12},{12,8},{16,20},{20,16},{24,28},{28,24},{1,5},{5... | collective-permute-start | bytes 786440 | tf_op jit(solution)/shard_map/ppermute | solution.py:306
  52.9 11.8 %copy-start.9 = (f32[256,256]{1,0:T(8,128)}, f32[256,256]{1,0:T(8,128)S(1)}, u32[]{:S(2)}) copy-start(f32[256,256]{1,0:T(8,128)S(1)} %collective-permute-done.11.refs_1_) | copy-start | bytes 786436
  52.9 11.8 %collective-permute-start.14 = (f32[256,256]{1,0:T(8,128)S(1)}, f32[256,256]{1,0:T(8,128)S(1)}, u32[]{:S(2)}, u32[]{:S(2)}) collective-permute-start(f32[256,256]{1,0:T(8,128)S(1)} %collective-permute-done.11.refs_1_), channel_id=1, source_target_pairs={{0,4},{4,0},{8,12},{12,8},{16,20},{20,16},{24,28},{28,24},{1,5},{5... | collective-permute-start | bytes 786440 | tf_op jit(solution)/shard_map/ppermute | solution.py:306
  53.0 11.8 %copy-start.10 = (f32[256,256]{1,0:T(8,128)}, f32[256,256]{1,0:T(8,128)S(1)}, u32[]{:S(2)}) copy-start(f32[256,256]{1,0:T(8,128)S(1)} %collective-permute-done.12.refs_2_) | copy-start | bytes 786436
  53.0 11.8 %collective-permute-start.15 = (f32[256,256]{1,0:T(8,128)S(1)}, f32[256,256]{1,0:T(8,128)S(1)}, u32[]{:S(2)}, u32[]{:S(2)}) collective-permute-start(f32[256,256]{1,0:T(8,128)S(1)} %collective-permute-done.12.refs_2_), channel_id=1, source_target_pairs={{0,4},{4,0},{8,12},{12,8},{16,20},{20,16},{24,28},{28,24},{1,5},{5... | collective-permute-start | bytes 786440 | tf_op jit(solution)/shard_map/ppermute | solution.py:306
  54.4 4.5 %collective-permute-start.7 = (f32[80,256]{1,0:T(8,128)S(1)}, f32[80,256]{1,0:T(8,128)S(1)}, u32[]{:S(2)}, u32[]{:S(2)}) collective-permute-start(f32[80,256]{1,0:T(8,128)S(1)} %add.18), channel_id=1, source_target_pairs={{0,8},{4,12},{8,0},{12,4},{16,24},{20,28},{24,16},{28,20},{1,9},{5... | collective-permute-start | bytes 245768 | tf_op jit(solution)/shard_map/ppermute | solution.py:306
  58.9 5.7 %collective-permute-start.8 = (f32[80,256]{1,0:T(8,128)S(1)}, f32[80,256]{1,0:T(8,128)S(1)}, u32[]{:S(2)}, u32[]{:S(2)}) collective-permute-start(f32[80,256]{1,0:T(8,128)S(1)} %add.19), channel_id=1, source_target_pairs={{0,16},{4,20},{8,24},{12,28},{16,0},{20,4},{24,8},{28,12},{1,17},{... | collective-permute-start | bytes 245768 | tf_op jit(solution)/shard_map/ppermute | solution.py:306
  64.6 4.0 %copy-start.3 = (f32[80,256]{1,0:T(8,128)}, f32[80,256]{1,0:T(8,128)S(1)}, u32[]{:S(2)}) copy-start(f32[80,256]{1,0:T(8,128)S(1)} %add.20.mine) | copy-start | bytes 245764
  64.6 4.0 %collective-permute-start.9 = (f32[80,256]{1,0:T(8,128)S(1)}, f32[80,256]{1,0:T(8,128)S(1)}, u32[]{:S(2)}, u32[]{:S(2)}) collective-permute-start(f32[80,256]{1,0:T(8,128)S(1)} %add.20.mine), channel_id=1, source_target_pairs={{0,4},{4,0},{8,12},{12,8},{16,20},{20,16},{24,28},{28,24},{1,5},{5... | collective-permute-start | bytes 245768 | tf_op jit(solution)/shard_map/ppermute | solution.py:306
  64.7 0.8 copy-start.12
  73.4 5.9 %collective-permute-start.16 = (f32[96,256]{1,0:T(8,128)}, f32[96,256]{1,0:T(8,128)S(1)}, u32[]{:S(2)}, u32[]{:S(2)}) collective-permute-start(f32[96,256]{1,0:T(8,128)} %get-tuple-element.71), channel_id=1, source_target_pairs={{0,1},{1,0},{2,3},{3,2},{4,5},{5,4},{6,7},{7,6},{8,9},{9,8},{10,11... | collective-permute-start | bytes 294920 | tf_op jit(solution)/shard_map/ppermute | solution.py:306
  74.1 5.3 %collective-permute-start.17 = (f32[96,256]{1,0:T(8,128)}, f32[96,256]{1,0:T(8,128)S(1)}, u32[]{:S(2)}, u32[]{:S(2)}) collective-permute-start(f32[96,256]{1,0:T(8,128)} %get-tuple-element.72), channel_id=1, source_target_pairs={{0,2},{1,3},{2,0},{3,1},{4,6},{5,7},{6,4},{7,5},{8,10},{9,11},{10,... | collective-permute-start | bytes 294920 | tf_op jit(solution)/shard_map/ppermute | solution.py:306
  75.4 6.1 %collective-permute-start.18 = (f32[96,256]{1,0:T(8,128)}, f32[96,256]{1,0:T(8,128)S(1)}, u32[]{:S(2)}, u32[]{:S(2)}) collective-permute-start(f32[96,256]{1,0:T(8,128)} %get-tuple-element.73), channel_id=1, source_target_pairs={{0,3},{1,2},{2,1},{3,0},{4,7},{5,6},{6,5},{7,4},{8,11},{9,10},{10,... | collective-permute-start | bytes 294920 | tf_op jit(solution)/shard_map/ppermute | solution.py:306
  79.4 2.1 %copy-start.15 = (f32[96,256]{1,0:T(8,128)}, f32[96,256]{1,0:T(8,128)S(1)}, u32[]{:S(2)}) copy-start(f32[96,256]{1,0:T(8,128)S(1)} %collective-permute-done.16.refs_1_) | copy-start | bytes 294916
  79.4 2.1 %copy-start.17 = (f32[96,256]{1,0:T(8,128)}, f32[96,256]{1,0:T(8,128)S(1)}, u32[]{:S(2)}) copy-start(f32[96,256]{1,0:T(8,128)S(1)} %collective-permute-done.17.refs_2_) | copy-start | bytes 294916
  94.6 5.9 %collective-permute-start.19 = (f32[96,256]{1,0:T(8,128)}, f32[96,256]{1,0:T(8,128)S(1)}, u32[]{:S(2)}, u32[]{:S(2)}) collective-permute-start(f32[96,256]{1,0:T(8,128)} %get-tuple-element.76), channel_id=1, source_target_pairs={{0,1},{1,0},{2,3},{3,2},{4,5},{5,4},{6,7},{7,6},{8,9},{9,8},{10,11... | collective-permute-start | bytes 294920 | tf_op jit(solution)/shard_map/ppermute | solution.py:306
  95.9 5.3 %collective-permute-start.20 = (f32[96,256]{1,0:T(8,128)}, f32[96,256]{1,0:T(8,128)S(1)}, u32[]{:S(2)}, u32[]{:S(2)}) collective-permute-start(f32[96,256]{1,0:T(8,128)} %get-tuple-element.77), channel_id=1, source_target_pairs={{0,2},{1,3},{2,0},{3,1},{4,6},{5,7},{6,4},{7,5},{8,10},{9,11},{10,... | collective-permute-start | bytes 294920 | tf_op jit(solution)/shard_map/ppermute | solution.py:306
  96.9 5.7 %collective-permute-start.21 = (f32[96,256]{1,0:T(8,128)}, f32[96,256]{1,0:T(8,128)S(1)}, u32[]{:S(2)}, u32[]{:S(2)}) collective-permute-start(f32[96,256]{1,0:T(8,128)} %get-tuple-element.78), channel_id=1, source_target_pairs={{0,3},{1,2},{2,1},{3,0},{4,7},{5,6},{6,5},{7,4},{8,11},{9,10},{10,... | collective-permute-start | bytes 294920 | tf_op jit(solution)/shard_map/ppermute | solution.py:306
  100.4 2.3 %copy-start.24 = (f32[96,256]{1,0:T(8,128)}, f32[96,256]{1,0:T(8,128)S(1)}, u32[]{:S(2)}) copy-start(f32[96,256]{1,0:T(8,128)S(1)} %collective-permute-done.19.refs_1_) | copy-start | bytes 294916
  101.2 1.5 %copy-start.25 = (f32[96,256]{1,0:T(8,128)}, f32[96,256]{1,0:T(8,128)S(1)}, u32[]{:S(2)}) copy-start(f32[96,256]{1,0:T(8,128)S(1)} %collective-permute-done.20.refs_2_) | copy-start | bytes 294916
  105.7 1.5 %collective-permute-start.22 = (f32[80,256]{1,0:T(8,128)}, f32[80,256]{1,0:T(8,128)S(1)}, u32[]{:S(2)}, u32[]{:S(2)}) collective-permute-start(f32[80,256]{1,0:T(8,128)} %get-tuple-element.81), channel_id=1, source_target_pairs={{0,4},{4,0},{8,12},{12,8},{16,20},{20,16},{24,28},{28,24},{1,5},{5... | collective-permute-start | bytes 245768 | tf_op jit(solution)/shard_map/ppermute | solution.py:306
  108.1 4.6 %collective-permute-start.23 = (f32[80,256]{1,0:T(8,128)S(1)}, f32[80,256]{1,0:T(8,128)S(1)}, u32[]{:S(2)}, u32[]{:S(2)}) collective-permute-start(f32[80,256]{1,0:T(8,128)S(1)} %add.21), channel_id=1, source_target_pairs={{0,8},{4,12},{8,0},{12,4},{16,24},{20,28},{24,16},{28,20},{1,9},{5... | collective-permute-start | bytes 245768 | tf_op jit(solution)/shard_map/ppermute | solution.py:306
  112.7 7.1 %collective-permute-start.24 = (f32[80,256]{1,0:T(8,128)S(1)}, f32[80,256]{1,0:T(8,128)S(1)}, u32[]{:S(2)}, u32[]{:S(2)}) collective-permute-start(f32[80,256]{1,0:T(8,128)S(1)} %add.22), channel_id=1, source_target_pairs={{0,16},{4,20},{8,24},{12,28},{16,0},{20,4},{24,8},{28,12},{1,17},{... | collective-permute-start | bytes 245768 | tf_op jit(solution)/shard_map/ppermute | solution.py:306
  119.8 1.4 copy-start.4
  119.8 1.3 collective-permute-start.25
  126.0 5.4 %collective-permute-start.26 = (f32[96,256]{1,0:T(8,128)}, f32[96,256]{1,0:T(8,128)S(1)}, u32[]{:S(2)}, u32[]{:S(2)}) collective-permute-start(f32[96,256]{1,0:T(8,128)} %get-tuple-element.83), channel_id=1, source_target_pairs={{0,1},{1,0},{2,3},{3,2},{4,5},{5,4},{6,7},{7,6},{8,9},{9,8},{10,11... | collective-permute-start | bytes 294920 | tf_op jit(solution)/shard_map/ppermute | solution.py:306
  127.0 6.9 %collective-permute-start.27 = (f32[96,256]{1,0:T(8,128)}, f32[96,256]{1,0:T(8,128)S(1)}, u32[]{:S(2)}, u32[]{:S(2)}) collective-permute-start(f32[96,256]{1,0:T(8,128)} %get-tuple-element.84), channel_id=1, source_target_pairs={{0,2},{1,3},{2,0},{3,1},{4,6},{5,7},{6,4},{7,5},{8,10},{9,11},{10,... | collective-permute-start | bytes 294920 | tf_op jit(solution)/shard_map/ppermute | solution.py:306
  128.0 5.9 %collective-permute-start.28 = (f32[96,256]{1,0:T(8,128)}, f32[96,256]{1,0:T(8,128)S(1)}, u32[]{:S(2)}, u32[]{:S(2)}) collective-permute-start(f32[96,256]{1,0:T(8,128)} %get-tuple-element.85), channel_id=1, source_target_pairs={{0,3},{1,2},{2,1},{3,0},{4,7},{5,6},{6,5},{7,4},{8,11},{9,10},{10,... | collective-permute-start | bytes 294920 | tf_op jit(solution)/shard_map/ppermute | solution.py:306
  131.4 2.5 %copy-start.16 = (f32[96,256]{1,0:T(8,128)}, f32[96,256]{1,0:T(8,128)S(1)}, u32[]{:S(2)}) copy-start(f32[96,256]{1,0:T(8,128)S(1)} %collective-permute-done.26.refs_1_) | copy-start | bytes 294916
  (10 other events, 6.7 us)

commit v2 on v1

v2 whole, which is shorter than its diff:
```python
import functools

import jax
import jax.numpy as jnp
from jax import lax
from jax.experimental import pallas as pl
from jax.experimental.pallas import tpu as pltpu
from jax.sharding import PartitionSpec as P


PASSES = 2
F32, BF = jnp.float32, jnp.bfloat16
VMEM = pl.BlockSpec(memory_space=pltpu.VMEM)
SMEM = pl.BlockSpec(memory_space=pltpu.SMEM)
HBM = pl.BlockSpec(memory_space=pltpu.HBM)


def by(rows, weights):
    return lax.dot_general(rows, weights, (((1,), (0,)), ((), ())), preferred_element_type=F32)


def by_t(rows, weights):
    return lax.dot_general(rows, weights, (((1,), (1,)), ((), ())), preferred_element_type=F32)


def fill_ancestors(parents, ancestors, leaves):
    ancestors[leaves] = 0
    for b in reversed(range(leaves)):
        ancestors[b] = jnp.left_shift(1, parents[b]) | ancestors[parents[b]]


def reach(ancestors, a, b):
    return (jnp.right_shift(ancestors[b], a) & 1).astype(F32)


def mask_of(widths, a, size):
    return (lax.broadcasted_iota(jnp.int32, (1, size), 1) < widths[a]).astype(F32)


def pair(a, b):
    return a * (a - 1) // 2 + b


LINKS = ("band", "strip", "summit")
NAMES = ("inverse", "pair") + LINKS


def forward(w, leaves, source, widths, ancestors, pending, totals, solved):
    size = pending.shape[2]

    def push(a, b, rows):
        term = reach(ancestors, a, b) * by_t(rows, w["pair"][pair(a, b)])
        if b:
            pending[a] += term
        else:
            pending[a] = term

    def links(b):
        for i, name in enumerate(LINKS):
            term = by_t(solved[b], w[name][b])
            if b:
                totals[i] += term
            else:
                totals[i] = term

    for b in range(leaves):
        mask = mask_of(widths, b, size)
        rows = source(b)
        if b:
            rows = rows - pending[b]
        rows = (mask * rows).astype(BF)
        rows = (mask * by_t(rows, w["inverse"][b])).astype(BF)
        solved[b] = rows
        if b:
            for a in range(b + 1, leaves):
                push(a, b - 1, solved[b - 1])
            links(b - 1)
        if b + 1 < leaves:
            push(b + 1, b, rows)
    links(leaves - 1)


def backward(w, leaves, tops, solved, widths, ancestors, pending, answer):
    size = pending.shape[2]

    def outer(a):
        return sum(by(top, w[name][a]) for top, name in zip(tops, LINKS))

    def push(a, b, rows):
        pending[b] += reach(ancestors, a, b) * by(rows, w["pair"][pair(a, b)])

    pending[leaves - 1] = outer(leaves - 1)
    for a in reversed(range(leaves)):
        mask = mask_of(widths, a, size)
        rows = (mask * (solved[a].astype(F32) - pending[a])).astype(BF)
        rows = (mask * by(rows, w["inverse"][a])).astype(BF)
        answer[a] = rows
        if a:
            pending[a - 1] = outer(a - 1) if a == leaves - 1 else pending[a - 1] + outer(a - 1)
            push(a, a - 1, rows)
        for b in range(a - 1):
            term = reach(ancestors, a, b) * by(rows, w["pair"][pair(a, b)])
            if a == leaves - 1:
                pending[b] = term
            else:
                pending[b] += term


def send_pieces(totals, sources, outs):
    peers = len(outs)
    part = totals.shape[1] // peers
    r, c = lax.axis_index("prow"), lax.axis_index("pcol")
    counted = (c == 0, r == 0, (r == 0) & (c == 0))
    for i, (here, source) in enumerate(zip(counted, sources)):

        @pl.when(here)
        def _(i=i, source=source):
            totals[i] -= source

    for m, out in enumerate(outs):
        rows = pl.ds(pl.multiple_of((c ^ m) * part, part), part)
        for i in range(3):
            out[pl.ds(i * part, part)] = totals[i, rows]


def join_pieces(pieces, tops):
    part = tops.shape[1] // len(pieces)
    for m, piece in enumerate(pieces):
        rows = pl.ds(pl.multiple_of((lax.axis_index("pcol") ^ m) * part, part), part)
        for i in range(3):
            tops[i, rows] = piece[pl.ds(i * part, part)]


def first_kernel(n, parents, widths, leaf_source, band_source, strip_source, summit_source, *refs):
    sources, outs, solved, (pending, totals, ancestors) = refs[:5], refs[5 : 5 + n], refs[5 + n], refs[6 + n :]
    w = dict(zip(NAMES, sources))
    leaves = leaf_source.shape[0]
    fill_ancestors(parents, ancestors, leaves)
    forward(w, leaves, lambda b: leaf_source[b].astype(F32).T, widths, ancestors, pending, totals, solved)
    send_pieces(totals, [ref[...].astype(F32).T for ref in (band_source, strip_source, summit_source)], outs)


def middle_kernel(n, last, parents, widths, solved_from, *refs):
    pieces, sources, refs = refs[:n], refs[n : n + 5], refs[n + 5 :]
    if last:
        leaf_answer, *top_answers = refs[:4]
        refs = refs[4:]
    else:
        outs, solved, refs = refs[:n], refs[n], refs[n + 1 :]
    pending, totals, tops, answer, solved_before, ancestors, sem = refs
    w = dict(zip(NAMES, sources))
    leaves = solved_before.shape[0]
    copy = pltpu.make_async_copy(solved_from, solved_before, sem)
    copy.start()
    fill_ancestors(parents, ancestors, leaves)
    join_pieces(pieces, tops)
    rows = [tops[i].astype(BF) for i in range(3)]
    copy.wait()
    backward(w, leaves, rows, solved_before, widths, ancestors, pending, answer)
    if last:
        for a in range(leaves):
            leaf_answer[a] = answer[a].astype(F32).T.astype(BF)
        for i, out in enumerate(top_answers):
            out[...] = tops[i].T.astype(BF)
    else:
        forward(w, leaves, lambda b: answer[b].astype(F32), widths, ancestors, pending, totals, solved)
        send_pieces(totals, [tops[i] for i in range(3)], outs)


def band_kernel(n, inverse, lift, *refs):
    pieces, links, (solved, keep, send), (both,) = refs[:n], refs[n : 2 * n], refs[2 * n : 2 * n + 3], refs[2 * n + 3 :]
    part = solved.shape[0]
    half = keep.shape[0]

    def block(piece, i):
        return piece[pl.ds(i * part, part)]

    partial = sum(block(piece, 0) for piece in pieces)
    rows = by_t((-partial).astype(BF), inverse[...]).astype(BF)
    solved[...] = rows
    for m in range(n):
        both[pl.ds(m * part, part)] = block(pieces[m], 1) + by_t(rows, links[m][...])
    both[pl.ds(n * part, part)] = sum(block(piece, 2) for piece in pieces) + by(rows, lift[...])
    if 2 * half > (n + 1) * part:
        both[pl.ds((n + 1) * part, 2 * half - (n + 1) * part)] = jnp.zeros((2 * half - (n + 1) * part, both.shape[1]), F32)
    core = (lax.axis_index("prow") & 1)
    keep[...] = both[pl.ds(pl.multiple_of(core * half, 8), half)]
    send[...] = both[pl.ds(pl.multiple_of((1 - core) * half, 8), half)]


def top_kernel(n, inverse, lift, summit_inverse, solved, mine, other, *refs):
    links, inverses, lifts = refs[:n], refs[n : 2 * n], refs[2 * n : 3 * n]
    outs, (both,) = refs[3 * n : 4 * n], refs[4 * n :]
    half = mine.shape[0]
    part = solved.shape[0]
    core = (lax.axis_index("prow") & 1)
    both[pl.ds(pl.multiple_of(core * half, 8), half)] = mine[...]
    both[pl.ds(pl.multiple_of((1 - core) * half, 8), half)] = other[...]
    strips = [
        by_t((-both[pl.ds(m * part, part)]).astype(BF), inverses[m][...]).astype(BF) for m in range(n)
    ]
    partial = both[pl.ds(n * part, part)] + sum(by(strips[m], lifts[m][...]) for m in range(n))
    summit = by_t((-partial).astype(BF), summit_inverse[...]).astype(BF)
    summit = by(summit, summit_inverse[...]).astype(BF)
    answers = [
        by((strips[m].astype(F32) - by_t(summit, lifts[m][...])).astype(BF), inverses[m][...]).astype(BF)
        for m in range(n)
    ]
    back = by_t(summit, lift[...]) + sum(by(answers[m], links[m][...]) for m in range(n))
    band = by((solved[...].astype(F32) - back).astype(BF), inverse[...]).astype(BF)
    for m in range(n):
        outs[m][pl.ds(0, part)] = band.astype(F32)
        outs[m][pl.ds(part, part)] = answers[m].astype(F32)
        outs[m][pl.ds(2 * part, part)] = summit.astype(F32)


def place_kernel(core):
    core[...] = jnp.full(core.shape, lax.axis_index("prow") & 1, jnp.int32)


def gather_kernel(n, own, own_inverse, slab, *refs):
    pieces, links, (lift, link, inverse) = refs[: n - 1], refs[n - 1 : 2 * n - 2], refs[2 * n - 2 :]
    link[...] = own[...]
    inverse[...] = own_inverse[...]
    rows = slab.shape[0]
    size = lift.shape[0]
    for m in range(n):
        spot = pl.ds(pl.multiple_of((lax.axis_index("pcol") ^ m) * rows, rows), rows)
        if m:
            links[m - 1][...] = pieces[m - 1][pl.ds(0, size)].astype(BF)
            lift[spot] = pieces[m - 1][pl.ds(size, rows)].astype(BF)
        else:
            lift[spot] = slab[...]


def sort_kernel(n, *refs):
    k = n - 1
    own, refs = refs[:3], refs[3:]
    mine, other, inverses, lifts = refs[:k], refs[k : 2 * k], refs[2 * k : 3 * k], refs[3 * k : 4 * k]
    for out, value in zip(refs[4 * k :], own):
        out[...] = value[...]

    @pl.when((lax.axis_index("prow") & 1) == 0)
    def _():
        for m in range(k):
            inverses[m][...] = mine[m][...].astype(BF)
            lifts[m][...] = other[m][...].astype(BF)

    @pl.when((lax.axis_index("prow") & 1) == 1)
    def _():
        for m in range(k):
            inverses[m][...] = other[m][...].astype(BF)
            lifts[m][...] = mine[m][...].astype(BF)


def cost(flops, moved):
    return pl.CostEstimate(flops=int(flops), bytes_accessed=int(moved), transcendentals=0)


def shape_of(shape, dtype):
    return jax.ShapeDtypeStruct(tuple(shape), dtype)


def swap(array, axis, mask, size):
    return lax.ppermute(array, axis, [(i, i ^ mask) for i in range(size)])


def spread(arrays, size):
    order = sorted(range(1, size), key=lambda m: -bin(m).count("1"))
    got = {m: swap(arrays[m - 1], "pcol", m, size) for m in order}
    return [got[m] for m in range(1, size)]


def inner(
    n_prow,
    n,
    leaf_source,
    band_source,
    strip_source,
    summit_source,
    leaf_inverse,
    band_inverse,
    strip_inverse,
    summit_inverse,
    leaf_blocks,
    band_blocks,
    strip_blocks,
    summit_blocks,
    coupling,
    summit_band,
    summit_strip,
    parents,
    widths,
):
    leaves, size, vectors = leaf_source.shape[2:]
    pairs = leaf_blocks.shape[2]
    part = vectors // n
    half = -(-(n + 1) * part // 16) * 8
    block = (size, size)
    leaf_weights = (leaf_inverse[0, 0], leaf_blocks[0, 0], band_blocks[0, 0], strip_blocks[0, 0], summit_blocks[0, 0])
    small = pltpu.CompilerParams(vmem_limit_bytes=16 * 2**20)
    scratch = [pltpu.VMEM((leaves, vectors, size), F32), pltpu.VMEM((3, vectors, size), F32)]
    ends = [pltpu.SMEM((leaves + 1,), jnp.int32)]
    pieces = [shape_of((3 * part, size), F32)] * n
    solved_shape = shape_of((leaves, vectors, size), BF)
    sweep_flops = 2 * vectors * size * size * (pairs + 4 * leaves)
    weight_bytes = 2 * size * size * (pairs + 4 * leaves)
    lists = (parents[0, 0], widths[0, 0])

    place = pl.pallas_call(
        place_kernel,
        out_shape=shape_of((8, 128), jnp.int32),
        out_specs=VMEM,
        cost_estimate=cost(20 * sweep_flops, weight_bytes),
        compiler_params=small,
        name="place",
    )()
    own_link, own_slab, place = lax.optimization_barrier((coupling[0, 0], summit_band[0], place))
    link_out = jnp.concatenate([own_link, own_slab], 0).astype(F32)
    strip_out = jnp.where(place[0, 0] == 0, strip_inverse[0], summit_strip[0]).astype(F32)
    link_in = spread([link_out] * (n - 1), n)

    *sent, solved = pl.pallas_call(
        functools.partial(first_kernel, n),
        out_shape=pieces + [solved_shape],
        in_specs=[SMEM] * 2 + [VMEM] * 9,
        out_specs=[VMEM] * (n + 1),
        scratch_shapes=scratch + ends,
        cost_estimate=cost(sweep_flops, weight_bytes),
        compiler_params=small,
        name="first_sweep",
    )(*lists, leaf_source[0, 0], band_source[0], strip_source[0], summit_source, *leaf_weights)

    *links, lift, link, band_inverse = pl.pallas_call(
        functools.partial(gather_kernel, n),
        out_shape=[shape_of(block, BF)] * (n + 2),
        in_specs=[VMEM] * (n + 2),
        out_specs=[VMEM] * (n + 2),
        cost_estimate=cost(0, 6 * n * size * size),
        compiler_params=small, name="gather_links",
    )(coupling[0, 0], band_inverse[0], summit_band[0], *link_in)
    links = [link] + links

    for step in range(PASSES):
        last = step == PASSES - 1
        got = list(sent[:1]) + spread(sent[1:], n)
        if step == 0:
            strip_in = spread([strip_out] * (n - 1), n)
            strip_over = [swap(array, "prow", 1, n_prow) for array in strip_in]
            sorted_in = pl.pallas_call(
                functools.partial(sort_kernel, n),
                out_shape=[shape_of(block, BF)] * (2 * n + 1),
                in_specs=[VMEM] * (2 * n + 1),
                out_specs=[VMEM] * (2 * n + 1),
                cost_estimate=cost(0, 12 * n * size * size),
                compiler_params=small, name="sort_strips",
            )(strip_inverse[0], summit_strip[0], summit_inverse, *strip_in, *strip_over)
            inverses = [sorted_in[2 * n - 2]] + list(sorted_in[: n - 1])
            lifts = [sorted_in[2 * n - 1]] + list(sorted_in[n - 1 : 2 * n - 2])
            summit_inverse = sorted_in[2 * n]
        band_solved, keep, send = pl.pallas_call(
            functools.partial(band_kernel, n),
            out_shape=[shape_of((part, size), BF)] + [shape_of((half, size), F32)] * 2,
            in_specs=[VMEM] * (2 * n + 2),
            out_specs=[VMEM] * 3,
            scratch_shapes=[pltpu.VMEM((2 * half, size), F32)],
            cost_estimate=cost(2 * part * size * size * (n + 2), 2 * size * size * (n + 2)),
            compiler_params=small, name="band_solve",
        )(band_inverse, lift, *got, *links)
        mine = keep + swap(send, "prow", 1, n_prow)
        mask = 2
        while mask < n_prow:
            mine = mine + swap(mine, "prow", mask, n_prow)
            mask *= 2
        other = swap(mine, "prow", 1, n_prow)
        back = pl.pallas_call(
            functools.partial(top_kernel, n),
            out_shape=pieces,
            in_specs=[VMEM] * (6 + 3 * n),
            out_specs=[VMEM] * n,
            scratch_shapes=[pltpu.VMEM((2 * half, size), F32)],
            cost_estimate=cost(2 * part * size * size * (5 * n + 4), 2 * size * size * (3 * n + 3)),
            compiler_params=small, name="top_solve",
        )(band_inverse, lift, summit_inverse, band_solved, mine, other, *links, *inverses, *lifts)
        tops = list(back[:1]) + spread(back[1:], n)
        if last:
            shapes = [shape_of((leaves, size, vectors), BF)] + [shape_of((size, vectors), BF)] * 3
        else:
            shapes = pieces + [solved_shape]
        results = pl.pallas_call(
            functools.partial(middle_kernel, n, last),
            out_shape=shapes,
            in_specs=[SMEM] * 2 + [HBM] + [VMEM] * (n + 5),
            out_specs=[VMEM] * len(shapes),
            scratch_shapes=scratch
            + [pltpu.VMEM((3, vectors, size), F32)]
            + [pltpu.VMEM((leaves, vectors, size), BF)] * 2
            + ends
            + [pltpu.SemaphoreType.DMA],
            cost_estimate=cost(sweep_flops * (1 if last else 2), weight_bytes),
            compiler_params=small,
            name="last_sweep" if last else "middle_sweep",
        )(*lists, solved, *tops, *leaf_weights)
        if not last:
            *sent, solved = results
    leaf_answer, band_answer, strip_answer, summit_answer = results
    return leaf_answer[None, None], band_answer[None], strip_answer[None], summit_answer


def solution(mesh):
    placed = (
        P("prow", "pcol", None, None, None),
        P("prow", None, None),
        P("pcol", None, None),
        P(),
        P("prow", "pcol", None, None, None),
        P("prow", None, None),
        P("pcol", None, None),
        P(),
        P("prow", "pcol", None, None, None),
        P("prow", "pcol", None, None, None),
        P("prow", "pcol", None, None, None),
        P("prow", "pcol", None, None, None),
        P("prow", "pcol", None, None),
        P("prow", "pcol", None),
        P("pcol", None, None),
        P("prow", "pcol", None),
        P("prow", "pcol", None),
    )
    return jax.shard_map(
        functools.partial(inner, mesh.shape["prow"], mesh.shape["pcol"]),
        mesh=mesh,
        in_specs=placed,
        out_specs=(
            P("prow", "pcol", None, None, None),
            P("prow", None, None),
            P("pcol", None, None),
            P(),
        ),
        check_vma=False,
    )
```

time: 144 us -> 104 us (0.72)
  Pallas kernels: 53.9 us -> 18 us
  local copies, waits for them, and re-layouts: 6.17 us -> 1.36 us
  waiting for transfers between devices: 46.3 us -> 49.6 us
  other arithmetic: 2.54 us -> 0.11 us
    pallas_call x9 -> x10, Pallas kernels: 53.9 us -> 18 us  [the longest x2 9.68 us: inner(): pl.pallas_call(functools.partial(middle_kernel, n, last), out_shape=shape...]
    unnamed x58 -> x34, local copies, waits for them, and re-layouts: 6.17 us -> 0.85 us
    ppermute x29, waiting for transfers between devices: 46.3 us -> 49.6 us  [swap(): return lax.ppermute(array, axis, [(i, i ^ mask) for i in range(size)])]
    add x6, other arithmetic: 1.84 us -> 0.07 us  [the longest x4 0.04 us: inner(): mine = mine + swap(mine, 'prow', mask, n_prow)]
  transfers between devices with their start and end apart: 29 -> 29, of which waited for: 15 -> 18; matrix products, arithmetic and copies ran while one was open for 1% -> 1% of each run, Pallas kernels for 5% -> 4%
where the time goes in v2:
time: 104 us
  waiting for transfers between devices  49.6 us (48%)
  starting transfers between devices  32.9 us (32%)
  Pallas kernels  18 us (17%)
  between operations  1.85 us (2%)
  local copies, waits for them, and re-layouts  1.36 us (1%)
    ppermute x29, waiting for transfers between devices, swap(): return lax.ppermute(array, axis, [(i, i ^ mask) for i in range(size)])  49.6 us
    ppermute x29, starting transfers between devices, swap(): return lax.ppermute(array, axis, [(i, i ^ mask) for i in range(size)])  32.9 us
    pallas_call x2, Pallas kernels, inner(): pl.pallas_call(functools.partial(middle_kernel, n, last), out_shape=shape...  9.68 us
    pallas_call x2, Pallas kernels, inner(): pl.pallas_call(functools.partial(top_kernel, n), out_shape=pieces, in_spe...  3.65 us
    pallas_call x1, Pallas kernels, inner(): pl.pallas_call(functools.partial(first_kernel, n), out_shape=pieces + [so...  3.56 us
  transfers between devices with their start and end apart: 29, of which 18 were waited for; matrix products, arithmetic and copies ran while one was open for 1% of the time, Pallas kernels for 4%

profile of v2, /device:TPU:0, one launch (start us, length us, event | category | flops | bytes accessed | tf_op | source)
XLA Modules:
  0.0 103.7 jit_solution(13337168786244645738)
XLA Ops:
  0.8 0.6 copy-done.10
  1.6 4.0 %collective-permute-start.2 = (f32[320,256]{1,0:T(8,128)S(1)}, f32[320,256]{1,0:T(8,128)S(1)}, u32[]{:S(2)}, u32[]{:S(2)}) collective-permute-start(f32[320,256]{1,0:T(8,128)S(1)} %maximum_convert_fusion), channel_id=1, source_target_pairs={{0,3},{1,2},{2,1},{3,0},{4,7},{5,6},{6,5},{7,4},{8,11},{9,10},{10,... | collective-permute-start | bytes 983048 | tf_op jit(solution)/shard_map/ppermute | solution.py:265
  5.6 0.5 collective-permute-start.1
  6.3 3.6 %first_sweep.1 = (f32[96,256]{1,0:T(8,128)S(1)}, f32[96,256]{1,0:T(8,128)S(1)}, f32[96,256]{1,0:T(8,128)S(1)}, f32[96,256]{1,0:T(8,128)S(1)}, bf16[8,128,256]{2,1,0:T(8,128)(2,1)S(1)}) custom-call(s32[8]{0:T(128)S(1)} %bitcast.46, s32[8]{0:T(128)S(1)} %bitcast.49, bf16[8,256,128]{2,1,0:T(8,128)(2,1)S(1)} %bitcast.36, bf16[256,128]{1,0:T(8,128)(2,1)S(1)} %bitcast.44, ...), custom_call_target="tpu_custom_call" | custom-call | flops 1006632960 | bytes 7864320 | tf_op jit(solution)/shard_map/first_sweep/pallas_call | solution.py:323
  9.9 1.9 %collective-permute-start.9 = (f32[96,256]{1,0:T(8,128)S(1)}, f32[96,256]{1,0:T(8,128)S(1)}, u32[]{:S(2)}, u32[]{:S(2)}) collective-permute-start(f32[96,256]{1,0:T(8,128)S(1)} %get-tuple-element.58), channel_id=1, source_target_pairs={{0,1},{1,0},{2,3},{3,2},{4,5},{5,4},{6,7},{7,6},{8,9},{9,8},{10,11... | collective-permute-start | bytes 294920 | tf_op jit(solution)/shard_map/ppermute | solution.py:265
  11.9 0.5 slice.3
  13.1 1.6 %collective-permute-start.5 = (f32[256,256]{1,0:T(8,128)S(1)}, f32[256,256]{1,0:T(8,128)S(1)}, u32[]{:S(2)}, u32[]{:S(2)}) collective-permute-start(f32[256,256]{1,0:T(8,128)S(1)} %select_convert_fusion), channel_id=1, source_target_pairs={{0,3},{1,2},{2,1},{3,0},{4,7},{5,6},{6,5},{7,4},{8,11},{9,10},{10,... | collective-permute-start | bytes 786440 | tf_op jit(solution)/shard_map/ppermute | solution.py:265
  14.6 9.2 %collective-permute-done.9.refs_1_ = f32[96,256]{1,0:T(8,128)S(1)} collective-permute-done((f32[96,256]{1,0:T(8,128)S(1)}, f32[96,256]{1,0:T(8,128)S(1)}, u32[]{:S(2)}, u32[]{:S(2)}) %collective-permute-start.9) | collective-permute-done | bytes 98336 | tf_op jit(solution)/shard_map/ppermute | solution.py:265
  23.9 2.0 %collective-permute-start.3 = (f32[256,256]{1,0:T(8,128)S(1)}, f32[256,256]{1,0:T(8,128)S(1)}, u32[]{:S(2)}, u32[]{:S(2)}) collective-permute-start(f32[256,256]{1,0:T(8,128)S(1)} %select_convert_fusion), channel_id=1, source_target_pairs={{0,1},{1,0},{2,3},{3,2},{4,5},{5,4},{6,7},{7,6},{8,9},{9,8},{10,11... | collective-permute-start | bytes 786440 | tf_op jit(solution)/shard_map/ppermute | solution.py:265
  25.8 1.5 %collective-permute-start.10 = (f32[96,256]{1,0:T(8,128)S(1)}, f32[96,256]{1,0:T(8,128)S(1)}, u32[]{:S(2)}, u32[]{:S(2)}) collective-permute-start(f32[96,256]{1,0:T(8,128)S(1)} %get-tuple-element.59), channel_id=1, source_target_pairs={{0,2},{1,3},{2,0},{3,1},{4,6},{5,7},{6,4},{7,5},{8,10},{9,11},{10,... | collective-permute-start | bytes 294920 | tf_op jit(solution)/shard_map/ppermute | solution.py:265
  27.5 10.4 %collective-permute-done.10.refs_2_ = f32[96,256]{1,0:T(8,128)S(1)} collective-permute-done((f32[96,256]{1,0:T(8,128)S(1)}, f32[96,256]{1,0:T(8,128)S(1)}, u32[]{:S(2)}, u32[]{:S(2)}) %collective-permute-start.10) | collective-permute-done | bytes 98336 | tf_op jit(solution)/shard_map/ppermute | solution.py:265
  37.9 0.4 band_solve.2
  38.4 0.5 collective-permute-start.8
  39.0 0.4 collective-permute-start.6
  39.4 0.2 collective-permute-done.12
  39.7 1.8 %collective-permute-start.13 = (f32[80,256]{1,0:T(8,128)S(1)}, f32[80,256]{1,0:T(8,128)S(1)}, u32[]{:S(2)}, u32[]{:S(2)}) collective-permute-start(f32[80,256]{1,0:T(8,128)S(1)} %add.18), channel_id=1, source_target_pairs={{0,8},{4,12},{8,0},{12,4},{16,24},{20,28},{24,16},{28,20},{1,9},{5... | collective-permute-start | bytes 245768 | tf_op jit(solution)/shard_map/ppermute | solution.py:265
  41.5 2.8 %collective-permute-done.13 = f32[80,256]{1,0:T(8,128)S(1)} collective-permute-done((f32[80,256]{1,0:T(8,128)S(1)}, f32[80,256]{1,0:T(8,128)S(1)}, u32[]{:S(2)}, u32[]{:S(2)}) %collective-permute-start.13) | collective-permute-done | bytes 81952 | tf_op jit(solution)/shard_map/ppermute | solution.py:265
  44.3 2.8 %collective-permute-start.14 = (f32[80,256]{1,0:T(8,128)S(1)}, f32[80,256]{1,0:T(8,128)S(1)}, u32[]{:S(2)}, u32[]{:S(2)}) collective-permute-start(f32[80,256]{1,0:T(8,128)S(1)} %add.19), channel_id=1, source_target_pairs={{0,16},{4,20},{8,24},{12,28},{16,0},{20,4},{24,8},{28,12},{1,17},{... | collective-permute-start | bytes 245768 | tf_op jit(solution)/shard_map/ppermute | solution.py:265
  47.1 3.0 %collective-permute-done.14 = f32[80,256]{1,0:T(8,128)S(1)} collective-permute-done((f32[80,256]{1,0:T(8,128)S(1)}, f32[80,256]{1,0:T(8,128)S(1)}, u32[]{:S(2)}, u32[]{:S(2)}) %collective-permute-start.14) | collective-permute-done | bytes 81952 | tf_op jit(solution)/shard_map/ppermute | solution.py:265
  50.4 1.1 %collective-permute-done.15.other = f32[80,256]{1,0:T(8,128)S(1)} collective-permute-done((f32[80,256]{1,0:T(8,128)S(1)}, f32[80,256]{1,0:T(8,128)S(1)}, u32[]{:S(2)}, u32[]{:S(2)}) %collective-permute-start.15) | collective-permute-done | bytes 81952 | tf_op jit(solution)/shard_map/ppermute | solution.py:265
  51.5 1.8 %top_solve.2 = (f32[96,256]{1,0:T(8,128)S(1)}, f32[96,256]{1,0:T(8,128)S(1)}, f32[96,256]{1,0:T(8,128)S(1)}, f32[96,256]{1,0:T(8,128)S(1)}) custom-call(bf16[256,256]{1,0:T(8,128)(2,1)S(1)} %get-tuple-element.53.inverse, bf16[256,256]{1,0:T(8,128)(2,1)S(1)} %get-tuple-element.54.lift, bf16[256,256]{1,0:T(8,128)(2,1)S(1)} %get-tuple-element.56.summit_inverse, ...), custom_call_target="tpu_custom_call" | custom-call | flops 100663296 | bytes 1966080 | tf_op jit(solution)/shard_map/top_solve/pallas_call | solution.py:376
  53.3 1.6 %collective-permute-start.16 = (f32[96,256]{1,0:T(8,128)S(1)}, f32[96,256]{1,0:T(8,128)S(1)}, u32[]{:S(2)}, u32[]{:S(2)}) collective-permute-start(f32[96,256]{1,0:T(8,128)S(1)} %get-tuple-element.77), channel_id=1, source_target_pairs={{0,1},{1,0},{2,3},{3,2},{4,5},{5,4},{6,7},{7,6},{8,9},{9,8},{10,11... | collective-permute-start | bytes 294920 | tf_op jit(solution)/shard_map/ppermute | solution.py:265
  54.9 1.3 %collective-permute-start.17 = (f32[96,256]{1,0:T(8,128)S(1)}, f32[96,256]{1,0:T(8,128)S(1)}, u32[]{:S(2)}, u32[]{:S(2)}) collective-permute-start(f32[96,256]{1,0:T(8,128)S(1)} %get-tuple-element.78), channel_id=1, source_target_pairs={{0,2},{1,3},{2,0},{3,1},{4,6},{5,7},{6,4},{7,5},{8,10},{9,11},{10,... | collective-permute-start | bytes 294920 | tf_op jit(solution)/shard_map/ppermute | solution.py:265
  56.2 0.7 collective-permute-start.18
  56.9 1.4 %collective-permute-done.16.refs_1_ = f32[96,256]{1,0:T(8,128)S(1)} collective-permute-done((f32[96,256]{1,0:T(8,128)S(1)}, f32[96,256]{1,0:T(8,128)S(1)}, u32[]{:S(2)}, u32[]{:S(2)}) %collective-permute-start.16) | collective-permute-done | bytes 98336 | tf_op jit(solution)/shard_map/ppermute | solution.py:265
  58.2 2.3 %collective-permute-done.17.refs_2_ = f32[96,256]{1,0:T(8,128)S(1)} collective-permute-done((f32[96,256]{1,0:T(8,128)S(1)}, f32[96,256]{1,0:T(8,128)S(1)}, u32[]{:S(2)}, u32[]{:S(2)}) %collective-permute-start.17) | collective-permute-done | bytes 98336 | tf_op jit(solution)/shard_map/ppermute | solution.py:265
  60.5 1.1 %collective-permute-done.18.refs_3_ = f32[96,256]{1,0:T(8,128)S(1)} collective-permute-done((f32[96,256]{1,0:T(8,128)S(1)}, f32[96,256]{1,0:T(8,128)S(1)}, u32[]{:S(2)}, u32[]{:S(2)}) %collective-permute-start.18) | collective-permute-done | bytes 98336 | tf_op jit(solution)/shard_map/ppermute | solution.py:265
  61.7 6.0 %middle_sweep.1 = (f32[96,256]{1,0:T(8,128)S(1)}, f32[96,256]{1,0:T(8,128)S(1)}, f32[96,256]{1,0:T(8,128)S(1)}, f32[96,256]{1,0:T(8,128)S(1)}, bf16[8,128,256]{2,1,0:T(8,128)(2,1)S(1)}) custom-call(s32[8]{0:T(128)S(1)} %bitcast.47, s32[8]{0:T(128)S(1)} %bitcast.50, bf16[8,128,256]{2,1,0:T(8,128)(2,1)S(1)} %get-tuple-element.50.solved_from, ...), custom_call_target="tpu_custom_call" | custom-call | flops 2013265920 | bytes 7864320 | tf_op jit(solution)/shard_map/middle_sweep/pallas_call | solution.py:390
  67.6 0.9 collective-permute-start.19
  68.6 0.8 collective-permute-start.20
  69.4 1.8 %collective-permute-start.21 = (f32[96,256]{1,0:T(8,128)S(1)}, f32[96,256]{1,0:T(8,128)S(1)}, u32[]{:S(2)}, u32[]{:S(2)}) collective-permute-start(f32[96,256]{1,0:T(8,128)S(1)} %get-tuple-element.84), channel_id=1, source_target_pairs={{0,3},{1,2},{2,1},{3,0},{4,7},{5,6},{6,5},{7,4},{8,11},{9,10},{10,... | collective-permute-start | bytes 294920 | tf_op jit(solution)/shard_map/ppermute | solution.py:265
  71.2 2.0 %collective-permute-done.19.refs_1_ = f32[96,256]{1,0:T(8,128)S(1)} collective-permute-done((f32[96,256]{1,0:T(8,128)S(1)}, f32[96,256]{1,0:T(8,128)S(1)}, u32[]{:S(2)}, u32[]{:S(2)}) %collective-permute-start.19) | collective-permute-done | bytes 98336 | tf_op jit(solution)/shard_map/ppermute | solution.py:265
  73.2 0.7 collective-permute-done.20.refs_2_
  73.9 1.1 %collective-permute-done.21.refs_3_ = f32[96,256]{1,0:T(8,128)S(1)} collective-permute-done((f32[96,256]{1,0:T(8,128)S(1)}, f32[96,256]{1,0:T(8,128)S(1)}, u32[]{:S(2)}, u32[]{:S(2)}) %collective-permute-start.21) | collective-permute-done | bytes 98336 | tf_op jit(solution)/shard_map/ppermute | solution.py:265
  74.9 0.4 band_solve.3
  75.4 1.3 %collective-permute-done.22 = f32[80,256]{1,0:T(8,128)S(1)} collective-permute-done((f32[80,256]{1,0:T(8,128)S(1)}, f32[80,256]{1,0:T(8,128)S(1)}, u32[]{:S(2)}, u32[]{:S(2)}) %collective-permute-start.22) | collective-permute-done | bytes 81952 | tf_op jit(solution)/shard_map/ppermute | solution.py:265
  76.7 1.5 %collective-permute-start.23 = (f32[80,256]{1,0:T(8,128)S(1)}, f32[80,256]{1,0:T(8,128)S(1)}, u32[]{:S(2)}, u32[]{:S(2)}) collective-permute-start(f32[80,256]{1,0:T(8,128)S(1)} %add.21), channel_id=1, source_target_pairs={{0,8},{4,12},{8,0},{12,4},{16,24},{20,28},{24,16},{28,20},{1,9},{5... | collective-permute-start | bytes 245768 | tf_op jit(solution)/shard_map/ppermute | solution.py:265
  78.2 3.1 %collective-permute-done.23 = f32[80,256]{1,0:T(8,128)S(1)} collective-permute-done((f32[80,256]{1,0:T(8,128)S(1)}, f32[80,256]{1,0:T(8,128)S(1)}, u32[]{:S(2)}, u32[]{:S(2)}) %collective-permute-start.23) | collective-permute-done | bytes 81952 | tf_op jit(solution)/shard_map/ppermute | solution.py:265
  81.3 3.1 %collective-permute-start.24 = (f32[80,256]{1,0:T(8,128)S(1)}, f32[80,256]{1,0:T(8,128)S(1)}, u32[]{:S(2)}, u32[]{:S(2)}) collective-permute-start(f32[80,256]{1,0:T(8,128)S(1)} %add.22), channel_id=1, source_target_pairs={{0,16},{4,20},{8,24},{12,28},{16,0},{20,4},{24,8},{28,12},{1,17},{... | collective-permute-start | bytes 245768 | tf_op jit(solution)/shard_map/ppermute | solution.py:265
  84.4 4.0 %collective-permute-done.24 = f32[80,256]{1,0:T(8,128)S(1)} collective-permute-done((f32[80,256]{1,0:T(8,128)S(1)}, f32[80,256]{1,0:T(8,128)S(1)}, u32[]{:S(2)}, u32[]{:S(2)}) %collective-permute-start.24) | collective-permute-done | bytes 81952 | tf_op jit(solution)/shard_map/ppermute | solution.py:265
  88.5 1.3 %collective-permute-done.25.other = f32[80,256]{1,0:T(8,128)S(1)} collective-permute-done((f32[80,256]{1,0:T(8,128)S(1)}, f32[80,256]{1,0:T(8,128)S(1)}, u32[]{:S(2)}, u32[]{:S(2)}) %collective-permute-start.25) | collective-permute-done | bytes 81952 | tf_op jit(solution)/shard_map/ppermute | solution.py:265
  89.7 1.8 %top_solve.3 = (f32[96,256]{1,0:T(8,128)S(1)}, f32[96,256]{1,0:T(8,128)S(1)}, f32[96,256]{1,0:T(8,128)S(1)}, f32[96,256]{1,0:T(8,128)S(1)}) custom-call(bf16[256,256]{1,0:T(8,128)(2,1)S(1)} %get-tuple-element.53.inverse, bf16[256,256]{1,0:T(8,128)(2,1)S(1)} %get-tuple-element.54.lift, bf16[256,256]{1,0:T(8,128)(2,1)S(1)} %get-tuple-element.56.summit_inverse, ...), custom_call_target="tpu_custom_call" | custom-call | flops 100663296 | bytes 1966080 | tf_op jit(solution)/shard_map/top_solve/pallas_call | solution.py:376
  91.6 1.6 %collective-permute-start.26 = (f32[96,256]{1,0:T(8,128)S(1)}, f32[96,256]{1,0:T(8,128)S(1)}, u32[]{:S(2)}, u32[]{:S(2)}) collective-permute-start(f32[96,256]{1,0:T(8,128)S(1)} %get-tuple-element.89), channel_id=1, source_target_pairs={{0,1},{1,0},{2,3},{3,2},{4,5},{5,4},{6,7},{7,6},{8,9},{9,8},{10,11... | collective-permute-start | bytes 294920 | tf_op jit(solution)/shard_map/ppermute | solution.py:265
  93.1 0.8 collective-permute-start.27
  94.0 1.2 %collective-permute-start.28 = (f32[96,256]{1,0:T(8,128)S(1)}, f32[96,256]{1,0:T(8,128)S(1)}, u32[]{:S(2)}, u32[]{:S(2)}) collective-permute-start(f32[96,256]{1,0:T(8,128)S(1)} %get-tuple-element.91), channel_id=1, source_target_pairs={{0,3},{1,2},{2,1},{3,0},{4,7},{5,6},{6,5},{7,4},{8,11},{9,10},{10,... | collective-permute-start | bytes 294920 | tf_op jit(solution)/shard_map/ppermute | solution.py:265
  95.1 1.4 %collective-permute-done.26.refs_1_ = f32[96,256]{1,0:T(8,128)S(1)} collective-permute-done((f32[96,256]{1,0:T(8,128)S(1)}, f32[96,256]{1,0:T(8,128)S(1)}, u32[]{:S(2)}, u32[]{:S(2)}) %collective-permute-start.26) | collective-permute-done | bytes 98336 | tf_op jit(solution)/shard_map/ppermute | solution.py:265
  96.5 3.4 %collective-permute-done.27.refs_2_ = f32[96,256]{1,0:T(8,128)S(1)} collective-permute-done((f32[96,256]{1,0:T(8,128)S(1)}, f32[96,256]{1,0:T(8,128)S(1)}, u32[]{:S(2)}, u32[]{:S(2)}) %collective-permute-start.27) | collective-permute-done | bytes 98336 | tf_op jit(solution)/shard_map/ppermute | solution.py:265
  99.9 3.7 %last_sweep.1 = (bf16[8,256,128]{2,1,0:T(8,128)(2,1)}, bf16[256,128]{1,0:T(8,128)(2,1)}, bf16[256,128]{1,0:T(8,128)(2,1)}, bf16[256,128]{1,0:T(8,128)(2,1)}) custom-call(s32[8]{0:T(128)S(1)} %bitcast.48, s32[8]{0:T(128)S(1)} %bitcast.51, bf16[8,128,256]{2,1,0:T(8,128)(2,1)S(1)} %get-tuple-element.80.solved_from, f32[96,256]{1,0:T(8,128)S(1)} %get-tuple-element.88.refs_0_, ...), custom_call_target="tpu_custom_call" | custom-call | flops 1006632960 | bytes 7864320 | tf_op jit(solution)/shard_map/last_sweep/pallas_call | solution.py:390
  (63 shorter events, 1.2 us)
Async XLA Ops:
  0.6 0.8 copy-start.10
  0.6 0.9 copy-start.6
  0.7 5.6 %copy-start.16 = (s32[1,1,8]{2,1,0:T(1,128)S(1)}, s32[1,1,8]{2,1,0:T(1,128)}, u32[]{:S(2)}) copy-start(s32[1,1,8]{2,1,0:T(1,128)} %param.33) | copy-start | bytes 100
  0.7 5.6 %copy-start.15 = (s32[1,1,8]{2,1,0:T(1,128)S(1)}, s32[1,1,8]{2,1,0:T(1,128)}, u32[]{:S(2)}) copy-start(s32[1,1,8]{2,1,0:T(1,128)} %param.32) | copy-start | bytes 100
  0.7 5.6 %copy-start.4 = (bf16[1,1,8,256,256]{4,3,2,1,0:T(8,128)(2,1)S(1)}, bf16[1,1,8,256,256]{4,3,2,1,0:T(8,128)(2,1)}, u32[]{:S(2)}) copy-start(bf16[1,1,8,256,256]{4,3,2,1,0:T(8,128)(2,1)} %param.28) | copy-start | bytes 3145732
  0.7 5.5 %copy-start.3 = (bf16[1,1,8,256,256]{4,3,2,1,0:T(8,128)(2,1)S(1)}, bf16[1,1,8,256,256]{4,3,2,1,0:T(8,128)(2,1)}, u32[]{:S(2)}) copy-start(bf16[1,1,8,256,256]{4,3,2,1,0:T(8,128)(2,1)} %param.27) | copy-start | bytes 3145732
  0.7 5.5 %copy-start.2 = (bf16[1,1,8,256,256]{4,3,2,1,0:T(8,128)(2,1)S(1)}, bf16[1,1,8,256,256]{4,3,2,1,0:T(8,128)(2,1)}, u32[]{:S(2)}) copy-start(bf16[1,1,8,256,256]{4,3,2,1,0:T(8,128)(2,1)} %param.26) | copy-start | bytes 3145732
  0.7 5.5 %copy-start = (bf16[1,1,28,256,256]{4,3,2,1,0:T(8,128)(2,1)S(1)}, bf16[1,1,28,256,256]{4,3,2,1,0:T(8,128)(2,1)}, u32[]{:S(2)}) copy-start(bf16[1,1,28,256,256]{4,3,2,1,0:T(8,128)(2,1)} %param.25) | copy-start | bytes 11010052
  0.7 5.5 %copy-start.1 = (bf16[1,1,8,256,256]{4,3,2,1,0:T(8,128)(2,1)S(1)}, bf16[1,1,8,256,256]{4,3,2,1,0:T(8,128)(2,1)}, u32[]{:S(2)}) copy-start(bf16[1,1,8,256,256]{4,3,2,1,0:T(8,128)(2,1)} %param.21) | copy-start | bytes 3145732
  0.7 5.5 %copy-start.14 = (bf16[256,128]{1,0:T(8,128)(2,1)S(1)}, bf16[256,128]{1,0:T(8,128)(2,1)}, u32[]{:S(2)}) copy-start(bf16[256,128]{1,0:T(8,128)(2,1)} %summit_source.1) | copy-start | bytes 196612
  0.7 5.5 %copy-start.13 = (bf16[1,256,128]{2,1,0:T(8,128)(2,1)S(1)}, bf16[1,256,128]{2,1,0:T(8,128)(2,1)}, u32[]{:S(2)}) copy-start(bf16[1,256,128]{2,1,0:T(8,128)(2,1)} %param.19) | copy-start | bytes 196612
  0.7 5.5 %copy-start.12 = (bf16[1,256,128]{2,1,0:T(8,128)(2,1)S(1)}, bf16[1,256,128]{2,1,0:T(8,128)(2,1)}, u32[]{:S(2)}) copy-start(bf16[1,256,128]{2,1,0:T(8,128)(2,1)} %param.18) | copy-start | bytes 196612
  0.8 5.5 %copy-start.5 = (bf16[1,1,8,256,128]{4,3,2,1,0:T(8,128)(2,1)S(1)}, bf16[1,1,8,256,128]{4,3,2,1,0:T(8,128)(2,1)}, u32[]{:S(2)}) copy-start(bf16[1,1,8,256,128]{4,3,2,1,0:T(8,128)(2,1)} %param.17) | copy-start | bytes 1572868
  1.6 22.3 %collective-permute-start.2 = (f32[320,256]{1,0:T(8,128)S(1)}, f32[320,256]{1,0:T(8,128)S(1)}, u32[]{:S(2)}, u32[]{:S(2)}) collective-permute-start(f32[320,256]{1,0:T(8,128)S(1)} %maximum_convert_fusion), channel_id=1, source_target_pairs={{0,3},{1,2},{2,1},{3,0},{4,7},{5,6},{6,5},{7,4},{8,11},{9,10},{10,... | collective-permute-start | bytes 983048 | tf_op jit(solution)/shard_map/ppermute | solution.py:265
  5.6 20.3 %collective-permute-start.1 = (f32[320,256]{1,0:T(8,128)S(1)}, f32[320,256]{1,0:T(8,128)S(1)}, u32[]{:S(2)}, u32[]{:S(2)}) collective-permute-start(f32[320,256]{1,0:T(8,128)S(1)} %maximum_convert_fusion), channel_id=1, source_target_pairs={{0,2},{1,3},{2,0},{3,1},{4,6},{5,7},{6,4},{7,5},{8,10},{9,11},{10,... | collective-permute-start | bytes 983048 | tf_op jit(solution)/shard_map/ppermute | solution.py:265
  6.1 21.2 %collective-permute-start = (f32[320,256]{1,0:T(8,128)S(1)}, f32[320,256]{1,0:T(8,128)S(1)}, u32[]{:S(2)}, u32[]{:S(2)}) collective-permute-start(f32[320,256]{1,0:T(8,128)S(1)} %maximum_convert_fusion), channel_id=1, source_target_pairs={{0,1},{1,0},{2,3},{3,2},{4,5},{5,4},{6,7},{7,6},{8,9},{9,8},{10,11... | collective-permute-start | bytes 983048 | tf_op jit(solution)/shard_map/ppermute | solution.py:265
  6.3 6.7 %copy-start.7 = (bf16[1,256,256]{2,1,0:T(8,128)(2,1)S(1)}, bf16[1,256,256]{2,1,0:T(8,128)(2,1)}, u32[]{:S(2)}) copy-start(bf16[1,256,256]{2,1,0:T(8,128)(2,1)} %param.23) | copy-start | bytes 393220
  6.3 6.7 %copy-start.8 = (bf16[1,256,256]{2,1,0:T(8,128)(2,1)S(1)}, bf16[1,256,256]{2,1,0:T(8,128)(2,1)}, u32[]{:S(2)}) copy-start(bf16[1,256,256]{2,1,0:T(8,128)(2,1)} %param.31) | copy-start | bytes 393220
  6.3 21.1 %copy-start.9 = (bf16[1,256,256]{2,1,0:T(8,128)(2,1)S(1)}, bf16[1,256,256]{2,1,0:T(8,128)(2,1)}, u32[]{:S(2)}) copy-start(bf16[1,256,256]{2,1,0:T(8,128)(2,1)} %param.22) | copy-start | bytes 393220
  9.9 40.3 %copy-start.11 = (bf16[256,256]{1,0:T(8,128)(2,1)S(1)}, bf16[256,256]{1,0:T(8,128)(2,1)}, u32[]{:S(2)}) copy-start(bf16[256,256]{1,0:T(8,128)(2,1)} %refs_2_.1) | copy-start | bytes 393220
  9.9 13.9 %collective-permute-start.9 = (f32[96,256]{1,0:T(8,128)S(1)}, f32[96,256]{1,0:T(8,128)S(1)}, u32[]{:S(2)}, u32[]{:S(2)}) collective-permute-start(f32[96,256]{1,0:T(8,128)S(1)} %get-tuple-element.58), channel_id=1, source_target_pairs={{0,1},{1,0},{2,3},{3,2},{4,5},{5,4},{6,7},{7,6},{8,9},{9,8},{10,11... | collective-permute-start | bytes 294920 | tf_op jit(solution)/shard_map/ppermute | solution.py:265
  13.1 25.4 %collective-permute-start.5 = (f32[256,256]{1,0:T(8,128)S(1)}, f32[256,256]{1,0:T(8,128)S(1)}, u32[]{:S(2)}, u32[]{:S(2)}) collective-permute-start(f32[256,256]{1,0:T(8,128)S(1)} %select_convert_fusion), channel_id=1, source_target_pairs={{0,3},{1,2},{2,1},{3,0},{4,7},{5,6},{6,5},{7,4},{8,11},{9,10},{10,... | collective-permute-start | bytes 786440 | tf_op jit(solution)/shard_map/ppermute | solution.py:265
  23.8 15.1 %collective-permute-start.4 = (f32[256,256]{1,0:T(8,128)S(1)}, f32[256,256]{1,0:T(8,128)S(1)}, u32[]{:S(2)}, u32[]{:S(2)}) collective-permute-start(f32[256,256]{1,0:T(8,128)S(1)} %select_convert_fusion), channel_id=1, source_target_pairs={{0,2},{1,3},{2,0},{3,1},{4,6},{5,7},{6,4},{7,5},{8,10},{9,11},{10,... | collective-permute-start | bytes 786440 | tf_op jit(solution)/shard_map/ppermute | solution.py:265
  23.9 15.1 %collective-permute-start.3 = (f32[256,256]{1,0:T(8,128)S(1)}, f32[256,256]{1,0:T(8,128)S(1)}, u32[]{:S(2)}, u32[]{:S(2)}) collective-permute-start(f32[256,256]{1,0:T(8,128)S(1)} %select_convert_fusion), channel_id=1, source_target_pairs={{0,1},{1,0},{2,3},{3,2},{4,5},{5,4},{6,7},{7,6},{8,9},{9,8},{10,11... | collective-permute-start | bytes 786440 | tf_op jit(solution)/shard_map/ppermute | solution.py:265
  25.8 12.1 %collective-permute-start.10 = (f32[96,256]{1,0:T(8,128)S(1)}, f32[96,256]{1,0:T(8,128)S(1)}, u32[]{:S(2)}, u32[]{:S(2)}) collective-permute-start(f32[96,256]{1,0:T(8,128)S(1)} %get-tuple-element.59), channel_id=1, source_target_pairs={{0,2},{1,3},{2,0},{3,1},{4,6},{5,7},{6,4},{7,5},{8,10},{9,11},{10,... | collective-permute-start | bytes 294920 | tf_op jit(solution)/shard_map/ppermute | solution.py:265
  27.3 10.6 %collective-permute-start.11 = (f32[96,256]{1,0:T(8,128)S(1)}, f32[96,256]{1,0:T(8,128)S(1)}, u32[]{:S(2)}, u32[]{:S(2)}) collective-permute-start(f32[96,256]{1,0:T(8,128)S(1)} %get-tuple-element.60), channel_id=1, source_target_pairs={{0,3},{1,2},{2,1},{3,0},{4,7},{5,6},{6,5},{7,4},{8,11},{9,10},{10,... | collective-permute-start | bytes 294920 | tf_op jit(solution)/shard_map/ppermute | solution.py:265
  38.3 1.3 %collective-permute-start.12 = (f32[80,256]{1,0:T(8,128)S(1)}, f32[80,256]{1,0:T(8,128)S(1)}, u32[]{:S(2)}, u32[]{:S(2)}) collective-permute-start(f32[80,256]{1,0:T(8,128)S(1)} %get-tuple-element.67), channel_id=1, source_target_pairs={{0,4},{4,0},{8,12},{12,8},{16,20},{20,16},{24,28},{28,24},{1,5},{5... | collective-permute-start | bytes 245768 | tf_op jit(solution)/shard_map/ppermute | solution.py:265
  38.4 11.8 %collective-permute-start.8 = (f32[256,256]{1,0:T(8,128)S(1)}, f32[256,256]{1,0:T(8,128)S(1)}, u32[]{:S(2)}, u32[]{:S(2)}) collective-permute-start(f32[256,256]{1,0:T(8,128)S(1)} %collective-permute-done.5.refs_5_), channel_id=1, source_target_pairs={{0,4},{4,0},{8,12},{12,8},{16,20},{20,16},{24,28},{28,24},{1,5},{5... | collective-permute-start | bytes 786440 | tf_op jit(solution)/shard_map/ppermute | solution.py:265
  38.9 11.3 %collective-permute-start.7 = (f32[256,256]{1,0:T(8,128)S(1)}, f32[256,256]{1,0:T(8,128)S(1)}, u32[]{:S(2)}, u32[]{:S(2)}) collective-permute-start(f32[256,256]{1,0:T(8,128)S(1)} %collective-permute-done.4.refs_4_), channel_id=1, source_target_pairs={{0,4},{4,0},{8,12},{12,8},{16,20},{20,16},{24,28},{28,24},{1,5},{5... | collective-permute-start | bytes 786440 | tf_op jit(solution)/shard_map/ppermute | solution.py:265
  39.0 11.2 %collective-permute-start.6 = (f32[256,256]{1,0:T(8,128)S(1)}, f32[256,256]{1,0:T(8,128)S(1)}, u32[]{:S(2)}, u32[]{:S(2)}) collective-permute-start(f32[256,256]{1,0:T(8,128)S(1)} %collective-permute-done.3.refs_3_), channel_id=1, source_target_pairs={{0,4},{4,0},{8,12},{12,8},{16,20},{20,16},{24,28},{28,24},{1,5},{5... | collective-permute-start | bytes 786440 | tf_op jit(solution)/shard_map/ppermute | solution.py:265
  39.7 4.6 %collective-permute-start.13 = (f32[80,256]{1,0:T(8,128)S(1)}, f32[80,256]{1,0:T(8,128)S(1)}, u32[]{:S(2)}, u32[]{:S(2)}) collective-permute-start(f32[80,256]{1,0:T(8,128)S(1)} %add.18), channel_id=1, source_target_pairs={{0,8},{4,12},{8,0},{12,4},{16,24},{20,28},{24,16},{28,20},{1,9},{5... | collective-permute-start | bytes 245768 | tf_op jit(solution)/shard_map/ppermute | solution.py:265
  44.3 5.8 %collective-permute-start.14 = (f32[80,256]{1,0:T(8,128)S(1)}, f32[80,256]{1,0:T(8,128)S(1)}, u32[]{:S(2)}, u32[]{:S(2)}) collective-permute-start(f32[80,256]{1,0:T(8,128)S(1)} %add.19), channel_id=1, source_target_pairs={{0,16},{4,20},{8,24},{12,28},{16,0},{20,4},{24,8},{28,12},{1,17},{... | collective-permute-start | bytes 245768 | tf_op jit(solution)/shard_map/ppermute | solution.py:265
  50.1 1.3 %collective-permute-start.15 = (f32[80,256]{1,0:T(8,128)S(1)}, f32[80,256]{1,0:T(8,128)S(1)}, u32[]{:S(2)}, u32[]{:S(2)}) collective-permute-start(f32[80,256]{1,0:T(8,128)S(1)} %add.20.mine), channel_id=1, source_target_pairs={{0,4},{4,0},{8,12},{12,8},{16,20},{20,16},{24,28},{28,24},{1,5},{5... | collective-permute-start | bytes 245768 | tf_op jit(solution)/shard_map/ppermute | solution.py:265
  53.3 4.9 %collective-permute-start.16 = (f32[96,256]{1,0:T(8,128)S(1)}, f32[96,256]{1,0:T(8,128)S(1)}, u32[]{:S(2)}, u32[]{:S(2)}) collective-permute-start(f32[96,256]{1,0:T(8,128)S(1)} %get-tuple-element.77), channel_id=1, source_target_pairs={{0,1},{1,0},{2,3},{3,2},{4,5},{5,4},{6,7},{7,6},{8,9},{9,8},{10,11... | collective-permute-start | bytes 294920 | tf_op jit(solution)/shard_map/ppermute | solution.py:265
  54.9 5.7 %collective-permute-start.17 = (f32[96,256]{1,0:T(8,128)S(1)}, f32[96,256]{1,0:T(8,128)S(1)}, u32[]{:S(2)}, u32[]{:S(2)}) collective-permute-start(f32[96,256]{1,0:T(8,128)S(1)} %get-tuple-element.78), channel_id=1, source_target_pairs={{0,2},{1,3},{2,0},{3,1},{4,6},{5,7},{6,4},{7,5},{8,10},{9,11},{10,... | collective-permute-start | bytes 294920 | tf_op jit(solution)/shard_map/ppermute | solution.py:265
  56.2 5.5 %collective-permute-start.18 = (f32[96,256]{1,0:T(8,128)S(1)}, f32[96,256]{1,0:T(8,128)S(1)}, u32[]{:S(2)}, u32[]{:S(2)}) collective-permute-start(f32[96,256]{1,0:T(8,128)S(1)} %get-tuple-element.79), channel_id=1, source_target_pairs={{0,3},{1,2},{2,1},{3,0},{4,7},{5,6},{6,5},{7,4},{8,11},{9,10},{10,... | collective-permute-start | bytes 294920 | tf_op jit(solution)/shard_map/ppermute | solution.py:265
  67.6 5.5 %collective-permute-start.19 = (f32[96,256]{1,0:T(8,128)S(1)}, f32[96,256]{1,0:T(8,128)S(1)}, u32[]{:S(2)}, u32[]{:S(2)}) collective-permute-start(f32[96,256]{1,0:T(8,128)S(1)} %get-tuple-element.82), channel_id=1, source_target_pairs={{0,1},{1,0},{2,3},{3,2},{4,5},{5,4},{6,7},{7,6},{8,9},{9,8},{10,11... | collective-permute-start | bytes 294920 | tf_op jit(solution)/shard_map/ppermute | solution.py:265
  68.6 5.3 %collective-permute-start.20 = (f32[96,256]{1,0:T(8,128)S(1)}, f32[96,256]{1,0:T(8,128)S(1)}, u32[]{:S(2)}, u32[]{:S(2)}) collective-permute-start(f32[96,256]{1,0:T(8,128)S(1)} %get-tuple-element.83), channel_id=1, source_target_pairs={{0,2},{1,3},{2,0},{3,1},{4,6},{5,7},{6,4},{7,5},{8,10},{9,11},{10,... | collective-permute-start | bytes 294920 | tf_op jit(solution)/shard_map/ppermute | solution.py:265
  69.4 5.5 %collective-permute-start.21 = (f32[96,256]{1,0:T(8,128)S(1)}, f32[96,256]{1,0:T(8,128)S(1)}, u32[]{:S(2)}, u32[]{:S(2)}) collective-permute-start(f32[96,256]{1,0:T(8,128)S(1)} %get-tuple-element.84), channel_id=1, source_target_pairs={{0,3},{1,2},{2,1},{3,0},{4,7},{5,6},{6,5},{7,4},{8,11},{9,10},{10,... | collective-permute-start | bytes 294920 | tf_op jit(solution)/shard_map/ppermute | solution.py:265
  75.4 1.3 %collective-permute-start.22 = (f32[80,256]{1,0:T(8,128)S(1)}, f32[80,256]{1,0:T(8,128)S(1)}, u32[]{:S(2)}, u32[]{:S(2)}) collective-permute-start(f32[80,256]{1,0:T(8,128)S(1)} %get-tuple-element.87), channel_id=1, source_target_pairs={{0,4},{4,0},{8,12},{12,8},{16,20},{20,16},{24,28},{28,24},{1,5},{5... | collective-permute-start | bytes 245768 | tf_op jit(solution)/shard_map/ppermute | solution.py:265
  76.7 4.6 %collective-permute-start.23 = (f32[80,256]{1,0:T(8,128)S(1)}, f32[80,256]{1,0:T(8,128)S(1)}, u32[]{:S(2)}, u32[]{:S(2)}) collective-permute-start(f32[80,256]{1,0:T(8,128)S(1)} %add.21), channel_id=1, source_target_pairs={{0,8},{4,12},{8,0},{12,4},{16,24},{20,28},{24,16},{28,20},{1,9},{5... | collective-permute-start | bytes 245768 | tf_op jit(solution)/shard_map/ppermute | solution.py:265
  81.3 7.1 %collective-permute-start.24 = (f32[80,256]{1,0:T(8,128)S(1)}, f32[80,256]{1,0:T(8,128)S(1)}, u32[]{:S(2)}, u32[]{:S(2)}) collective-permute-start(f32[80,256]{1,0:T(8,128)S(1)} %add.22), channel_id=1, source_target_pairs={{0,16},{4,20},{8,24},{12,28},{16,0},{20,4},{24,8},{28,12},{1,17},{... | collective-permute-start | bytes 245768 | tf_op jit(solution)/shard_map/ppermute | solution.py:265
  88.4 1.3 %collective-permute-start.25 = (f32[80,256]{1,0:T(8,128)S(1)}, f32[80,256]{1,0:T(8,128)S(1)}, u32[]{:S(2)}, u32[]{:S(2)}) collective-permute-start(f32[80,256]{1,0:T(8,128)S(1)} %add.23.mine), channel_id=1, source_target_pairs={{0,4},{4,0},{8,12},{12,8},{16,20},{20,16},{24,28},{28,24},{1,5},{5... | collective-permute-start | bytes 245768 | tf_op jit(solution)/shard_map/ppermute | solution.py:265
  91.6 4.9 %collective-permute-start.26 = (f32[96,256]{1,0:T(8,128)S(1)}, f32[96,256]{1,0:T(8,128)S(1)}, u32[]{:S(2)}, u32[]{:S(2)}) collective-permute-start(f32[96,256]{1,0:T(8,128)S(1)} %get-tuple-element.89), channel_id=1, source_target_pairs={{0,1},{1,0},{2,3},{3,2},{4,5},{5,4},{6,7},{7,6},{8,9},{9,8},{10,11... | collective-permute-start | bytes 294920 | tf_op jit(solution)/shard_map/ppermute | solution.py:265
  93.1 6.7 %collective-permute-start.27 = (f32[96,256]{1,0:T(8,128)S(1)}, f32[96,256]{1,0:T(8,128)S(1)}, u32[]{:S(2)}, u32[]{:S(2)}) collective-permute-start(f32[96,256]{1,0:T(8,128)S(1)} %get-tuple-element.90), channel_id=1, source_target_pairs={{0,2},{1,3},{2,0},{3,1},{4,6},{5,7},{6,4},{7,5},{8,10},{9,11},{10,... | collective-permute-start | bytes 294920 | tf_op jit(solution)/shard_map/ppermute | solution.py:265
  94.0 5.9 %collective-permute-start.28 = (f32[96,256]{1,0:T(8,128)S(1)}, f32[96,256]{1,0:T(8,128)S(1)}, u32[]{:S(2)}, u32[]{:S(2)}) collective-permute-start(f32[96,256]{1,0:T(8,128)S(1)} %get-tuple-element.91), channel_id=1, source_target_pairs={{0,3},{1,2},{2,1},{3,0},{4,7},{5,6},{6,5},{7,4},{8,11},{9,10},{10,... | collective-permute-start | bytes 294920 | tf_op jit(solution)/shard_map/ppermute | solution.py:265

commit v3 on v2

--- a/solution.py
+++ b/solution.py
@@ -9,6 +9,7 @@
 
 
 PASSES = 2
+FEW = 4
 F32, BF = jnp.float32, jnp.bfloat16
 VMEM = pl.BlockSpec(memory_space=pltpu.VMEM)
 SMEM = pl.BlockSpec(memory_space=pltpu.SMEM)
@@ -80,30 +81,50 @@
     links(leaves - 1)
 
 
-def backward(w, leaves, tops, solved, widths, ancestors, pending, answer):
-    size = pending.shape[2]
-
-    def outer(a):
-        return sum(by(top, w[name][a]) for top, name in zip(tops, LINKS))
-
-    def push(a, b, rows):
-        pending[b] += reach(ancestors, a, b) * by(rows, w["pair"][pair(a, b)])
-
-    pending[leaves - 1] = outer(leaves - 1)
+def invert_kernel(first, parents, widths, inverse, pairs, *refs):
+    stack, scaled, terms, ancestors = refs[-4:]
+    leaves, size = inverse.shape[:2]
+    rows_here = scaled.shape[0]
+    fill_ancestors(parents, ancestors, leaves)
+
+    def span(first, last):
+        return pl.ds(first * size, (last - first) * size)
+
+    for i in range(rows_here):
+        a = first + i
+        mask = mask_of(widths, a, size)
+        rows = (lax.broadcasted_iota(jnp.int32, (size, 1), 0) < widths[a]).astype(F32)
+        stack[a, span(a, a + 1)] = (rows * inverse[a].astype(F32) * mask).astype(BF)
+        for k in range(a):
+            weight = jnp.full((1, size), reach(ancestors, a, k), F32).astype(BF)
+            scaled[i, :, span(k, k + 1)] = pairs[pair(a, k)] * weight
+    for i in range(rows_here):
+        a = first + i
+        if not a:
+            continue
+        for b in reversed(range(a)):
+            terms[:, span(b, b + 1)] = by(scaled[i, :, span(b, a)], stack[b, span(b, a)]).astype(BF)
+        rows = -by(stack[a, span(a, a + 1)], terms[:, span(0, a)])
+        for b in range(a):
+            stack[b, span(a, a + 1)] = rows[:, b * size : (b + 1) * size].astype(BF)
+
+
+def forward_again(stack, links, source, totals, solved):
+    leaves, size = stack.shape[0], stack.shape[2]
+    for a in range(leaves):
+        rows = sum(by_t(source(b), stack[b, pl.ds(a * size, size)]) for b in range(a + 1))
+        solved[a] = rows.astype(BF)
+    for i, link in enumerate(links):
+        totals[i] = sum(by_t(solved[a], link[a]) for a in range(leaves))
+
+
+def backward(stack, links, tops, solved, residual, put):
+    leaves, size = stack.shape[0], stack.shape[2]
     for a in reversed(range(leaves)):
-        mask = mask_of(widths, a, size)
-        rows = (mask * (solved[a].astype(F32) - pending[a])).astype(BF)
-        rows = (mask * by(rows, w["inverse"][a])).astype(BF)
-        answer[a] = rows
-        if a:
-            pending[a - 1] = outer(a - 1) if a == leaves - 1 else pending[a - 1] + outer(a - 1)
-            push(a, a - 1, rows)
-        for b in range(a - 1):
-            term = reach(ancestors, a, b) * by(rows, w["pair"][pair(a, b)])
-            if a == leaves - 1:
-                pending[b] = term
-            else:
-                pending[b] += term
+        outer = sum(by(top, link[a]) for top, link in zip(tops, links))
+        residual[:, pl.ds(a * size, size)] = (solved[a].astype(F32) - outer).astype(BF)
+        rest = pl.ds(a * size, (leaves - a) * size)
+        put(a, by(residual[:, rest], stack[a, rest]).astype(BF))
 
 
 def send_pieces(totals, sources, outs):
@@ -140,30 +161,27 @@
     send_pieces(totals, [ref[...].astype(F32).T for ref in (band_source, strip_source, summit_source)], outs)
 
 
-def middle_kernel(n, last, parents, widths, solved_from, *refs):
-    pieces, sources, refs = refs[:n], refs[n : n + 5], refs[n + 5 :]
+def middle_kernel(n, last, solved_before, *refs):
+    pieces, stack, links, refs = refs[:n], refs[n], refs[n + 1 : n + 4], refs[n + 4 :]
     if last:
         leaf_answer, *top_answers = refs[:4]
-        refs = refs[4:]
+        tops, residual = refs[4:]
     else:
-        outs, solved, refs = refs[:n], refs[n], refs[n + 1 :]
-    pending, totals, tops, answer, solved_before, ancestors, sem = refs
-    w = dict(zip(NAMES, sources))
-    leaves = solved_before.shape[0]
-    copy = pltpu.make_async_copy(solved_from, solved_before, sem)
-    copy.start()
-    fill_ancestors(parents, ancestors, leaves)
+        outs, solved, (tops, residual, answer, totals) = refs[:n], refs[n], refs[n + 1 :]
     join_pieces(pieces, tops)
-    rows = [tops[i].astype(BF) for i in range(3)]
-    copy.wait()
-    backward(w, leaves, rows, solved_before, widths, ancestors, pending, answer)
+
+    def put(a, rows):
+        if last:
+            leaf_answer[a] = rows.astype(F32).T.astype(BF)
+        else:
+            answer[a] = rows
+
+    backward(stack, links, [tops[i].astype(BF) for i in range(3)], solved_before, residual, put)
     if last:
-        for a in range(leaves):
-            leaf_answer[a] = answer[a].astype(F32).T.astype(BF)
         for i, out in enumerate(top_answers):
             out[...] = tops[i].T.astype(BF)
     else:
-        forward(w, leaves, lambda b: answer[b].astype(F32), widths, ancestors, pending, totals, solved)
+        forward_again(stack, links, lambda b: answer[b], totals, solved)
         send_pieces(totals, [tops[i] for i in range(3)], outs)
 
 
@@ -218,39 +236,38 @@
     core[...] = jnp.full(core.shape, lax.axis_index("prow") & 1, jnp.int32)
 
 
-def gather_kernel(n, own, own_inverse, slab, *refs):
-    pieces, links, (lift, link, inverse) = refs[: n - 1], refs[n - 1 : 2 * n - 2], refs[2 * n - 2 :]
+def gather_kernel(counts, own, own_inverse, slab, *refs):
+    n = len(counts) + 1
+    pieces, refs = group(refs, counts)
+    links, (lift, link, inverse) = refs[: n - 1], refs[n - 1 :]
     link[...] = own[...]
     inverse[...] = own_inverse[...]
     rows = slab.shape[0]
     size = lift.shape[0]
     for m in range(n):
-        spot = pl.ds(pl.multiple_of((lax.axis_index("pcol") ^ m) * rows, rows), rows)
+        spot = pl.multiple_of((lax.axis_index("pcol") ^ m) * rows, rows)
         if m:
-            links[m - 1][...] = pieces[m - 1][pl.ds(0, size)].astype(BF)
-            lift[spot] = pieces[m - 1][pl.ds(size, rows)].astype(BF)
+            put_rows(links[m - 1], 0, pieces[m - 1], 0, size)
+            put_rows(lift, spot, pieces[m - 1], size, size + rows)
         else:
-            lift[spot] = slab[...]
-
-
-def sort_kernel(n, *refs):
-    k = n - 1
+            lift[pl.ds(spot, rows)] = slab[...]
+
+
+def sort_kernel(counts, *refs):
     own, refs = refs[:3], refs[3:]
-    mine, other, inverses, lifts = refs[:k], refs[k : 2 * k], refs[2 * k : 3 * k], refs[3 * k : 4 * k]
-    for out, value in zip(refs[4 * k :], own):
+    k = len(counts)
+    mine, refs = group(refs, counts)
+    other, refs = group(refs, counts)
+    inverses, lifts = refs[:k], refs[k : 2 * k]
+    for out, value in zip(refs[2 * k :], own):
         out[...] = value[...]
-
-    @pl.when((lax.axis_index("prow") & 1) == 0)
-    def _():
-        for m in range(k):
-            inverses[m][...] = mine[m][...].astype(BF)
-            lifts[m][...] = other[m][...].astype(BF)
-
-    @pl.when((lax.axis_index("prow") & 1) == 1)
-    def _():
-        for m in range(k):
-            inverses[m][...] = other[m][...].astype(BF)
-            lifts[m][...] = mine[m][...].astype(BF)
+    for core, (first, second) in enumerate(((mine, other), (other, mine))):
+
+        @pl.when((lax.axis_index("prow") & 1) == core)
+        def _(first=first, second=second):
+            for m in range(k):
+                put_rows(inverses[m], 0, first[m], 0, inverses[m].shape[0])
+                put_rows(lifts[m], 0, second[m], 0, lifts[m].shape[0])
 
 
 def cost(flops, moved):
@@ -269,6 +286,47 @@
     order = sorted(range(1, size), key=lambda m: -bin(m).count("1"))
     got = {m: swap(arrays[m - 1], "pcol", m, size) for m in order}
     return [got[m] for m in range(1, size)]
+
+
+def gather(array, size):
+    got = {}
+    half = array.shape[0] // 2
+    for m in sorted(range(1, size), key=lambda m: bin(m).count("1")):
+        low, high = m & -m, 1 << (m.bit_length() - 1)
+        if low == high:
+            got[m] = (swap(array, "pcol", m, size),)
+            continue
+        near, far = got[m ^ low], got[m ^ high]
+        top = near[0][:half] if len(near) == 1 else near[0]
+        rest = far[0][half:] if len(far) == 1 else far[1]
+        got[m] = (swap(top, "pcol", low, size), swap(rest, "pcol", high, size))
+    return [got[m] for m in range(1, size)]
+
+
+def read_parts(parts):
+    def read(first, last):
+        out, start = [], 0
+        for part in parts:
+            end = start + part.shape[0]
+            if first < end and last > start:
+                out.append((max(first, start) - first, part, max(first, start) - start, min(last, end) - max(first, start)))
+            start = end
+        return out
+
+    return read
+
+
+def put_rows(out, base, parts, first, last):
+    for offset, part, start, count in read_parts(parts)(first, last):
+        out[pl.ds(base + offset, count)] = part[pl.ds(start, count)].astype(BF)
+
+
+def group(refs, counts):
+    out, i = [], 0
+    for count in counts:
+        out.append(refs[i : i + count])
+        i += count
+    return out, refs[i:]
 
 
 def inner(
@@ -318,7 +376,8 @@
     own_link, own_slab, place = lax.optimization_barrier((coupling[0, 0], summit_band[0], place))
     link_out = jnp.concatenate([own_link, own_slab], 0).astype(F32)
     strip_out = jnp.where(place[0, 0] == 0, strip_inverse[0], summit_strip[0]).astype(F32)
-    link_in = spread([link_out] * (n - 1), n)
+    link_in = gather(link_out, n)
+    counts = [len(parts) for parts in link_in]
 
     *sent, solved = pl.pallas_call(
         functools.partial(first_kernel, n),
@@ -331,26 +390,46 @@
         name="first_sweep",
     )(*lists, leaf_source[0, 0], band_source[0], strip_source[0], summit_source, *leaf_weights)
 
+    cut = leaves - leaves // 4
+
+    def invert(first, last, *stack):
+        return pl.pallas_call(
+            functools.partial(invert_kernel, first),
+            out_shape=[shape_of((leaves, leaves * size, size), BF)],
+            in_specs=[SMEM] * 2 + [VMEM] * (2 + len(stack)),
+            out_specs=[VMEM],
+            scratch_shapes=[
+                pltpu.VMEM((last - first, size, leaves * size), BF),
+                pltpu.VMEM((size, leaves * size), BF),
+                pltpu.SMEM((leaves + 1,), jnp.int32),
+            ],
+            input_output_aliases={4: 0} if stack else {},
+            cost_estimate=cost(5 * size**3 * pairs, weight_bytes),
+            compiler_params=small,
+        )(*lists, *leaf_weights[:2], *stack)[0]
+
+    stack = invert(0, cut)
+
     *links, lift, link, band_inverse = pl.pallas_call(
-        functools.partial(gather_kernel, n),
+        functools.partial(gather_kernel, counts),
         out_shape=[shape_of(block, BF)] * (n + 2),
-        in_specs=[VMEM] * (n + 2),
+        in_specs=[VMEM] * (3 + sum(counts)),
         out_specs=[VMEM] * (n + 2),
         cost_estimate=cost(0, 6 * n * size * size),
         compiler_params=small, name="gather_links",
-    )(coupling[0, 0], band_inverse[0], summit_band[0], *link_in)
+    )(coupling[0, 0], band_inverse[0], summit_band[0], *sum(link_in, ()))
     links = [link] + links
 
     for step in range(PASSES):
         last = step == PASSES - 1
         got = list(sent[:1]) + spread(sent[1:], n)
         if step == 0:
-            strip_in = spread([strip_out] * (n - 1), n)
+            strip_in = sum(gather(strip_out, n), ())
             strip_over = [swap(array, "prow", 1, n_prow) for array in strip_in]
             sorted_in = pl.pallas_call(
-                functools.partial(sort_kernel, n),
+                functools.partial(sort_kernel, counts),
                 out_shape=[shape_of(block, BF)] * (2 * n + 1),
-                in_specs=[VMEM] * (2 * n + 1),
+                in_specs=[VMEM] * (3 + 2 * sum(counts)),
                 out_specs=[VMEM] * (2 * n + 1),
                 cost_estimate=cost(0, 12 * n * size * size),
                 compiler_params=small, name="sort_strips",
@@ -368,10 +447,16 @@
             compiler_params=small, name="band_solve",
         )(band_inverse, lift, *got, *links)
         mine = keep + swap(send, "prow", 1, n_prow)
-        mask = 2
-        while mask < n_prow:
-            mine = mine + swap(mine, "prow", mask, n_prow)
-            mask *= 2
+        if step and n_prow // 2 <= FEW:
+            terms = [mine] + [swap(mine, "prow", mask, n_prow) for mask in range(2, n_prow, 2)]
+            while len(terms) > 1:
+                terms = [one + two for one, two in zip(terms[::2], terms[1::2])]
+            mine = terms[0]
+        else:
+            mask = 2
+            while mask < n_prow:
+                mine = mine + swap(mine, "prow", mask, n_prow)
+                mask *= 2
         other = swap(mine, "prow", 1, n_prow)
         back = pl.pallas_call(
             functools.partial(top_kernel, n),
@@ -383,6 +468,8 @@
             compiler_params=small, name="top_solve",
         )(band_inverse, lift, summit_inverse, band_solved, mine, other, *links, *inverses, *lifts)
         tops = list(back[:1]) + spread(back[1:], n)
+        if not last:
+            stack = invert(cut, leaves, stack)
         if last:
             shapes = [shape_of((leaves, size, vectors), BF)] + [shape_of((size, vectors), BF)] * 3
         else:
@@ -390,17 +477,14 @@
         results = pl.pallas_call(
             functools.partial(middle_kernel, n, last),
             out_shape=shapes,
-            in_specs=[SMEM] * 2 + [HBM] + [VMEM] * (n + 5),
+            in_specs=[VMEM] * (n + 5),
             out_specs=[VMEM] * len(shapes),
-            scratch_shapes=scratch
-            + [pltpu.VMEM((3, vectors, size), F32)]
-            + [pltpu.VMEM((leaves, vectors, size), BF)] * 2
-            + ends
-            + [pltpu.SemaphoreType.DMA],
+            scratch_shapes=[pltpu.VMEM((3, vectors, size), F32), pltpu.VMEM((vectors, leaves * size), BF)]
+            + ([] if last else [pltpu.VMEM((leaves, vectors, size), BF), pltpu.VMEM((3, vectors, size), F32)]),
             cost_estimate=cost(sweep_flops * (1 if last else 2), weight_bytes),
             compiler_params=small,
             name="last_sweep" if last else "middle_sweep",
-        )(*lists, solved, *tops, *leaf_weights)
+        )(solved, *tops, stack, *leaf_weights[2:])
         if not last:
             *sent, solved = results
     leaf_answer, band_answer, strip_answer, summit_answer = results

time: 104 us -> 92.9 us (0.89)
  waiting for transfers between devices: 49.6 us -> 31.4 us
  Pallas kernels: 18 us -> 21.9 us
  starting transfers between devices: 32.9 us -> 36.2 us
    ppermute x29 -> x33, waiting for transfers between devices: 49.6 us -> 31.4 us  [swap(): return lax.ppermute(array, axis, [(i, i ^ mask) for i in range(size)])]
    pallas_call x2 -> x4, Pallas kernels: 0.18 us -> 7.07 us  [the longest x2 6.7 us: invert(): pl.pallas_call(functools.partial(invert_kernel, first), out_shape=[shape_...]
    ppermute x29 -> x33, starting transfers between devices: 32.9 us -> 36.2 us  [swap(): return lax.ppermute(array, axis, [(i, i ^ mask) for i in range(size)])]
    pallas_call x2, Pallas kernels: 9.68 us -> 6.76 us  [inner(): pl.pallas_call(functools.partial(middle_kernel, n, last), out_shape=shape...]
  transfers between devices with their start and end apart: 29 -> 33, of which waited for: 18 -> 18; matrix products, arithmetic and copies ran while one was open for 1% -> 1% of each run, Pallas kernels for 4% -> 12%
where the time goes in v3:
time: 92.9 us; the launch traced here: 92.7 us
  starting transfers between devices  36.2 us (39%)
  waiting for transfers between devices  31.4 us (34%)
  Pallas kernels  21.9 us (24%)
  between operations  1.71 us (2%)
  local copies, waits for them, and re-layouts  1.36 us (1%)
    ppermute x33, starting transfers between devices, swap(): return lax.ppermute(array, axis, [(i, i ^ mask) for i in range(size)])  36.2 us
    ppermute x33, waiting for transfers between devices, swap(): return lax.ppermute(array, axis, [(i, i ^ mask) for i in range(size)])  31.4 us
    pallas_call x2, Pallas kernels, inner(): pl.pallas_call(functools.partial(middle_kernel, n, last), out_shape=shape...  6.76 us
    pallas_call x2, Pallas kernels, invert(): pl.pallas_call(functools.partial(invert_kernel, first), out_shape=[shape_...  6.7 us
    pallas_call x2, Pallas kernels, inner(): pl.pallas_call(functools.partial(top_kernel, n), out_shape=pieces, in_spe...  3.66 us
    pallas_call x1, Pallas kernels, inner(): pl.pallas_call(functools.partial(first_kernel, n), out_shape=pieces + [so...  3.57 us
  transfers between devices with their start and end apart: 33, of which 18 were waited for; matrix products, arithmetic and copies ran while one was open for 1% of the time, Pallas kernels for 12%

profile of v3, /device:TPU:0, one launch (start us, length us, event | category | flops | bytes accessed | tf_op | source)
XLA Modules:
  0.0 92.7 jit_solution(483829592374681761)
XLA Ops:
  0.8 0.6 copy-done.10
  1.6 3.1 %collective-permute-start.1 = (f32[320,256]{1,0:T(8,128)S(1)}, f32[320,256]{1,0:T(8,128)S(1)}, u32[]{:S(2)}, u32[]{:S(2)}) collective-permute-start(f32[320,256]{1,0:T(8,128)S(1)} %maximum_convert_fusion), channel_id=1, source_target_pairs={{0,2},{1,3},{2,0},{3,1},{4,6},{5,7},{6,4},{7,5},{8,10},{9,11},{10,... | collective-permute-start | bytes 983048 | tf_op jit(solution)/shard_map/ppermute | solution.py:282
  4.6 1.5 %collective-permute-start = (f32[320,256]{1,0:T(8,128)S(1)}, f32[320,256]{1,0:T(8,128)S(1)}, u32[]{:S(2)}, u32[]{:S(2)}) collective-permute-start(f32[320,256]{1,0:T(8,128)S(1)} %maximum_convert_fusion), channel_id=1, source_target_pairs={{0,1},{1,0},{2,3},{3,2},{4,5},{5,4},{6,7},{7,6},{8,9},{9,8},{10,11... | collective-permute-start | bytes 983048 | tf_op jit(solution)/shard_map/ppermute | solution.py:282
  7.3 5.1 %collective-permute-done.1.refs_1_ = f32[320,256]{1,0:T(8,128)S(1)} collective-permute-done((f32[320,256]{1,0:T(8,128)S(1)}, f32[320,256]{1,0:T(8,128)S(1)}, u32[]{:S(2)}, u32[]{:S(2)}) %collective-permute-start.1) | collective-permute-done | bytes 327712 | tf_op jit(solution)/shard_map/ppermute | solution.py:282
  12.4 1.8 %collective-permute-start.2 = (f32[160,256]{1,0:T(8,128)S(1)}, f32[160,256]{1,0:T(8,128)S(1)}, u32[]{:S(2)}, u32[]{:S(2)}) collective-permute-start(f32[160,256]{1,0:T(8,128)S(1)} %slice.20), channel_id=1, source_target_pairs={{0,1},{1,0},{2,3},{3,2},{4,5},{5,4},{6,7},{7,6},{8,9},{9,8},{10,11... | collective-permute-start | bytes 491528 | tf_op jit(solution)/shard_map/ppermute | solution.py:282
  14.2 1.6 %collective-permute-start.3 = (f32[160,256]{1,0:T(8,128)S(1)}, f32[160,256]{1,0:T(8,128)S(1)}, u32[]{:S(2)}, u32[]{:S(2)}) collective-permute-start(f32[160,256]{1,0:T(8,128)S(1)} %slice.21), channel_id=1, source_target_pairs={{0,2},{1,3},{2,0},{3,1},{4,6},{5,7},{6,4},{7,5},{8,10},{9,11},{10,... | collective-permute-start | bytes 491528 | tf_op jit(solution)/shard_map/ppermute | solution.py:282
  16.4 1.2 %collective-permute-start.4 = (f32[256,256]{1,0:T(8,128)S(1)}, f32[256,256]{1,0:T(8,128)S(1)}, u32[]{:S(2)}, u32[]{:S(2)}) collective-permute-start(f32[256,256]{1,0:T(8,128)S(1)} %select_convert_fusion), channel_id=1, source_target_pairs={{0,1},{1,0},{2,3},{3,2},{4,5},{5,4},{6,7},{7,6},{8,9},{9,8},{10,11... | collective-permute-start | bytes 786440 | tf_op jit(solution)/shard_map/ppermute | solution.py:282
  17.6 3.6 %first_sweep.1 = (f32[96,256]{1,0:T(8,128)S(1)}, f32[96,256]{1,0:T(8,128)S(1)}, f32[96,256]{1,0:T(8,128)S(1)}, f32[96,256]{1,0:T(8,128)S(1)}, bf16[8,128,256]{2,1,0:T(8,128)(2,1)S(1)}) custom-call(s32[8]{0:T(128)S(1)} %bitcast.46, s32[8]{0:T(128)S(1)} %bitcast.49, bf16[8,256,128]{2,1,0:T(8,128)(2,1)S(1)} %bitcast.36, bf16[256,128]{1,0:T(8,128)(2,1)S(1)} %bitcast.44, ...), custom_call_target="tpu_custom_call" | custom-call | flops 1006632960 | bytes 7864320 | tf_op jit(solution)/shard_map/first_sweep/pallas_call | solution.py:382
  21.2 0.9 collective-permute-start.12
  22.1 1.5 %collective-permute-start.13 = (f32[96,256]{1,0:T(8,128)S(1)}, f32[96,256]{1,0:T(8,128)S(1)}, u32[]{:S(2)}, u32[]{:S(2)}) collective-permute-start(f32[96,256]{1,0:T(8,128)S(1)} %get-tuple-element.59), channel_id=1, source_target_pairs={{0,2},{1,3},{2,0},{3,1},{4,6},{5,7},{6,4},{7,5},{8,10},{9,11},{10,... | collective-permute-start | bytes 294920 | tf_op jit(solution)/shard_map/ppermute | solution.py:282
  23.6 1.1 %collective-permute-start.14 = (f32[96,256]{1,0:T(8,128)S(1)}, f32[96,256]{1,0:T(8,128)S(1)}, u32[]{:S(2)}, u32[]{:S(2)}) collective-permute-start(f32[96,256]{1,0:T(8,128)S(1)} %get-tuple-element.60), channel_id=1, source_target_pairs={{0,3},{1,2},{2,1},{3,0},{4,7},{5,6},{6,5},{7,4},{8,11},{9,10},{10,... | collective-permute-start | bytes 294920 | tf_op jit(solution)/shard_map/ppermute | solution.py:282
  24.8 1.8 %collective-permute-done.12.refs_1_ = f32[96,256]{1,0:T(8,128)S(1)} collective-permute-done((f32[96,256]{1,0:T(8,128)S(1)}, f32[96,256]{1,0:T(8,128)S(1)}, u32[]{:S(2)}, u32[]{:S(2)}) %collective-permute-start.12) | collective-permute-done | bytes 98336 | tf_op jit(solution)/shard_map/ppermute | solution.py:282
  26.6 1.3 %collective-permute-done.13.refs_2_ = f32[96,256]{1,0:T(8,128)S(1)} collective-permute-done((f32[96,256]{1,0:T(8,128)S(1)}, f32[96,256]{1,0:T(8,128)S(1)}, u32[]{:S(2)}, u32[]{:S(2)}) %collective-permute-start.13) | collective-permute-done | bytes 98336 | tf_op jit(solution)/shard_map/ppermute | solution.py:282
  27.9 1.2 %collective-permute-done.14.refs_3_ = f32[96,256]{1,0:T(8,128)S(1)} collective-permute-done((f32[96,256]{1,0:T(8,128)S(1)}, f32[96,256]{1,0:T(8,128)S(1)}, u32[]{:S(2)}, u32[]{:S(2)}) %collective-permute-start.14) | collective-permute-done | bytes 98336 | tf_op jit(solution)/shard_map/ppermute | solution.py:282
  29.7 1.3 %collective-permute-done.15 = f32[80,256]{1,0:T(8,128)S(1)} collective-permute-done((f32[80,256]{1,0:T(8,128)S(1)}, f32[80,256]{1,0:T(8,128)S(1)}, u32[]{:S(2)}, u32[]{:S(2)}) %collective-permute-start.15) | collective-permute-done | bytes 81952 | tf_op jit(solution)/shard_map/ppermute | solution.py:282
  30.9 1.6 %collective-permute-start.16 = (f32[80,256]{1,0:T(8,128)S(1)}, f32[80,256]{1,0:T(8,128)S(1)}, u32[]{:S(2)}, u32[]{:S(2)}) collective-permute-start(f32[80,256]{1,0:T(8,128)S(1)} %add.21), channel_id=1, source_target_pairs={{0,8},{4,12},{8,0},{12,4},{16,24},{20,28},{24,16},{28,20},{1,9},{5... | collective-permute-start | bytes 245768 | tf_op jit(solution)/shard_map/ppermute | solution.py:282
  32.6 1.1 %collective-permute-start.6 = (f32[128,256]{1,0:T(8,128)S(1)}, f32[128,256]{1,0:T(8,128)S(1)}, u32[]{:S(2)}, u32[]{:S(2)}) collective-permute-start(f32[128,256]{1,0:T(8,128)S(1)} %slice.22), channel_id=1, source_target_pairs={{0,1},{1,0},{2,3},{3,2},{4,5},{5,4},{6,7},{7,6},{8,9},{9,8},{10,11... | collective-permute-start | bytes 393224 | tf_op jit(solution)/shard_map/ppermute | solution.py:282
  33.7 0.8 collective-permute-start.7
  34.5 1.0 %collective-permute-done.16 = f32[80,256]{1,0:T(8,128)S(1)} collective-permute-done((f32[80,256]{1,0:T(8,128)S(1)}, f32[80,256]{1,0:T(8,128)S(1)}, u32[]{:S(2)}, u32[]{:S(2)}) %collective-permute-start.16) | collective-permute-done | bytes 81952 | tf_op jit(solution)/shard_map/ppermute | solution.py:282
  35.5 2.6 %collective-permute-start.17 = (f32[80,256]{1,0:T(8,128)S(1)}, f32[80,256]{1,0:T(8,128)S(1)}, u32[]{:S(2)}, u32[]{:S(2)}) collective-permute-start(f32[80,256]{1,0:T(8,128)S(1)} %add.22), channel_id=1, source_target_pairs={{0,16},{4,20},{8,24},{12,28},{16,0},{20,4},{24,8},{28,12},{1,17},{... | collective-permute-start | bytes 245768 | tf_op jit(solution)/shard_map/ppermute | solution.py:282
  39.2 1.9 %collective-permute-done.17 = f32[80,256]{1,0:T(8,128)S(1)} collective-permute-done((f32[80,256]{1,0:T(8,128)S(1)}, f32[80,256]{1,0:T(8,128)S(1)}, u32[]{:S(2)}, u32[]{:S(2)}) %collective-permute-start.17) | collective-permute-done | bytes 81952 | tf_op jit(solution)/shard_map/ppermute | solution.py:282
  41.2 3.4 %shard_map.192.refs_0_ = bf16[8,2048,256]{2,1,0:T(8,128)(2,1)S(1)} custom-call(s32[8]{0:T(128)S(1)} %bitcast.47, s32[8]{0:T(128)S(1)} %bitcast.50, bf16[8,256,256]{2,1,0:T(8,128)(2,1)S(1)} %bitcast.34, bf16[28,256,256]{2,1,0:T(8,128)(2,1)S(1)} %bitcast.22), custom_call_target="tpu_custom_call" | custom-call | flops 2348810240 | bytes 7864320 | tf_op jit(solution)/shard_map/pallas_call | solution.py:396
  45.0 1.8 %top_solve.2 = (f32[96,256]{1,0:T(8,128)S(1)}, f32[96,256]{1,0:T(8,128)S(1)}, f32[96,256]{1,0:T(8,128)S(1)}, f32[96,256]{1,0:T(8,128)S(1)}) custom-call(bf16[256,256]{1,0:T(8,128)(2,1)S(1)} %get-tuple-element.53.inverse, bf16[256,256]{1,0:T(8,128)(2,1)S(1)} %get-tuple-element.54.lift, bf16[256,256]{1,0:T(8,128)(2,1)S(1)} %get-tuple-element.56.summit_inverse, ...), custom_call_target="tpu_custom_call" | custom-call | flops 100663296 | bytes 1966080 | tf_op jit(solution)/shard_map/top_solve/pallas_call | solution.py:461
  46.9 1.1 %collective-permute-start.19 = (f32[96,256]{1,0:T(8,128)S(1)}, f32[96,256]{1,0:T(8,128)S(1)}, u32[]{:S(2)}, u32[]{:S(2)}) collective-permute-start(f32[96,256]{1,0:T(8,128)S(1)} %get-tuple-element.77), channel_id=1, source_target_pairs={{0,1},{1,0},{2,3},{3,2},{4,5},{5,4},{6,7},{7,6},{8,9},{9,8},{10,11... | collective-permute-start | bytes 294920 | tf_op jit(solution)/shard_map/ppermute | solution.py:282
  48.0 0.8 collective-permute-start.20
  48.7 1.7 %collective-permute-start.21 = (f32[96,256]{1,0:T(8,128)S(1)}, f32[96,256]{1,0:T(8,128)S(1)}, u32[]{:S(2)}, u32[]{:S(2)}) collective-permute-start(f32[96,256]{1,0:T(8,128)S(1)} %get-tuple-element.79), channel_id=1, source_target_pairs={{0,3},{1,2},{2,1},{3,0},{4,7},{5,6},{6,5},{7,4},{8,11},{9,10},{10,... | collective-permute-start | bytes 294920 | tf_op jit(solution)/shard_map/ppermute | solution.py:282
  50.4 3.3 %shard_map.193.refs_4_ = bf16[8,2048,256]{2,1,0:T(8,128)(2,1)S(1)} custom-call(s32[8]{0:T(128)S(1)} %bitcast.48, s32[8]{0:T(128)S(1)} %bitcast.51, bf16[8,256,256]{2,1,0:T(8,128)(2,1)S(1)} %bitcast.35, bf16[28,256,256]{2,1,0:T(8,128)(2,1)S(1)} %bitcast.23, bf16[8,2048,256]{2,1,0:T(8,128)(2,1)S(1)} %shard_map.192.refs_0_), custom_call_target="tpu_custom_call", output_to_operand_aliasing={{}: (4, {})} | custom-call | flops 2348810240 | bytes 7864320 | tf_op jit(solution)/shard_map/pallas_call | solution.py:396
  53.7 1.3 %collective-permute-done.21.refs_3_ = f32[96,256]{1,0:T(8,128)S(1)} collective-permute-done((f32[96,256]{1,0:T(8,128)S(1)}, f32[96,256]{1,0:T(8,128)S(1)}, u32[]{:S(2)}, u32[]{:S(2)}) %collective-permute-start.21) | collective-permute-done | bytes 98336 | tf_op jit(solution)/shard_map/ppermute | solution.py:282
  55.0 4.4 %middle_sweep.1 = (f32[96,256]{1,0:T(8,128)S(1)}, f32[96,256]{1,0:T(8,128)S(1)}, f32[96,256]{1,0:T(8,128)S(1)}, f32[96,256]{1,0:T(8,128)S(1)}, bf16[8,128,256]{2,1,0:T(8,128)(2,1)S(1)}) custom-call(bf16[8,128,256]{2,1,0:T(8,128)(2,1)S(1)} %get-tuple-element.50.solved_before, f32[96,256]{1,0:T(8,128)S(1)} %get-tuple-element.76.refs_0_, ...), custom_call_target="tpu_custom_call" | custom-call | flops 2013265920 | bytes 7864320 | tf_op jit(solution)/shard_map/middle_sweep/pallas_call | solution.py:477
  59.4 1.1 %collective-permute-start.22 = (f32[96,256]{1,0:T(8,128)S(1)}, f32[96,256]{1,0:T(8,128)S(1)}, u32[]{:S(2)}, u32[]{:S(2)}) collective-permute-start(f32[96,256]{1,0:T(8,128)S(1)} %get-tuple-element.82), channel_id=1, source_target_pairs={{0,1},{1,0},{2,3},{3,2},{4,5},{5,4},{6,7},{7,6},{8,9},{9,8},{10,11... | collective-permute-start | bytes 294920 | tf_op jit(solution)/shard_map/ppermute | solution.py:282
  60.4 1.3 %collective-permute-start.23 = (f32[96,256]{1,0:T(8,128)S(1)}, f32[96,256]{1,0:T(8,128)S(1)}, u32[]{:S(2)}, u32[]{:S(2)}) collective-permute-start(f32[96,256]{1,0:T(8,128)S(1)} %get-tuple-element.83), channel_id=1, source_target_pairs={{0,2},{1,3},{2,0},{3,1},{4,6},{5,7},{6,4},{7,5},{8,10},{9,11},{10,... | collective-permute-start | bytes 294920 | tf_op jit(solution)/shard_map/ppermute | solution.py:282
  61.7 1.2 %collective-permute-start.24 = (f32[96,256]{1,0:T(8,128)S(1)}, f32[96,256]{1,0:T(8,128)S(1)}, u32[]{:S(2)}, u32[]{:S(2)}) collective-permute-start(f32[96,256]{1,0:T(8,128)S(1)} %get-tuple-element.84), channel_id=1, source_target_pairs={{0,3},{1,2},{2,1},{3,0},{4,7},{5,6},{6,5},{7,4},{8,11},{9,10},{10,... | collective-permute-start | bytes 294920 | tf_op jit(solution)/shard_map/ppermute | solution.py:282
  62.9 2.0 %collective-permute-done.22.refs_1_ = f32[96,256]{1,0:T(8,128)S(1)} collective-permute-done((f32[96,256]{1,0:T(8,128)S(1)}, f32[96,256]{1,0:T(8,128)S(1)}, u32[]{:S(2)}, u32[]{:S(2)}) %collective-permute-start.22) | collective-permute-done | bytes 98336 | tf_op jit(solution)/shard_map/ppermute | solution.py:282
  65.0 0.8 collective-permute-done.23.refs_2_
  65.8 1.4 %collective-permute-done.24.refs_3_ = f32[96,256]{1,0:T(8,128)S(1)} collective-permute-done((f32[96,256]{1,0:T(8,128)S(1)}, f32[96,256]{1,0:T(8,128)S(1)}, u32[]{:S(2)}, u32[]{:S(2)}) %collective-permute-start.24) | collective-permute-done | bytes 98336 | tf_op jit(solution)/shard_map/ppermute | solution.py:282
  67.7 1.3 %collective-permute-done.25 = f32[80,256]{1,0:T(8,128)S(1)} collective-permute-done((f32[80,256]{1,0:T(8,128)S(1)}, f32[80,256]{1,0:T(8,128)S(1)}, u32[]{:S(2)}, u32[]{:S(2)}) %collective-permute-start.25) | collective-permute-done | bytes 81952 | tf_op jit(solution)/shard_map/ppermute | solution.py:282
  69.0 4.3 %collective-permute-start.28 = (f32[80,256]{1,0:T(8,128)S(1)}, f32[80,256]{1,0:T(8,128)S(1)}, u32[]{:S(2)}, u32[]{:S(2)}) collective-permute-start(f32[80,256]{1,0:T(8,128)S(1)} %add.24), channel_id=1, source_target_pairs={{0,24},{4,28},{8,16},{12,20},{16,8},{20,12},{24,0},{28,4},{1,25},{... | collective-permute-start | bytes 245768 | tf_op jit(solution)/shard_map/ppermute | solution.py:282
  73.3 0.6 collective-permute-start.26
  73.9 2.8 %collective-permute-done.28 = f32[80,256]{1,0:T(8,128)S(1)} collective-permute-done((f32[80,256]{1,0:T(8,128)S(1)}, f32[80,256]{1,0:T(8,128)S(1)}, u32[]{:S(2)}, u32[]{:S(2)}) %collective-permute-start.28) | collective-permute-done | bytes 81952 | tf_op jit(solution)/shard_map/ppermute | solution.py:282
  76.7 3.0 %collective-permute-done.27 = f32[80,256]{1,0:T(8,128)S(1)} collective-permute-done((f32[80,256]{1,0:T(8,128)S(1)}, f32[80,256]{1,0:T(8,128)S(1)}, u32[]{:S(2)}, u32[]{:S(2)}) %collective-permute-start.27) | collective-permute-done | bytes 81952 | tf_op jit(solution)/shard_map/ppermute | solution.py:282
  79.8 1.2 %collective-permute-done.29.other = f32[80,256]{1,0:T(8,128)S(1)} collective-permute-done((f32[80,256]{1,0:T(8,128)S(1)}, f32[80,256]{1,0:T(8,128)S(1)}, u32[]{:S(2)}, u32[]{:S(2)}) %collective-permute-start.29) | collective-permute-done | bytes 81952 | tf_op jit(solution)/shard_map/ppermute | solution.py:282
  81.1 1.8 %top_solve.3 = (f32[96,256]{1,0:T(8,128)S(1)}, f32[96,256]{1,0:T(8,128)S(1)}, f32[96,256]{1,0:T(8,128)S(1)}, f32[96,256]{1,0:T(8,128)S(1)}) custom-call(bf16[256,256]{1,0:T(8,128)(2,1)S(1)} %get-tuple-element.53.inverse, bf16[256,256]{1,0:T(8,128)(2,1)S(1)} %get-tuple-element.54.lift, bf16[256,256]{1,0:T(8,128)(2,1)S(1)} %get-tuple-element.56.summit_inverse, ...), custom_call_target="tpu_custom_call" | custom-call | flops 100663296 | bytes 1966080 | tf_op jit(solution)/shard_map/top_solve/pallas_call | solution.py:461
  82.9 0.6 collective-permute-start.30
  83.5 1.3 %collective-permute-start.31 = (f32[96,256]{1,0:T(8,128)S(1)}, f32[96,256]{1,0:T(8,128)S(1)}, u32[]{:S(2)}, u32[]{:S(2)}) collective-permute-start(f32[96,256]{1,0:T(8,128)S(1)} %get-tuple-element.90), channel_id=1, source_target_pairs={{0,2},{1,3},{2,0},{3,1},{4,6},{5,7},{6,4},{7,5},{8,10},{9,11},{10,... | collective-permute-start | bytes 294920 | tf_op jit(solution)/shard_map/ppermute | solution.py:282
  84.8 1.7 %collective-permute-start.32 = (f32[96,256]{1,0:T(8,128)S(1)}, f32[96,256]{1,0:T(8,128)S(1)}, u32[]{:S(2)}, u32[]{:S(2)}) collective-permute-start(f32[96,256]{1,0:T(8,128)S(1)} %get-tuple-element.91), channel_id=1, source_target_pairs={{0,3},{1,2},{2,1},{3,0},{4,7},{5,6},{6,5},{7,4},{8,11},{9,10},{10,... | collective-permute-start | bytes 294920 | tf_op jit(solution)/shard_map/ppermute | solution.py:282
  86.5 2.0 %collective-permute-done.30.refs_1_ = f32[96,256]{1,0:T(8,128)S(1)} collective-permute-done((f32[96,256]{1,0:T(8,128)S(1)}, f32[96,256]{1,0:T(8,128)S(1)}, u32[]{:S(2)}, u32[]{:S(2)}) %collective-permute-start.30) | collective-permute-done | bytes 98336 | tf_op jit(solution)/shard_map/ppermute | solution.py:282
  88.5 1.8 %collective-permute-done.32.refs_3_ = f32[96,256]{1,0:T(8,128)S(1)} collective-permute-done((f32[96,256]{1,0:T(8,128)S(1)}, f32[96,256]{1,0:T(8,128)S(1)}, u32[]{:S(2)}, u32[]{:S(2)}) %collective-permute-start.32) | collective-permute-done | bytes 98336 | tf_op jit(solution)/shard_map/ppermute | solution.py:282
  90.3 2.4 %last_sweep.1 = (bf16[8,256,128]{2,1,0:T(8,128)(2,1)}, bf16[256,128]{1,0:T(8,128)(2,1)}, bf16[256,128]{1,0:T(8,128)(2,1)}, bf16[256,128]{1,0:T(8,128)(2,1)}) custom-call(bf16[8,128,256]{2,1,0:T(8,128)(2,1)S(1)} %get-tuple-element.80.solved_before, f32[96,256]{1,0:T(8,128)S(1)} %get-tuple-element.88.refs_0_, f32[96,256]{1,0:T(8,128)S(1)} %collective-permute-done.30.refs_1_, ...), custom_call_target="tpu_custom_call" | custom-call | flops 1006632960 | bytes 7864320 | tf_op jit(solution)/shard_map/last_sweep/pallas_call | solution.py:477
  (76 shorter events, 4.1 us)
Async XLA Ops:
  0.7 15.1 %copy-start.8 = (bf16[1,256,256]{2,1,0:T(8,128)(2,1)S(1)}, bf16[1,256,256]{2,1,0:T(8,128)(2,1)}, u32[]{:S(2)}) copy-start(bf16[1,256,256]{2,1,0:T(8,128)(2,1)} %param.31) | copy-start | bytes 393220
  0.7 15.1 %copy-start.7 = (bf16[1,256,256]{2,1,0:T(8,128)(2,1)S(1)}, bf16[1,256,256]{2,1,0:T(8,128)(2,1)}, u32[]{:S(2)}) copy-start(bf16[1,256,256]{2,1,0:T(8,128)(2,1)} %param.23) | copy-start | bytes 393220
  0.7 16.8 %copy-start.16 = (s32[1,1,8]{2,1,0:T(1,128)S(1)}, s32[1,1,8]{2,1,0:T(1,128)}, u32[]{:S(2)}) copy-start(s32[1,1,8]{2,1,0:T(1,128)} %param.33) | copy-start | bytes 100
  0.7 16.8 %copy-start.15 = (s32[1,1,8]{2,1,0:T(1,128)S(1)}, s32[1,1,8]{2,1,0:T(1,128)}, u32[]{:S(2)}) copy-start(s32[1,1,8]{2,1,0:T(1,128)} %param.32) | copy-start | bytes 100
  0.7 16.8 %copy-start.3 = (bf16[1,1,8,256,256]{4,3,2,1,0:T(8,128)(2,1)S(1)}, bf16[1,1,8,256,256]{4,3,2,1,0:T(8,128)(2,1)}, u32[]{:S(2)}) copy-start(bf16[1,1,8,256,256]{4,3,2,1,0:T(8,128)(2,1)} %param.28) | copy-start | bytes 3145732
  0.7 16.8 %copy-start.2 = (bf16[1,1,8,256,256]{4,3,2,1,0:T(8,128)(2,1)S(1)}, bf16[1,1,8,256,256]{4,3,2,1,0:T(8,128)(2,1)}, u32[]{:S(2)}) copy-start(bf16[1,1,8,256,256]{4,3,2,1,0:T(8,128)(2,1)} %param.27) | copy-start | bytes 3145732
  0.7 16.8 %copy-start.1 = (bf16[1,1,8,256,256]{4,3,2,1,0:T(8,128)(2,1)S(1)}, bf16[1,1,8,256,256]{4,3,2,1,0:T(8,128)(2,1)}, u32[]{:S(2)}) copy-start(bf16[1,1,8,256,256]{4,3,2,1,0:T(8,128)(2,1)} %param.26) | copy-start | bytes 3145732
  0.7 16.8 %copy-start = (bf16[1,1,28,256,256]{4,3,2,1,0:T(8,128)(2,1)S(1)}, bf16[1,1,28,256,256]{4,3,2,1,0:T(8,128)(2,1)}, u32[]{:S(2)}) copy-start(bf16[1,1,28,256,256]{4,3,2,1,0:T(8,128)(2,1)} %param.25) | copy-start | bytes 11010052
  0.7 16.8 %copy-start.4 = (bf16[1,1,8,256,256]{4,3,2,1,0:T(8,128)(2,1)S(1)}, bf16[1,1,8,256,256]{4,3,2,1,0:T(8,128)(2,1)}, u32[]{:S(2)}) copy-start(bf16[1,1,8,256,256]{4,3,2,1,0:T(8,128)(2,1)} %param.21) | copy-start | bytes 3145732
  0.7 16.8 %copy-start.14 = (bf16[256,128]{1,0:T(8,128)(2,1)S(1)}, bf16[256,128]{1,0:T(8,128)(2,1)}, u32[]{:S(2)}) copy-start(bf16[256,128]{1,0:T(8,128)(2,1)} %summit_source.1) | copy-start | bytes 196612
  0.8 16.8 %copy-start.13 = (bf16[1,256,128]{2,1,0:T(8,128)(2,1)S(1)}, bf16[1,256,128]{2,1,0:T(8,128)(2,1)}, u32[]{:S(2)}) copy-start(bf16[1,256,128]{2,1,0:T(8,128)(2,1)} %param.19) | copy-start | bytes 196612
  0.8 16.8 %copy-start.12 = (bf16[1,256,128]{2,1,0:T(8,128)(2,1)S(1)}, bf16[1,256,128]{2,1,0:T(8,128)(2,1)}, u32[]{:S(2)}) copy-start(bf16[1,256,128]{2,1,0:T(8,128)(2,1)} %param.18) | copy-start | bytes 196612
  0.8 16.8 %copy-start.5 = (bf16[1,1,8,256,128]{4,3,2,1,0:T(8,128)(2,1)S(1)}, bf16[1,1,8,256,128]{4,3,2,1,0:T(8,128)(2,1)}, u32[]{:S(2)}) copy-start(bf16[1,1,8,256,128]{4,3,2,1,0:T(8,128)(2,1)} %param.17) | copy-start | bytes 1572868
  0.8 23.9 %copy-start.9 = (bf16[1,256,256]{2,1,0:T(8,128)(2,1)S(1)}, bf16[1,256,256]{2,1,0:T(8,128)(2,1)}, u32[]{:S(2)}) copy-start(bf16[1,256,256]{2,1,0:T(8,128)(2,1)} %param.22) | copy-start | bytes 393220
  1.6 10.8 %collective-permute-start.1 = (f32[320,256]{1,0:T(8,128)S(1)}, f32[320,256]{1,0:T(8,128)S(1)}, u32[]{:S(2)}, u32[]{:S(2)}) collective-permute-start(f32[320,256]{1,0:T(8,128)S(1)} %maximum_convert_fusion), channel_id=1, source_target_pairs={{0,2},{1,3},{2,0},{3,1},{4,6},{5,7},{6,4},{7,5},{8,10},{9,11},{10,... | collective-permute-start | bytes 983048 | tf_op jit(solution)/shard_map/ppermute | solution.py:282
  4.6 9.5 %collective-permute-start = (f32[320,256]{1,0:T(8,128)S(1)}, f32[320,256]{1,0:T(8,128)S(1)}, u32[]{:S(2)}, u32[]{:S(2)}) collective-permute-start(f32[320,256]{1,0:T(8,128)S(1)} %maximum_convert_fusion), channel_id=1, source_target_pairs={{0,1},{1,0},{2,3},{3,2},{4,5},{5,4},{6,7},{7,6},{8,9},{9,8},{10,11... | collective-permute-start | bytes 983048 | tf_op jit(solution)/shard_map/ppermute | solution.py:282
  12.4 9.7 %collective-permute-start.2 = (f32[160,256]{1,0:T(8,128)S(1)}, f32[160,256]{1,0:T(8,128)S(1)}, u32[]{:S(2)}, u32[]{:S(2)}) collective-permute-start(f32[160,256]{1,0:T(8,128)S(1)} %slice.20), channel_id=1, source_target_pairs={{0,1},{1,0},{2,3},{3,2},{4,5},{5,4},{6,7},{7,6},{8,9},{9,8},{10,11... | collective-permute-start | bytes 491528 | tf_op jit(solution)/shard_map/ppermute | solution.py:282
  14.2 9.5 %collective-permute-start.3 = (f32[160,256]{1,0:T(8,128)S(1)}, f32[160,256]{1,0:T(8,128)S(1)}, u32[]{:S(2)}, u32[]{:S(2)}) collective-permute-start(f32[160,256]{1,0:T(8,128)S(1)} %slice.21), channel_id=1, source_target_pairs={{0,2},{1,3},{2,0},{3,1},{4,6},{5,7},{6,4},{7,5},{8,10},{9,11},{10,... | collective-permute-start | bytes 491528 | tf_op jit(solution)/shard_map/ppermute | solution.py:282
  15.8 16.8 %collective-permute-start.5 = (f32[256,256]{1,0:T(8,128)S(1)}, f32[256,256]{1,0:T(8,128)S(1)}, u32[]{:S(2)}, u32[]{:S(2)}) collective-permute-start(f32[256,256]{1,0:T(8,128)S(1)} %select_convert_fusion), channel_id=1, source_target_pairs={{0,2},{1,3},{2,0},{3,1},{4,6},{5,7},{6,4},{7,5},{8,10},{9,11},{10,... | collective-permute-start | bytes 786440 | tf_op jit(solution)/shard_map/ppermute | solution.py:282
  16.4 17.3 %collective-permute-start.4 = (f32[256,256]{1,0:T(8,128)S(1)}, f32[256,256]{1,0:T(8,128)S(1)}, u32[]{:S(2)}, u32[]{:S(2)}) collective-permute-start(f32[256,256]{1,0:T(8,128)S(1)} %select_convert_fusion), channel_id=1, source_target_pairs={{0,1},{1,0},{2,3},{3,2},{4,5},{5,4},{6,7},{7,6},{8,9},{9,8},{10,11... | collective-permute-start | bytes 786440 | tf_op jit(solution)/shard_map/ppermute | solution.py:282
  21.2 5.4 %collective-permute-start.12 = (f32[96,256]{1,0:T(8,128)S(1)}, f32[96,256]{1,0:T(8,128)S(1)}, u32[]{:S(2)}, u32[]{:S(2)}) collective-permute-start(f32[96,256]{1,0:T(8,128)S(1)} %get-tuple-element.58), channel_id=1, source_target_pairs={{0,1},{1,0},{2,3},{3,2},{4,5},{5,4},{6,7},{7,6},{8,9},{9,8},{10,11... | collective-permute-start | bytes 294920 | tf_op jit(solution)/shard_map/ppermute | solution.py:282
  22.1 5.8 %collective-permute-start.13 = (f32[96,256]{1,0:T(8,128)S(1)}, f32[96,256]{1,0:T(8,128)S(1)}, u32[]{:S(2)}, u32[]{:S(2)}) collective-permute-start(f32[96,256]{1,0:T(8,128)S(1)} %get-tuple-element.59), channel_id=1, source_target_pairs={{0,2},{1,3},{2,0},{3,1},{4,6},{5,7},{6,4},{7,5},{8,10},{9,11},{10,... | collective-permute-start | bytes 294920 | tf_op jit(solution)/shard_map/ppermute | solution.py:282
  23.6 5.5 %collective-permute-start.14 = (f32[96,256]{1,0:T(8,128)S(1)}, f32[96,256]{1,0:T(8,128)S(1)}, u32[]{:S(2)}, u32[]{:S(2)}) collective-permute-start(f32[96,256]{1,0:T(8,128)S(1)} %get-tuple-element.60), channel_id=1, source_target_pairs={{0,3},{1,2},{2,1},{3,0},{4,7},{5,6},{6,5},{7,4},{8,11},{9,10},{10,... | collective-permute-start | bytes 294920 | tf_op jit(solution)/shard_map/ppermute | solution.py:282
  24.7 20.0 %copy-start.11 = (bf16[256,256]{1,0:T(8,128)(2,1)S(1)}, bf16[256,256]{1,0:T(8,128)(2,1)}, u32[]{:S(2)}) copy-start(bf16[256,256]{1,0:T(8,128)(2,1)} %refs_2_.1) | copy-start | bytes 393220
  29.6 1.3 %collective-permute-start.15 = (f32[80,256]{1,0:T(8,128)S(1)}, f32[80,256]{1,0:T(8,128)S(1)}, u32[]{:S(2)}, u32[]{:S(2)}) collective-permute-start(f32[80,256]{1,0:T(8,128)S(1)} %get-tuple-element.67), channel_id=1, source_target_pairs={{0,4},{4,0},{8,12},{12,8},{16,20},{20,16},{24,28},{28,24},{1,5},{5... | collective-permute-start | bytes 245768 | tf_op jit(solution)/shard_map/ppermute | solution.py:282
  30.9 4.6 %collective-permute-start.16 = (f32[80,256]{1,0:T(8,128)S(1)}, f32[80,256]{1,0:T(8,128)S(1)}, u32[]{:S(2)}, u32[]{:S(2)}) collective-permute-start(f32[80,256]{1,0:T(8,128)S(1)} %add.21), channel_id=1, source_target_pairs={{0,8},{4,12},{8,0},{12,4},{16,24},{20,28},{24,16},{28,20},{1,9},{5... | collective-permute-start | bytes 245768 | tf_op jit(solution)/shard_map/ppermute | solution.py:282
  32.6 6.1 %collective-permute-start.6 = (f32[128,256]{1,0:T(8,128)S(1)}, f32[128,256]{1,0:T(8,128)S(1)}, u32[]{:S(2)}, u32[]{:S(2)}) collective-permute-start(f32[128,256]{1,0:T(8,128)S(1)} %slice.22), channel_id=1, source_target_pairs={{0,1},{1,0},{2,3},{3,2},{4,5},{5,4},{6,7},{7,6},{8,9},{9,8},{10,11... | collective-permute-start | bytes 393224 | tf_op jit(solution)/shard_map/ppermute | solution.py:282
  33.7 5.1 %collective-permute-start.7 = (f32[128,256]{1,0:T(8,128)S(1)}, f32[128,256]{1,0:T(8,128)S(1)}, u32[]{:S(2)}, u32[]{:S(2)}) collective-permute-start(f32[128,256]{1,0:T(8,128)S(1)} %slice.23), channel_id=1, source_target_pairs={{0,2},{1,3},{2,0},{3,1},{4,6},{5,7},{6,4},{7,5},{8,10},{9,11},{10,... | collective-permute-start | bytes 393224 | tf_op jit(solution)/shard_map/ppermute | solution.py:282
  35.5 5.6 %collective-permute-start.17 = (f32[80,256]{1,0:T(8,128)S(1)}, f32[80,256]{1,0:T(8,128)S(1)}, u32[]{:S(2)}, u32[]{:S(2)}) collective-permute-start(f32[80,256]{1,0:T(8,128)S(1)} %add.22), channel_id=1, source_target_pairs={{0,16},{4,20},{8,24},{12,28},{16,0},{20,4},{24,8},{28,12},{1,17},{... | collective-permute-start | bytes 245768 | tf_op jit(solution)/shard_map/ppermute | solution.py:282
  38.2 6.5 %collective-permute-start.9 = (f32[256,256]{1,0:T(8,128)S(1)}, f32[256,256]{1,0:T(8,128)S(1)}, u32[]{:S(2)}, u32[]{:S(2)}) collective-permute-start(f32[256,256]{1,0:T(8,128)S(1)} %collective-permute-done.5.refs_4_), channel_id=1, source_target_pairs={{0,4},{4,0},{8,12},{12,8},{16,20},{20,16},{24,28},{28,24},{1,5},{5... | collective-permute-start | bytes 786440 | tf_op jit(solution)/shard_map/ppermute | solution.py:282
  38.2 6.5 %collective-permute-start.8 = (f32[256,256]{1,0:T(8,128)S(1)}, f32[256,256]{1,0:T(8,128)S(1)}, u32[]{:S(2)}, u32[]{:S(2)}) collective-permute-start(f32[256,256]{1,0:T(8,128)S(1)} %collective-permute-done.4.refs_3_), channel_id=1, source_target_pairs={{0,4},{4,0},{8,12},{12,8},{16,20},{20,16},{24,28},{28,24},{1,5},{5... | collective-permute-start | bytes 786440 | tf_op jit(solution)/shard_map/ppermute | solution.py:282
  38.7 6.0 %collective-permute-start.10 = (f32[128,256]{1,0:T(8,128)S(1)}, f32[128,256]{1,0:T(8,128)S(1)}, u32[]{:S(2)}, u32[]{:S(2)}) collective-permute-start(f32[128,256]{1,0:T(8,128)S(1)} %collective-permute-done.6.refs_5_), channel_id=1, source_target_pairs={{0,4},{4,0},{8,12},{12,8},{16,20},{20,16},{24,28},{28,24},{1,5},{5... | collective-permute-start | bytes 393224 | tf_op jit(solution)/shard_map/ppermute | solution.py:282
  38.8 5.9 %collective-permute-start.11 = (f32[128,256]{1,0:T(8,128)S(1)}, f32[128,256]{1,0:T(8,128)S(1)}, u32[]{:S(2)}, u32[]{:S(2)}) collective-permute-start(f32[128,256]{1,0:T(8,128)S(1)} %collective-permute-done.7.refs_6_), channel_id=1, source_target_pairs={{0,4},{4,0},{8,12},{12,8},{16,20},{20,16},{24,28},{28,24},{1,5},{5... | collective-permute-start | bytes 393224 | tf_op jit(solution)/shard_map/ppermute | solution.py:282
  41.2 3.9 %collective-permute-start.18 = (f32[80,256]{1,0:T(8,128)S(1)}, f32[80,256]{1,0:T(8,128)S(1)}, u32[]{:S(2)}, u32[]{:S(2)}) collective-permute-start(f32[80,256]{1,0:T(8,128)S(1)} %add.23.mine), channel_id=1, source_target_pairs={{0,4},{4,0},{8,12},{12,8},{16,20},{20,16},{24,28},{28,24},{1,5},{5... | collective-permute-start | bytes 245768 | tf_op jit(solution)/shard_map/ppermute | solution.py:282
  46.9 6.8 %collective-permute-start.19 = (f32[96,256]{1,0:T(8,128)S(1)}, f32[96,256]{1,0:T(8,128)S(1)}, u32[]{:S(2)}, u32[]{:S(2)}) collective-permute-start(f32[96,256]{1,0:T(8,128)S(1)} %get-tuple-element.77), channel_id=1, source_target_pairs={{0,1},{1,0},{2,3},{3,2},{4,5},{5,4},{6,7},{7,6},{8,9},{9,8},{10,11... | collective-permute-start | bytes 294920 | tf_op jit(solution)/shard_map/ppermute | solution.py:282
  48.0 5.7 %collective-permute-start.20 = (f32[96,256]{1,0:T(8,128)S(1)}, f32[96,256]{1,0:T(8,128)S(1)}, u32[]{:S(2)}, u32[]{:S(2)}) collective-permute-start(f32[96,256]{1,0:T(8,128)S(1)} %get-tuple-element.78), channel_id=1, source_target_pairs={{0,2},{1,3},{2,0},{3,1},{4,6},{5,7},{6,4},{7,5},{8,10},{9,11},{10,... | collective-permute-start | bytes 294920 | tf_op jit(solution)/shard_map/ppermute | solution.py:282
  48.7 6.3 %collective-permute-start.21 = (f32[96,256]{1,0:T(8,128)S(1)}, f32[96,256]{1,0:T(8,128)S(1)}, u32[]{:S(2)}, u32[]{:S(2)}) collective-permute-start(f32[96,256]{1,0:T(8,128)S(1)} %get-tuple-element.79), channel_id=1, source_target_pairs={{0,3},{1,2},{2,1},{3,0},{4,7},{5,6},{6,5},{7,4},{8,11},{9,10},{10,... | collective-permute-start | bytes 294920 | tf_op jit(solution)/shard_map/ppermute | solution.py:282
  59.4 5.6 %collective-permute-start.22 = (f32[96,256]{1,0:T(8,128)S(1)}, f32[96,256]{1,0:T(8,128)S(1)}, u32[]{:S(2)}, u32[]{:S(2)}) collective-permute-start(f32[96,256]{1,0:T(8,128)S(1)} %get-tuple-element.82), channel_id=1, source_target_pairs={{0,1},{1,0},{2,3},{3,2},{4,5},{5,4},{6,7},{7,6},{8,9},{9,8},{10,11... | collective-permute-start | bytes 294920 | tf_op jit(solution)/shard_map/ppermute | solution.py:282
  60.4 5.4 %collective-permute-start.23 = (f32[96,256]{1,0:T(8,128)S(1)}, f32[96,256]{1,0:T(8,128)S(1)}, u32[]{:S(2)}, u32[]{:S(2)}) collective-permute-start(f32[96,256]{1,0:T(8,128)S(1)} %get-tuple-element.83), channel_id=1, source_target_pairs={{0,2},{1,3},{2,0},{3,1},{4,6},{5,7},{6,4},{7,5},{8,10},{9,11},{10,... | collective-permute-start | bytes 294920 | tf_op jit(solution)/shard_map/ppermute | solution.py:282
  61.7 5.5 %collective-permute-start.24 = (f32[96,256]{1,0:T(8,128)S(1)}, f32[96,256]{1,0:T(8,128)S(1)}, u32[]{:S(2)}, u32[]{:S(2)}) collective-permute-start(f32[96,256]{1,0:T(8,128)S(1)} %get-tuple-element.84), channel_id=1, source_target_pairs={{0,3},{1,2},{2,1},{3,0},{4,7},{5,6},{6,5},{7,4},{8,11},{9,10},{10,... | collective-permute-start | bytes 294920 | tf_op jit(solution)/shard_map/ppermute | solution.py:282
  67.6 1.3 %collective-permute-start.25 = (f32[80,256]{1,0:T(8,128)S(1)}, f32[80,256]{1,0:T(8,128)S(1)}, u32[]{:S(2)}, u32[]{:S(2)}) collective-permute-start(f32[80,256]{1,0:T(8,128)S(1)} %get-tuple-element.87), channel_id=1, source_target_pairs={{0,4},{4,0},{8,12},{12,8},{16,20},{20,16},{24,28},{28,24},{1,5},{5... | collective-permute-start | bytes 245768 | tf_op jit(solution)/shard_map/ppermute | solution.py:282
  69.0 7.7 %collective-permute-start.28 = (f32[80,256]{1,0:T(8,128)S(1)}, f32[80,256]{1,0:T(8,128)S(1)}, u32[]{:S(2)}, u32[]{:S(2)}) collective-permute-start(f32[80,256]{1,0:T(8,128)S(1)} %add.24), channel_id=1, source_target_pairs={{0,24},{4,28},{8,16},{12,20},{16,8},{20,12},{24,0},{28,4},{1,25},{... | collective-permute-start | bytes 245768 | tf_op jit(solution)/shard_map/ppermute | solution.py:282
  73.3 6.4 %collective-permute-start.27 = (f32[80,256]{1,0:T(8,128)S(1)}, f32[80,256]{1,0:T(8,128)S(1)}, u32[]{:S(2)}, u32[]{:S(2)}) collective-permute-start(f32[80,256]{1,0:T(8,128)S(1)} %add.24), channel_id=1, source_target_pairs={{0,16},{4,20},{8,24},{12,28},{16,0},{20,4},{24,8},{28,12},{1,17},{... | collective-permute-start | bytes 245768 | tf_op jit(solution)/shard_map/ppermute | solution.py:282
  73.3 6.4 %collective-permute-start.26 = (f32[80,256]{1,0:T(8,128)S(1)}, f32[80,256]{1,0:T(8,128)S(1)}, u32[]{:S(2)}, u32[]{:S(2)}) collective-permute-start(f32[80,256]{1,0:T(8,128)S(1)} %add.24), channel_id=1, source_target_pairs={{0,8},{4,12},{8,0},{12,4},{16,24},{20,28},{24,16},{28,20},{1,9},{5... | collective-permute-start | bytes 245768 | tf_op jit(solution)/shard_map/ppermute | solution.py:282
  79.7 1.3 %collective-permute-start.29 = (f32[80,256]{1,0:T(8,128)S(1)}, f32[80,256]{1,0:T(8,128)S(1)}, u32[]{:S(2)}, u32[]{:S(2)}) collective-permute-start(f32[80,256]{1,0:T(8,128)S(1)} %add_add_fusion.mine), channel_id=1, source_target_pairs={{0,4},{4,0},{8,12},{12,8},{16,20},{20,16},{24,28},{28,24},{1,5},{5... | collective-permute-start | bytes 245768 | tf_op jit(solution)/shard_map/ppermute | solution.py:282
  82.9 5.6 %collective-permute-start.30 = (f32[96,256]{1,0:T(8,128)S(1)}, f32[96,256]{1,0:T(8,128)S(1)}, u32[]{:S(2)}, u32[]{:S(2)}) collective-permute-start(f32[96,256]{1,0:T(8,128)S(1)} %get-tuple-element.89), channel_id=1, source_target_pairs={{0,1},{1,0},{2,3},{3,2},{4,5},{5,4},{6,7},{7,6},{8,9},{9,8},{10,11... | collective-permute-start | bytes 294920 | tf_op jit(solution)/shard_map/ppermute | solution.py:282
  83.5 5.0 %collective-permute-start.31 = (f32[96,256]{1,0:T(8,128)S(1)}, f32[96,256]{1,0:T(8,128)S(1)}, u32[]{:S(2)}, u32[]{:S(2)}) collective-permute-start(f32[96,256]{1,0:T(8,128)S(1)} %get-tuple-element.90), channel_id=1, source_target_pairs={{0,2},{1,3},{2,0},{3,1},{4,6},{5,7},{6,4},{7,5},{8,10},{9,11},{10,... | collective-permute-start | bytes 294920 | tf_op jit(solution)/shard_map/ppermute | solution.py:282
  84.8 5.5 %collective-permute-start.32 = (f32[96,256]{1,0:T(8,128)S(1)}, f32[96,256]{1,0:T(8,128)S(1)}, u32[]{:S(2)}, u32[]{:S(2)}) collective-permute-start(f32[96,256]{1,0:T(8,128)S(1)} %get-tuple-element.91), channel_id=1, source_target_pairs={{0,3},{1,2},{2,1},{3,0},{4,7},{5,6},{6,5},{7,4},{8,11},{9,10},{10,... | collective-permute-start | bytes 294920 | tf_op jit(solution)/shard_map/ppermute | solution.py:282
  (2 other events, 1.7 us)
